TPU v7x, 32 devices: a whole 2x2x4 slice. The times are simulated.
32 devices in a mesh: rows: 32 (over z, y, x, core).
Axes of the slice: x: 2, y: 2, z: 4, core: 2. Of those that a mesh axis runs over, the one named last changes fastest.
Arguments:
- tracers_init: float32 [16384, 256], P('rows'), may hold values from -6 to 6
- source: float32 [16384, 256], P('rows'), may hold values from -4 to 4
- explicit_tiles: float32 [128, 8, 128, 128], P('rows'), may hold values from -0.0625 to 0.0625
- implicit_tiles: float32 [128, 8, 128, 128], P('rows'), may hold values from -0.0625 to 0.0625
- explicit_cols: int32 [128, 8], P('rows'), may hold values from 0 to 6, as said below
- implicit_cols: int32 [128, 8], P('rows'), may hold values from 0 to 6, as said below
- send_rows: int32 [256, 48], P('rows'), may hold values from 0 to 511
Outputs:
- tracers: float32 [16384, 256], P('rows')
Inputs may be any that keep to these rules, and one draw needn't show every extreme that they name: `explicit_cols`: each entry names one of the 7 blocks of the device's own rows followed by its halo rows. `implicit_cols`: each entry names one of the 7 blocks of the device's own rows followed by its halo rows. `send_rows`: local row numbers of the sending device.
All inputs are finite; a program needn't handle non-finite values.
Results may differ from a plain program's by a relative error of at most 0.0001.
Values sent between devices are 32-bit elements; how exact they have to be, the bound alone decides.
No kernel may reach another device: no remote copies, remote signals or barrier semaphores. Data moves between devices by JAX's collectives and lax.ppermute only.
A program may use at most 64 MiB of HBM per device.

v0:
```python
import functools

import jax
import jax.numpy as jnp
from jax import lax
from jax.experimental import pallas as pl
from jax.experimental.pallas import tpu as pltpu
from jax.sharding import PartitionSpec as P


STEPS = 3
GRANT = 14 * 2**20

VMEM = pl.BlockSpec(memory_space=pltpu.VMEM)
SMEM = pl.BlockSpec(memory_space=pltpu.SMEM)
F32, BF16 = jnp.float32, jnp.bfloat16


def call(kernel, outs, in_specs, args, scratch=()):
    return pl.pallas_call(
        kernel,
        out_shape=[jax.ShapeDtypeStruct(shape, dtype) for shape, dtype in outs],
        in_specs=in_specs,
        out_specs=[VMEM] * len(outs),
        scratch_shapes=list(scratch),
        compiler_params=pltpu.CompilerParams(vmem_limit_bytes=GRANT),
    )(*args)


def partner_offset(offset_index):
    return (offset_index // 2 + 1) * (1 if offset_index % 2 == 0 else -1)


def routes(partners):
    found = {}
    for sender in range(2):
        for offset_index in range(partners):
            to = sender + partner_offset(offset_index)
            found.setdefault(to // 2, []).append((sender, offset_index, to % 2))
    far = sorted((hop for hop in found if hop > 0)) + sorted((hop for hop in found if hop < 0), reverse=True)
    return [(hop, found[hop]) for hop in [0] + far]


def side():
    return lax.rem(lax.axis_index("rows"), 2)


def swap(x):
    devices = lax.axis_size("rows")
    return lax.ppermute(x, "rows", [(i, i ^ 1) for i in range(devices)])


def split2(x):
    high = x.astype(BF16)
    return high, (x - high.astype(F32)).astype(BF16)


def dot(a, b):
    return jnp.dot(a, b, preferred_element_type=F32)


def product(m_high, m_low, x):
    half = x.shape[1] // 2
    big, small = dot(m_high, x), dot(m_low, x)
    return big[:, :half] + (big[:, half:] + (small[:, :half] + small[:, half:]))


def pick_rows(onehot, x):
    half = x.shape[1]
    high = x.astype(BF16)
    rest = x - high.astype(F32)
    mid = rest.astype(BF16)
    low = (rest - mid.astype(F32)).astype(BF16)
    got = dot(onehot, jnp.concatenate([high, mid, low], axis=1))
    return got[:, :half] + (got[:, half : 2 * half] + got[:, 2 * half :])


def fill_onehot(rows, onehot):
    lists, length = rows.shape
    width = onehot.shape[1]
    down = lax.broadcasted_iota(jnp.int32, (length, length), 0)
    along = lax.broadcasted_iota(jnp.int32, (length, length), 1)
    lanes = lax.broadcasted_iota(jnp.int32, (length, width), 1)
    for i in range(lists):
        spread = jnp.broadcast_to(rows[i : i + 1, :], (length, length))
        column = jnp.sum(jnp.where(down == along, spread, 0).astype(F32), axis=1, keepdims=True)
        hit = jnp.broadcast_to(column, (length, width)) == lanes.astype(F32)
        onehot[i * length : (i + 1) * length, :] = jnp.where(hit, 1.0, 0.0).astype(BF16)


def halves_kernel(x, keep, give):
    half = keep.shape[1]

    @pl.when(side() == 0)
    def _():
        keep[...] = x[:, :half]
        give[...] = x[:, half:]

    @pl.when(side() == 1)
    def _():
        keep[...] = x[:, half:]
        give[...] = x[:, :half]


def merge_kernel(columns, tiles, total):
    blocks, slots = tiles.shape[:2]
    total[...] = jnp.zeros_like(total)
    for block in range(blocks):
        for slot in range(slots):
            column = columns[block, slot]
            total[block, column] += tiles[block, slot]


def split_kernel(total, onehot, own_high, own_low, far_high, far_low, out_high, out_low):
    blocks, columns, size, _ = total.shape
    for block in range(blocks):
        at = slice(block * size, (block + 1) * size)
        for column in range(columns):
            high, low = split2(total[block, column])
            to_high, to_low = (own_high, own_low) if column < blocks else (far_high, far_low)
            place = column if column < blocks else column - blocks
            to_high[at, place * size : (place + 1) * size] = high
            to_low[at, place * size : (place + 1) * size] = low
    out_high[...] = dot(onehot[...], far_high[...]).astype(BF16)
    out_low[...] = dot(onehot[...], far_low[...]).astype(BF16)


def deal(route, lists, outs):
    for (_, group), out in zip(route, outs):
        length = out.shape[0] // len(group)
        for i, (sender, offset_index, _) in enumerate(group):
            out[i * length : (i + 1) * length, :] = lists[sender, offset_index * length : (offset_index + 1) * length, :]


def collect(route, arrived, halo):
    for (_, group), piece in zip(route, arrived):
        length = piece.shape[0] // len(group)
        half = piece.shape[1]
        for i, (_, offset_index, receiver) in enumerate(group):
            high, low = split2(piece[i * length : (i + 1) * length, :])
            at = slice(offset_index * length, (offset_index + 1) * length)
            halo[receiver, at, :half] = high
            halo[receiver, at, half:] = low


def first_kernel(route, mine, other, rows_mine, rows_other, *refs):
    outs = refs[: len(route)]
    onehot_mine, onehot_other, lists = refs[len(route) :]
    fill_onehot(rows_mine, onehot_mine)
    fill_onehot(rows_other, onehot_other)
    lists[side()] = pick_rows(onehot_mine[...], mine[...])
    lists[1 - side()] = pick_rows(onehot_other[...], other[...])
    deal(route, lists, outs)


def own_kernel(route, has_source, first, *refs):
    refs = list(refs)

    def take(count):
        taken = refs[:count]
        del refs[:count]
        return taken

    onehots = take(2)
    owns = [take(2), take(2)]
    sources = take(2) if has_source else None
    states = take(2)
    if not first:
        fars = [take(2), take(2)]
        arrived = take(len(route))
    bases, picks = take(2), take(2)
    if not first:
        (halo,) = refs
        collect(route, arrived, halo)
    for role in range(2):
        now = states[role][...]
        if not first:
            slot = side() if role == 0 else 1 - side()
            now = now + product(fars[role][0][...], fars[role][1][...], halo[slot])
        total = now + product(owns[role][0][...], owns[role][1][...], jnp.concatenate(split2(now), axis=1))
        if has_source:
            total = total + sources[role][...]
        bases[role][...] = total
        picks[role][...] = pick_rows(onehots[role][...], total)


def payload_kernel(route, *refs):
    count = len(route)
    picks, outs_of = refs[:2], (refs[2:4], refs[4:6])
    arrived, outs = refs[6 : 6 + count], refs[6 + count : 6 + 2 * count]
    halo, lists = refs[6 + 2 * count :]
    collect(route, arrived, halo)
    for role in range(2):
        slot = side() if role == 0 else 1 - side()
        lists[slot] = picks[role][...] + product(outs_of[role][0][...], outs_of[role][1][...], halo[slot])
    deal(route, lists, outs)


def last_kernel(route, role, base, far_high, far_low, *refs):
    arrived, (out, halo) = refs[: len(route)], refs[len(route) :]
    collect(route, arrived, halo)
    slot = side() if role == 0 else 1 - side()
    out[...] = base[...] + product(far_high[...], far_low[...], halo[slot])


def join_kernel(kept, got, out):
    half = kept.shape[1]

    @pl.when(side() == 0)
    def _():
        out[:, :half] = kept[...]
        out[:, half:] = got[...]

    @pl.when(side() == 1)
    def _():
        out[:, :half] = got[...]
        out[:, half:] = kept[...]


def on_device(
    tracers_init, source, explicit_tiles, implicit_tiles, explicit_cols, implicit_cols, send_rows
):
    devices = lax.axis_size("rows")
    local_rows, panels = tracers_init.shape
    half = panels // 2
    blocks, _, size, _ = explicit_tiles.shape
    partners, length = send_rows.shape
    halo_rows = partners * length
    columns = blocks + halo_rows // size
    route = routes(partners)
    state_half = ((local_rows, half), F32)
    list_half = ((halo_rows, half), F32)
    pieces_out = [((len(group) * length, half), F32) for _, group in route]
    halo_scratch = pltpu.VMEM((2, halo_rows, panels), BF16)
    lists_scratch = pltpu.VMEM((2, halo_rows, half), F32)

    def halves(x):
        return call(halves_kernel, [state_half] * 2, [VMEM], (x,))

    def merge(tiles, cols):
        return call(merge_kernel, [((blocks, columns, size, size), F32)], [SMEM, VMEM], (cols, tiles))[0]

    def split(total, onehot):
        return call(
            split_kernel,
            [((local_rows, local_rows), BF16)] * 2
            + [((local_rows, halo_rows), BF16)] * 2
            + [((halo_rows, halo_rows), BF16)] * 2,
            [VMEM] * 2,
            (total, onehot),
        )

    def exchange(pieces):
        arrived = [pieces[0]]
        for (hop, _), piece in zip(route[1:], pieces[1:]):
            pairs = [(d, (d + 2 * hop) % devices) for d in range(devices)]
            arrived.append(lax.ppermute(piece, "rows", pairs))
        return arrived

    applies = 2 * STEPS
    for number in range(applies):
        if number == 0:
            rows_other = swap(send_rows)
            state, give = halves(tracers_init)
            state_other = swap(give)
            merged_e = merge(explicit_tiles, explicit_cols)
            merged_e_other = swap(merged_e)
            *pieces, onehot, onehot_other = call(
                functools.partial(first_kernel, route),
                pieces_out + [((halo_rows, local_rows), BF16)] * 2,
                [VMEM] * 4,
                (state, state_other, send_rows, rows_other),
                [lists_scratch],
            )
            states = (state, state_other)
        else:
            pieces = call(
                functools.partial(payload_kernel, route),
                pieces_out,
                [VMEM] * (6 + len(route)),
                (*picks, *matrix[0][4:], *matrix[1][4:], *arrived),
                [halo_scratch, lists_scratch],
            )
        fresh = exchange(pieces)
        if number == 0:
            give_s = halves(source)
            sources = (give_s[0], swap(give_s[1]))
            matrix_e = (split(merged_e, onehot), split(merged_e_other, onehot_other))
            merged_i = merge(implicit_tiles, implicit_cols)
            merged_i_other = swap(merged_i)
        if number == 1:
            matrix_i = (split(merged_i, onehot), split(merged_i_other, onehot_other))
        last_matrix = matrix if number else None
        matrix = matrix_i if number % 2 else matrix_e
        has_source = number % 2 == 0
        args = (onehot, onehot_other, *matrix[0][:2], *matrix[1][:2])
        if has_source:
            args += sources
        args += tuple(states)
        if number:
            args += (*last_matrix[0][2:4], *last_matrix[1][2:4], *arrived)
        out = call(
            functools.partial(own_kernel, route, has_source, number == 0),
            [state_half] * 2 + [list_half] * 2,
            [VMEM] * len(args),
            args,
            [halo_scratch] if number else [],
        )
        states, picks = out[:2], out[2:]
        arrived = fresh

    def last(role):
        return call(
            functools.partial(last_kernel, route, role),
            [state_half],
            [VMEM] * (3 + len(route)),
            (states[role], *matrix[role][2:4], *arrived),
            [halo_scratch],
        )[0]

    got = swap(last(1))
    return call(join_kernel, [((local_rows, panels), F32)], [VMEM] * 2, (last(0), got))[0]


def solution(mesh):
    return jax.shard_map(
        on_device,
        mesh=mesh,
        in_specs=(
            P("rows", None),
            P("rows", None),
            P("rows", None, None, None),
            P("rows", None, None, None),
            P("rows", None),
            P("rows", None),
            P("rows", None),
        ),
        out_specs=P("rows", None),
        check_vma=False,
    )
```

profile of v0, /device:TPU:0, one launch (start us, length us, event | category | flops | bytes accessed | tf_op | source)
XLA Modules:
  0.0 98.0 jit_solution(18288423986376294181)
XLA Ops:
  0.0 1.6 %copy-done = f32[4,8,128,128]{3,2,1,0:T(8,128)S(1)} copy-done((f32[4,8,128,128]{3,2,1,0:T(8,128)S(1)}, f32[4,8,128,128]{3,2,1,0:T(8,128)}, u32[]{:S(2)}) %copy-start) | copy-done | bytes 2097176
  1.6 0.7 copy-done.5
  2.3 0.9 shard_map.78.total
  3.2 0.0 copy-start.2
  3.2 0.0 copy-start.3
  3.2 0.0 copy-start.4
  3.2 0.6 collective-permute-start.3
  3.8 0.1 copy-done.1
  3.9 0.9 shard_map.75.total
  4.8 0.6 collective-permute-start.2
  5.4 0.1 collective-permute-start
  5.5 0.5 collective-permute-start.4
  6.1 0.1 collective-permute-start.1
  6.2 4.4 %collective-permute-done.1.rows_other = s32[8,48]{1,0:T(8,128)S(1)} collective-permute-done((s32[8,48]{1,0:T(8,128)S(1)}, s32[8,48]{1,0:T(8,128)S(1)}, u32[]{:S(2)}, u32[]{:S(2)}) %collective-permute-start.1) | collective-permute-done | bytes 1568 | tf_op jit(solution)/shard_map/ppermute | solution.py:50
  10.6 0.7 shard_map.74
  11.3 2.9 %collective-permute-start.5 = (f32[192,128]{1,0:T(8,128)S(1)}, f32[192,128]{1,0:T(8,128)S(1)}, u32[]{:S(2)}, u32[]{:S(2)}) collective-permute-start(f32[192,128]{1,0:T(8,128)S(1)} %get-tuple-element.108), channel_id=1, source_target_pairs={{0,2},{1,3},{2,4},{3,5},{4,6},{5,7},{6,8},{7,9},{8,10},{9,11},{10,... | collective-permute-start | bytes 294920 | tf_op jit(solution)/shard_map/ppermute | solution.py:257
  14.2 4.1 %collective-permute-start.7 = (f32[192,128]{1,0:T(8,128)S(1)}, f32[192,128]{1,0:T(8,128)S(1)}, u32[]{:S(2)}, u32[]{:S(2)}) collective-permute-start(f32[192,128]{1,0:T(8,128)S(1)} %get-tuple-element.110), channel_id=1, source_target_pairs={{0,30},{1,31},{2,0},{3,1},{4,2},{5,3},{6,4},{7,5},{8,6},{9,7},{10,... | collective-permute-start | bytes 294920 | tf_op jit(solution)/shard_map/ppermute | solution.py:257
  18.3 0.0 collective-permute-done.4.refs_7_
  18.3 0.0 collective-permute-start.6
  18.3 0.0 collective-permute-done.3.total
  18.3 4.7 %collective-permute-start.8 = (f32[144,128]{1,0:T(8,128)S(1)}, f32[144,128]{1,0:T(8,128)S(1)}, u32[]{:S(2)}, u32[]{:S(2)}) collective-permute-start(f32[144,128]{1,0:T(8,128)S(1)} %get-tuple-element.111), channel_id=1, source_target_pairs={{0,28},{1,29},{2,30},{3,31},{4,0},{5,1},{6,2},{7,3},{8,4},{9,5},{1... | collective-permute-start | bytes 221192 | tf_op jit(solution)/shard_map/ppermute | solution.py:257
  23.0 0.8 shard_map.79
  23.8 0.8 shard_map.80
  24.6 1.3 %shard_map.82 = (f32[512,128]{1,0:T(8,128)S(1)}, f32[512,128]{1,0:T(8,128)S(1)}, f32[384,128]{1,0:T(8,128)S(1)}, f32[384,128]{1,0:T(8,128)S(1)}) custom-call(bf16[384,512]{1,0:T(8,128)(2,1)S(1)} %get-tuple-element.89.onehot.refs_0_, bf16[384,512]{1,0:T(8,128)(2,1)S(1)} %get-tuple-element.90.onehot.refs_1_, bf16[512,512]{1,0:T(8,128)(2,1)S(1)} %get-tuple-element.95.refs_2_, ...), custom_call_target="tpu_custom_call" | custom-call | tf_op jit(solution)/shard_map/pallas_call | solution.py:20
  25.9 0.0 collective-permute-done.6.refs_14_.refs_8_
  25.9 0.0 collective-permute-done.5.refs_13_.refs_7_
  25.9 0.0 collective-permute-done.7.refs_15_.refs_9_
  25.9 0.7 shard_map.84
  26.7 0.1 collective-permute-start.9
  26.7 5.6 %collective-permute-start.11 = (f32[192,128]{1,0:T(8,128)S(1)}, f32[192,128]{1,0:T(8,128)S(1)}, u32[]{:S(2)}, u32[]{:S(2)}) collective-permute-start(f32[192,128]{1,0:T(8,128)S(1)} %get-tuple-element.127), channel_id=1, source_target_pairs={{0,30},{1,31},{2,0},{3,1},{4,2},{5,3},{6,4},{7,5},{8,6},{9,7},{10,... | collective-permute-start | bytes 294920 | tf_op jit(solution)/shard_map/ppermute | solution.py:257
  32.4 4.7 %collective-permute-start.12 = (f32[144,128]{1,0:T(8,128)S(1)}, f32[144,128]{1,0:T(8,128)S(1)}, u32[]{:S(2)}, u32[]{:S(2)}) collective-permute-start(f32[144,128]{1,0:T(8,128)S(1)} %get-tuple-element.128), channel_id=1, source_target_pairs={{0,28},{1,29},{2,30},{3,31},{4,0},{5,1},{6,2},{7,3},{8,4},{9,5},{1... | collective-permute-start | bytes 221192 | tf_op jit(solution)/shard_map/ppermute | solution.py:257
  37.1 0.8 shard_map.76
  37.9 0.0 collective-permute-done.2.total
  37.9 0.8 shard_map.77
  38.7 2.1 %shard_map.83 = (f32[512,128]{1,0:T(8,128)S(1)}, f32[512,128]{1,0:T(8,128)S(1)}, f32[384,128]{1,0:T(8,128)S(1)}, f32[384,128]{1,0:T(8,128)S(1)}) custom-call(bf16[384,512]{1,0:T(8,128)(2,1)S(1)} %get-tuple-element.89.onehot.refs_0_, bf16[384,512]{1,0:T(8,128)(2,1)S(1)} %get-tuple-element.90.onehot.refs_1_, bf16[512,512]{1,0:T(8,128)(2,1)S(1)} %get-tuple-element.91.refs_2_, ...), custom_call_target="tpu_custom_call" | custom-call | tf_op jit(solution)/shard_map/pallas_call | solution.py:20
  40.8 0.0 collective-permute-done.12.refs_18_.refs_10_
  40.8 0.7 shard_map.86
  41.5 0.1 collective-permute-start.13
  41.6 5.6 %collective-permute-start.15 = (f32[192,128]{1,0:T(8,128)S(1)}, f32[192,128]{1,0:T(8,128)S(1)}, u32[]{:S(2)}, u32[]{:S(2)}) collective-permute-start(f32[192,128]{1,0:T(8,128)S(1)} %get-tuple-element.140), channel_id=1, source_target_pairs={{0,30},{1,31},{2,0},{3,1},{4,2},{5,3},{6,4},{7,5},{8,6},{9,7},{10,... | collective-permute-start | bytes 294920 | tf_op jit(solution)/shard_map/ppermute | solution.py:257
  47.2 4.7 %collective-permute-start.16 = (f32[144,128]{1,0:T(8,128)S(1)}, f32[144,128]{1,0:T(8,128)S(1)}, u32[]{:S(2)}, u32[]{:S(2)}) collective-permute-start(f32[144,128]{1,0:T(8,128)S(1)} %get-tuple-element.141), channel_id=1, source_target_pairs={{0,28},{1,29},{2,30},{3,31},{4,0},{5,1},{6,2},{7,3},{8,4},{9,5},{1... | collective-permute-start | bytes 221192 | tf_op jit(solution)/shard_map/ppermute | solution.py:257
  51.9 2.0 %shard_map.85 = (f32[512,128]{1,0:T(8,128)S(1)}, f32[512,128]{1,0:T(8,128)S(1)}, f32[384,128]{1,0:T(8,128)S(1)}, f32[384,128]{1,0:T(8,128)S(1)}) custom-call(bf16[384,512]{1,0:T(8,128)(2,1)S(1)} %get-tuple-element.89.onehot.refs_0_, bf16[384,512]{1,0:T(8,128)(2,1)S(1)} %get-tuple-element.90.onehot.refs_1_, bf16[512,512]{1,0:T(8,128)(2,1)S(1)} %get-tuple-element.95.refs_2_, ...), custom_call_target="tpu_custom_call" | custom-call | tf_op jit(solution)/shard_map/pallas_call | solution.py:20
  54.0 0.3 collective-permute-done.14.refs_14_.refs_8_
  54.3 0.7 shard_map.88
  55.0 0.1 collective-permute-start.17
  55.1 5.6 %collective-permute-start.19 = (f32[192,128]{1,0:T(8,128)S(1)}, f32[192,128]{1,0:T(8,128)S(1)}, u32[]{:S(2)}, u32[]{:S(2)}) collective-permute-start(f32[192,128]{1,0:T(8,128)S(1)} %get-tuple-element.149), channel_id=1, source_target_pairs={{0,30},{1,31},{2,0},{3,1},{4,2},{5,3},{6,4},{7,5},{8,6},{9,7},{10,... | collective-permute-start | bytes 294920 | tf_op jit(solution)/shard_map/ppermute | solution.py:257
  60.7 4.7 %collective-permute-start.20 = (f32[144,128]{1,0:T(8,128)S(1)}, f32[144,128]{1,0:T(8,128)S(1)}, u32[]{:S(2)}, u32[]{:S(2)}) collective-permute-start(f32[144,128]{1,0:T(8,128)S(1)} %get-tuple-element.150), channel_id=1, source_target_pairs={{0,28},{1,29},{2,30},{3,31},{4,0},{5,1},{6,2},{7,3},{8,4},{9,5},{1... | collective-permute-start | bytes 221192 | tf_op jit(solution)/shard_map/ppermute | solution.py:257
  65.4 2.1 %shard_map.87 = (f32[512,128]{1,0:T(8,128)S(1)}, f32[512,128]{1,0:T(8,128)S(1)}, f32[384,128]{1,0:T(8,128)S(1)}, f32[384,128]{1,0:T(8,128)S(1)}) custom-call(bf16[384,512]{1,0:T(8,128)(2,1)S(1)} %get-tuple-element.89.onehot.refs_0_, bf16[384,512]{1,0:T(8,128)(2,1)S(1)} %get-tuple-element.90.onehot.refs_1_, bf16[512,512]{1,0:T(8,128)(2,1)S(1)} %get-tuple-element.91.refs_2_, ...), custom_call_target="tpu_custom_call" | custom-call | tf_op jit(solution)/shard_map/pallas_call | solution.py:20
  67.5 0.3 collective-permute-done.18.refs_16_.refs_8_
  67.7 0.7 shard_map.90
  68.5 0.1 collective-permute-start.21
  68.5 5.6 %collective-permute-start.23 = (f32[192,128]{1,0:T(8,128)S(1)}, f32[192,128]{1,0:T(8,128)S(1)}, u32[]{:S(2)}, u32[]{:S(2)}) collective-permute-start(f32[192,128]{1,0:T(8,128)S(1)} %get-tuple-element.158), channel_id=1, source_target_pairs={{0,30},{1,31},{2,0},{3,1},{4,2},{5,3},{6,4},{7,5},{8,6},{9,7},{10,... | collective-permute-start | bytes 294920 | tf_op jit(solution)/shard_map/ppermute | solution.py:257
  74.1 4.7 %collective-permute-start.24 = (f32[144,128]{1,0:T(8,128)S(1)}, f32[144,128]{1,0:T(8,128)S(1)}, u32[]{:S(2)}, u32[]{:S(2)}) collective-permute-start(f32[144,128]{1,0:T(8,128)S(1)} %get-tuple-element.159), channel_id=1, source_target_pairs={{0,28},{1,29},{2,30},{3,31},{4,0},{5,1},{6,2},{7,3},{8,4},{9,5},{1... | collective-permute-start | bytes 221192 | tf_op jit(solution)/shard_map/ppermute | solution.py:257
  78.9 2.0 %shard_map.89 = (f32[512,128]{1,0:T(8,128)S(1)}, f32[512,128]{1,0:T(8,128)S(1)}, f32[384,128]{1,0:T(8,128)S(1)}, f32[384,128]{1,0:T(8,128)S(1)}) custom-call(bf16[384,512]{1,0:T(8,128)(2,1)S(1)} %get-tuple-element.89.onehot.refs_0_, bf16[384,512]{1,0:T(8,128)(2,1)S(1)} %get-tuple-element.90.onehot.refs_1_, bf16[512,512]{1,0:T(8,128)(2,1)S(1)} %get-tuple-element.95.refs_2_, ...), custom_call_target="tpu_custom_call" | custom-call | tf_op jit(solution)/shard_map/pallas_call | solution.py:20
  80.9 0.3 collective-permute-done.22.refs_14_.refs_8_
  81.2 0.7 shard_map.92
  81.9 0.1 collective-permute-start.25
  82.0 5.6 %collective-permute-start.27 = (f32[192,128]{1,0:T(8,128)S(1)}, f32[192,128]{1,0:T(8,128)S(1)}, u32[]{:S(2)}, u32[]{:S(2)}) collective-permute-start(f32[192,128]{1,0:T(8,128)S(1)} %get-tuple-element.166), channel_id=1, source_target_pairs={{0,30},{1,31},{2,0},{3,1},{4,2},{5,3},{6,4},{7,5},{8,6},{9,7},{10,... | collective-permute-start | bytes 294920 | tf_op jit(solution)/shard_map/ppermute | solution.py:257
  87.6 4.7 %collective-permute-start.28 = (f32[144,128]{1,0:T(8,128)S(1)}, f32[144,128]{1,0:T(8,128)S(1)}, u32[]{:S(2)}, u32[]{:S(2)}) collective-permute-start(f32[144,128]{1,0:T(8,128)S(1)} %get-tuple-element.167), channel_id=1, source_target_pairs={{0,28},{1,29},{2,30},{3,31},{4,0},{5,1},{6,2},{7,3},{8,4},{9,5},{1... | collective-permute-start | bytes 221192 | tf_op jit(solution)/shard_map/ppermute | solution.py:257
  92.3 2.7 %shard_map.91 = (f32[512,128]{1,0:T(8,128)S(1)}, f32[512,128]{1,0:T(8,128)S(1)}, f32[384,128]{1,0:T(8,128)}, f32[384,128]{1,0:T(8,128)}) custom-call(bf16[384,512]{1,0:T(8,128)(2,1)S(1)} %get-tuple-element.89.onehot.refs_0_, bf16[384,512]{1,0:T(8,128)(2,1)S(1)} %get-tuple-element.90.onehot.refs_1_, bf16[512,512]{1,0:T(8,128)(2,1)S(1)} %get-tuple-element.91.refs_2_, ...), custom_call_target="tpu_custom_call" | custom-call | tf_op jit(solution)/shard_map/pallas_call | solution.py:20
  95.1 0.5 shard_map.94
  95.6 0.1 collective-permute-start.29
  95.7 0.5 shard_map.93.kept
  96.2 1.0 %collective-permute-done.29.got = f32[512,128]{1,0:T(8,128)S(1)} collective-permute-done((f32[512,128]{1,0:T(8,128)S(1)}, f32[512,128]{1,0:T(8,128)S(1)}, u32[]{:S(2)}, u32[]{:S(2)}) %collective-permute-start.29) | collective-permute-done | bytes 262176 | tf_op jit(solution)/shard_map/ppermute | solution.py:50
  97.2 0.8 shard_map.95
  (33 shorter events, 0.1 us)
Async XLA Ops:
  0.0 1.6 %copy-start = (f32[4,8,128,128]{3,2,1,0:T(8,128)S(1)}, f32[4,8,128,128]{3,2,1,0:T(8,128)}, u32[]{:S(2)}) copy-start(f32[4,8,128,128]{3,2,1,0:T(8,128)} %tiles.3) | copy-start | bytes 6291460
  1.6 0.7 copy-start.5
  2.3 1.6 %copy-start.1 = (f32[4,8,128,128]{3,2,1,0:T(8,128)S(1)}, f32[4,8,128,128]{3,2,1,0:T(8,128)}, u32[]{:S(2)}) copy-start(f32[4,8,128,128]{3,2,1,0:T(8,128)} %tiles.2) | copy-start | bytes 6291460
  2.3 1.6 %copy-start.6 = (s32[4,8]{1,0:T(4,128)S(1)}, s32[4,8]{1,0:T(4,128)}, u32[]{:S(2)}) copy-start(s32[4,8]{1,0:T(4,128)} %columns.2) | copy-start | bytes 388
  3.2 2.1 %copy-start.2 = (f32[512,256]{1,0:T(8,128)S(1)}, f32[512,256]{1,0:T(8,128)}, u32[]{:S(2)}) copy-start(f32[512,256]{1,0:T(8,128)} %x.2) | copy-start | bytes 1572868
  3.2 2.3 %copy-start.3 = (f32[512,256]{1,0:T(8,128)S(1)}, f32[512,256]{1,0:T(8,128)}, u32[]{:S(2)}) copy-start(f32[512,256]{1,0:T(8,128)} %x.3) | copy-start | bytes 1572868
  3.2 2.9 %copy-start.4 = (s32[8,48]{1,0:T(8,128)S(1)}, s32[8,48]{1,0:T(8,128)}, u32[]{:S(2)}) copy-start(s32[8,48]{1,0:T(8,128)} %rows_mine.1) | copy-start | bytes 4612
  3.2 15.0 %collective-permute-start.3 = (f32[4,7,128,128]{3,2,1,0:T(8,128)S(1)}, f32[4,7,128,128]{3,2,1,0:T(8,128)S(1)}, u32[]{:S(2)}, u32[]{:S(2)}) collective-permute-start(f32[4,7,128,128]{3,2,1,0:T(8,128)S(1)} %shard_map.78.total), channel_id=1, source_target_pairs={{0,1},{1,0},{2,3},{3,2},{4,5},{5,4},{6,7},{7,6},{8,9},{9,8},{10,11... | collective-permute-start | bytes 5505032 | tf_op jit(solution)/shard_map/ppermute | solution.py:50
  4.8 33.1 %collective-permute-start.2 = (f32[4,7,128,128]{3,2,1,0:T(8,128)S(1)}, f32[4,7,128,128]{3,2,1,0:T(8,128)S(1)}, u32[]{:S(2)}, u32[]{:S(2)}) collective-permute-start(f32[4,7,128,128]{3,2,1,0:T(8,128)S(1)} %shard_map.75.total), channel_id=1, source_target_pairs={{0,1},{1,0},{2,3},{3,2},{4,5},{5,4},{6,7},{7,6},{8,9},{9,8},{10,11... | collective-permute-start | bytes 5505032 | tf_op jit(solution)/shard_map/ppermute | solution.py:50
  5.4 5.2 %collective-permute-start = (f32[512,128]{1,0:T(8,128)S(1)}, f32[512,128]{1,0:T(8,128)S(1)}, u32[]{:S(2)}, u32[]{:S(2)}) collective-permute-start(f32[512,128]{1,0:T(8,128)S(1)} %get-tuple-element.88), channel_id=1, source_target_pairs={{0,1},{1,0},{2,3},{3,2},{4,5},{5,4},{6,7},{7,6},{8,9},{9,8},{10,11... | collective-permute-start | bytes 786440 | tf_op jit(solution)/shard_map/ppermute | solution.py:50
  5.5 12.7 %collective-permute-start.4 = (f32[512,128]{1,0:T(8,128)S(1)}, f32[512,128]{1,0:T(8,128)S(1)}, u32[]{:S(2)}, u32[]{:S(2)}) collective-permute-start(f32[512,128]{1,0:T(8,128)S(1)} %get-tuple-element.100), channel_id=1, source_target_pairs={{0,1},{1,0},{2,3},{3,2},{4,5},{5,4},{6,7},{7,6},{8,9},{9,8},{10,11... | collective-permute-start | bytes 786440 | tf_op jit(solution)/shard_map/ppermute | solution.py:50
  6.1 4.5 %collective-permute-start.1 = (s32[8,48]{1,0:T(8,128)S(1)}, s32[8,48]{1,0:T(8,128)S(1)}, u32[]{:S(2)}, u32[]{:S(2)}) collective-permute-start(s32[8,48]{1,0:T(8,128)S(1)} %copy-done.4), channel_id=1, source_target_pairs={{0,1},{1,0},{2,3},{3,2},{4,5},{5,4},{6,7},{7,6},{8,9},{9,8},{10,11... | collective-permute-start | bytes 4616 | tf_op jit(solution)/shard_map/ppermute | solution.py:50
  11.3 14.6 %collective-permute-start.5 = (f32[192,128]{1,0:T(8,128)S(1)}, f32[192,128]{1,0:T(8,128)S(1)}, u32[]{:S(2)}, u32[]{:S(2)}) collective-permute-start(f32[192,128]{1,0:T(8,128)S(1)} %get-tuple-element.108), channel_id=1, source_target_pairs={{0,2},{1,3},{2,4},{3,5},{4,6},{5,7},{6,8},{7,9},{8,10},{9,11},{10,... | collective-permute-start | bytes 294920 | tf_op jit(solution)/shard_map/ppermute | solution.py:257
  14.2 11.7 %collective-permute-start.7 = (f32[192,128]{1,0:T(8,128)S(1)}, f32[192,128]{1,0:T(8,128)S(1)}, u32[]{:S(2)}, u32[]{:S(2)}) collective-permute-start(f32[192,128]{1,0:T(8,128)S(1)} %get-tuple-element.110), channel_id=1, source_target_pairs={{0,30},{1,31},{2,0},{3,1},{4,2},{5,3},{6,4},{7,5},{8,6},{9,7},{10,... | collective-permute-start | bytes 294920 | tf_op jit(solution)/shard_map/ppermute | solution.py:257
  18.3 7.6 %collective-permute-start.6 = (f32[144,128]{1,0:T(8,128)S(1)}, f32[144,128]{1,0:T(8,128)S(1)}, u32[]{:S(2)}, u32[]{:S(2)}) collective-permute-start(f32[144,128]{1,0:T(8,128)S(1)} %get-tuple-element.109), channel_id=1, source_target_pairs={{0,4},{1,5},{2,6},{3,7},{4,8},{5,9},{6,10},{7,11},{8,12},{9,13},{1... | collective-permute-start | bytes 221192 | tf_op jit(solution)/shard_map/ppermute | solution.py:257
  18.3 7.6 %collective-permute-start.8 = (f32[144,128]{1,0:T(8,128)S(1)}, f32[144,128]{1,0:T(8,128)S(1)}, u32[]{:S(2)}, u32[]{:S(2)}) collective-permute-start(f32[144,128]{1,0:T(8,128)S(1)} %get-tuple-element.111), channel_id=1, source_target_pairs={{0,28},{1,29},{2,30},{3,31},{4,0},{5,1},{6,2},{7,3},{8,4},{9,5},{1... | collective-permute-start | bytes 221192 | tf_op jit(solution)/shard_map/ppermute | solution.py:257
  26.7 14.1 %collective-permute-start.9 = (f32[192,128]{1,0:T(8,128)S(1)}, f32[192,128]{1,0:T(8,128)S(1)}, u32[]{:S(2)}, u32[]{:S(2)}) collective-permute-start(f32[192,128]{1,0:T(8,128)S(1)} %get-tuple-element.125), channel_id=1, source_target_pairs={{0,2},{1,3},{2,4},{3,5},{4,6},{5,7},{6,8},{7,9},{8,10},{9,11},{10,... | collective-permute-start | bytes 294920 | tf_op jit(solution)/shard_map/ppermute | solution.py:257
  26.7 14.0 %collective-permute-start.11 = (f32[192,128]{1,0:T(8,128)S(1)}, f32[192,128]{1,0:T(8,128)S(1)}, u32[]{:S(2)}, u32[]{:S(2)}) collective-permute-start(f32[192,128]{1,0:T(8,128)S(1)} %get-tuple-element.127), channel_id=1, source_target_pairs={{0,30},{1,31},{2,0},{3,1},{4,2},{5,3},{6,4},{7,5},{8,6},{9,7},{10,... | collective-permute-start | bytes 294920 | tf_op jit(solution)/shard_map/ppermute | solution.py:257
  32.4 8.4 %collective-permute-start.10 = (f32[144,128]{1,0:T(8,128)S(1)}, f32[144,128]{1,0:T(8,128)S(1)}, u32[]{:S(2)}, u32[]{:S(2)}) collective-permute-start(f32[144,128]{1,0:T(8,128)S(1)} %get-tuple-element.126), channel_id=1, source_target_pairs={{0,4},{1,5},{2,6},{3,7},{4,8},{5,9},{6,10},{7,11},{8,12},{9,13},{1... | collective-permute-start | bytes 221192 | tf_op jit(solution)/shard_map/ppermute | solution.py:257
  32.4 8.4 %collective-permute-start.12 = (f32[144,128]{1,0:T(8,128)S(1)}, f32[144,128]{1,0:T(8,128)S(1)}, u32[]{:S(2)}, u32[]{:S(2)}) collective-permute-start(f32[144,128]{1,0:T(8,128)S(1)} %get-tuple-element.128), channel_id=1, source_target_pairs={{0,28},{1,29},{2,30},{3,31},{4,0},{5,1},{6,2},{7,3},{8,4},{9,5},{1... | collective-permute-start | bytes 221192 | tf_op jit(solution)/shard_map/ppermute | solution.py:257
  41.5 12.7 %collective-permute-start.13 = (f32[192,128]{1,0:T(8,128)S(1)}, f32[192,128]{1,0:T(8,128)S(1)}, u32[]{:S(2)}, u32[]{:S(2)}) collective-permute-start(f32[192,128]{1,0:T(8,128)S(1)} %get-tuple-element.138), channel_id=1, source_target_pairs={{0,2},{1,3},{2,4},{3,5},{4,6},{5,7},{6,8},{7,9},{8,10},{9,11},{10,... | collective-permute-start | bytes 294920 | tf_op jit(solution)/shard_map/ppermute | solution.py:257
  41.6 12.7 %collective-permute-start.15 = (f32[192,128]{1,0:T(8,128)S(1)}, f32[192,128]{1,0:T(8,128)S(1)}, u32[]{:S(2)}, u32[]{:S(2)}) collective-permute-start(f32[192,128]{1,0:T(8,128)S(1)} %get-tuple-element.140), channel_id=1, source_target_pairs={{0,30},{1,31},{2,0},{3,1},{4,2},{5,3},{6,4},{7,5},{8,6},{9,7},{10,... | collective-permute-start | bytes 294920 | tf_op jit(solution)/shard_map/ppermute | solution.py:257
  47.2 7.0 %collective-permute-start.14 = (f32[144,128]{1,0:T(8,128)S(1)}, f32[144,128]{1,0:T(8,128)S(1)}, u32[]{:S(2)}, u32[]{:S(2)}) collective-permute-start(f32[144,128]{1,0:T(8,128)S(1)} %get-tuple-element.139), channel_id=1, source_target_pairs={{0,4},{1,5},{2,6},{3,7},{4,8},{5,9},{6,10},{7,11},{8,12},{9,13},{1... | collective-permute-start | bytes 221192 | tf_op jit(solution)/shard_map/ppermute | solution.py:257
  47.2 7.0 %collective-permute-start.16 = (f32[144,128]{1,0:T(8,128)S(1)}, f32[144,128]{1,0:T(8,128)S(1)}, u32[]{:S(2)}, u32[]{:S(2)}) collective-permute-start(f32[144,128]{1,0:T(8,128)S(1)} %get-tuple-element.141), channel_id=1, source_target_pairs={{0,28},{1,29},{2,30},{3,31},{4,0},{5,1},{6,2},{7,3},{8,4},{9,5},{1... | collective-permute-start | bytes 221192 | tf_op jit(solution)/shard_map/ppermute | solution.py:257
  55.0 12.7 %collective-permute-start.17 = (f32[192,128]{1,0:T(8,128)S(1)}, f32[192,128]{1,0:T(8,128)S(1)}, u32[]{:S(2)}, u32[]{:S(2)}) collective-permute-start(f32[192,128]{1,0:T(8,128)S(1)} %get-tuple-element.147), channel_id=1, source_target_pairs={{0,2},{1,3},{2,4},{3,5},{4,6},{5,7},{6,8},{7,9},{8,10},{9,11},{10,... | collective-permute-start | bytes 294920 | tf_op jit(solution)/shard_map/ppermute | solution.py:257
  55.1 12.7 %collective-permute-start.19 = (f32[192,128]{1,0:T(8,128)S(1)}, f32[192,128]{1,0:T(8,128)S(1)}, u32[]{:S(2)}, u32[]{:S(2)}) collective-permute-start(f32[192,128]{1,0:T(8,128)S(1)} %get-tuple-element.149), channel_id=1, source_target_pairs={{0,30},{1,31},{2,0},{3,1},{4,2},{5,3},{6,4},{7,5},{8,6},{9,7},{10,... | collective-permute-start | bytes 294920 | tf_op jit(solution)/shard_map/ppermute | solution.py:257
  60.7 7.0 %collective-permute-start.18 = (f32[144,128]{1,0:T(8,128)S(1)}, f32[144,128]{1,0:T(8,128)S(1)}, u32[]{:S(2)}, u32[]{:S(2)}) collective-permute-start(f32[144,128]{1,0:T(8,128)S(1)} %get-tuple-element.148), channel_id=1, source_target_pairs={{0,4},{1,5},{2,6},{3,7},{4,8},{5,9},{6,10},{7,11},{8,12},{9,13},{1... | collective-permute-start | bytes 221192 | tf_op jit(solution)/shard_map/ppermute | solution.py:257
  60.7 7.0 %collective-permute-start.20 = (f32[144,128]{1,0:T(8,128)S(1)}, f32[144,128]{1,0:T(8,128)S(1)}, u32[]{:S(2)}, u32[]{:S(2)}) collective-permute-start(f32[144,128]{1,0:T(8,128)S(1)} %get-tuple-element.150), channel_id=1, source_target_pairs={{0,28},{1,29},{2,30},{3,31},{4,0},{5,1},{6,2},{7,3},{8,4},{9,5},{1... | collective-permute-start | bytes 221192 | tf_op jit(solution)/shard_map/ppermute | solution.py:257
  68.5 12.7 %collective-permute-start.21 = (f32[192,128]{1,0:T(8,128)S(1)}, f32[192,128]{1,0:T(8,128)S(1)}, u32[]{:S(2)}, u32[]{:S(2)}) collective-permute-start(f32[192,128]{1,0:T(8,128)S(1)} %get-tuple-element.156), channel_id=1, source_target_pairs={{0,2},{1,3},{2,4},{3,5},{4,6},{5,7},{6,8},{7,9},{8,10},{9,11},{10,... | collective-permute-start | bytes 294920 | tf_op jit(solution)/shard_map/ppermute | solution.py:257
  68.5 12.7 %collective-permute-start.23 = (f32[192,128]{1,0:T(8,128)S(1)}, f32[192,128]{1,0:T(8,128)S(1)}, u32[]{:S(2)}, u32[]{:S(2)}) collective-permute-start(f32[192,128]{1,0:T(8,128)S(1)} %get-tuple-element.158), channel_id=1, source_target_pairs={{0,30},{1,31},{2,0},{3,1},{4,2},{5,3},{6,4},{7,5},{8,6},{9,7},{10,... | collective-permute-start | bytes 294920 | tf_op jit(solution)/shard_map/ppermute | solution.py:257
  74.1 7.0 %collective-permute-start.22 = (f32[144,128]{1,0:T(8,128)S(1)}, f32[144,128]{1,0:T(8,128)S(1)}, u32[]{:S(2)}, u32[]{:S(2)}) collective-permute-start(f32[144,128]{1,0:T(8,128)S(1)} %get-tuple-element.157), channel_id=1, source_target_pairs={{0,4},{1,5},{2,6},{3,7},{4,8},{5,9},{6,10},{7,11},{8,12},{9,13},{1... | collective-permute-start | bytes 221192 | tf_op jit(solution)/shard_map/ppermute | solution.py:257
  74.1 7.0 %collective-permute-start.24 = (f32[144,128]{1,0:T(8,128)S(1)}, f32[144,128]{1,0:T(8,128)S(1)}, u32[]{:S(2)}, u32[]{:S(2)}) collective-permute-start(f32[144,128]{1,0:T(8,128)S(1)} %get-tuple-element.159), channel_id=1, source_target_pairs={{0,28},{1,29},{2,30},{3,31},{4,0},{5,1},{6,2},{7,3},{8,4},{9,5},{1... | collective-permute-start | bytes 221192 | tf_op jit(solution)/shard_map/ppermute | solution.py:257
  81.9 13.1 %collective-permute-start.25 = (f32[192,128]{1,0:T(8,128)S(1)}, f32[192,128]{1,0:T(8,128)S(1)}, u32[]{:S(2)}, u32[]{:S(2)}) collective-permute-start(f32[192,128]{1,0:T(8,128)S(1)} %get-tuple-element.164), channel_id=1, source_target_pairs={{0,2},{1,3},{2,4},{3,5},{4,6},{5,7},{6,8},{7,9},{8,10},{9,11},{10,... | collective-permute-start | bytes 294920 | tf_op jit(solution)/shard_map/ppermute | solution.py:257
  82.0 13.1 %collective-permute-start.27 = (f32[192,128]{1,0:T(8,128)S(1)}, f32[192,128]{1,0:T(8,128)S(1)}, u32[]{:S(2)}, u32[]{:S(2)}) collective-permute-start(f32[192,128]{1,0:T(8,128)S(1)} %get-tuple-element.166), channel_id=1, source_target_pairs={{0,30},{1,31},{2,0},{3,1},{4,2},{5,3},{6,4},{7,5},{8,6},{9,7},{10,... | collective-permute-start | bytes 294920 | tf_op jit(solution)/shard_map/ppermute | solution.py:257
  87.6 7.5 %collective-permute-start.26 = (f32[144,128]{1,0:T(8,128)S(1)}, f32[144,128]{1,0:T(8,128)S(1)}, u32[]{:S(2)}, u32[]{:S(2)}) collective-permute-start(f32[144,128]{1,0:T(8,128)S(1)} %get-tuple-element.165), channel_id=1, source_target_pairs={{0,4},{1,5},{2,6},{3,7},{4,8},{5,9},{6,10},{7,11},{8,12},{9,13},{1... | collective-permute-start | bytes 221192 | tf_op jit(solution)/shard_map/ppermute | solution.py:257
  87.6 7.5 %collective-permute-start.28 = (f32[144,128]{1,0:T(8,128)S(1)}, f32[144,128]{1,0:T(8,128)S(1)}, u32[]{:S(2)}, u32[]{:S(2)}) collective-permute-start(f32[144,128]{1,0:T(8,128)S(1)} %get-tuple-element.167), channel_id=1, source_target_pairs={{0,28},{1,29},{2,30},{3,31},{4,0},{5,1},{6,2},{7,3},{8,4},{9,5},{1... | collective-permute-start | bytes 221192 | tf_op jit(solution)/shard_map/ppermute | solution.py:257
  95.6 1.6 %collective-permute-start.29 = (f32[512,128]{1,0:T(8,128)S(1)}, f32[512,128]{1,0:T(8,128)S(1)}, u32[]{:S(2)}, u32[]{:S(2)}) collective-permute-start(f32[512,128]{1,0:T(8,128)S(1)} %shard_map.94), channel_id=1, source_target_pairs={{0,1},{1,0},{2,3},{3,2},{4,5},{5,4},{6,7},{7,6},{8,9},{9,8},{10,11... | collective-permute-start | bytes 786440 | tf_op jit(solution)/shard_map/ppermute | solution.py:50
where the time goes:
time: 98.2 us; the launch traced here: 98 us
  starting transfers between devices  65.5 us (67%)
  Pallas kernels  23.5 us (24%)
  waiting for transfers between devices  6.3 us (6%)
  local copies, waits for them, and re-layouts  2.37 us (2%)
    ppermute x24, starting transfers between devices, exchange(): arrived.append(lax.ppermute(piece, 'rows', pairs))  63.6 us
    pallas_call x23, Pallas kernels, call(): pl.pallas_call(kernel, out_shape=[jax.ShapeDtypeStruct(shape, dtype) for...  23.5 us
    ppermute x6, waiting for transfers between devices, swap(): return lax.ppermute(x, 'rows', [(i, i ^ 1) for i in range(devices)])  5.43 us
    unnamed x14, local copies, waits for them, and re-layouts  2.37 us
  transfers between devices with their start and end apart: 30, of which 5 were waited for; matrix products, arithmetic and copies ran while one was open for 0% of the time, Pallas kernels for 19%

commit v1 on v0

v1 whole, which is shorter than its diff:
```python
import functools

import jax
import jax.numpy as jnp
from jax import lax
from jax.experimental import pallas as pl
from jax.experimental.pallas import tpu as pltpu
from jax.sharding import PartitionSpec as P


STEPS = 3
GRANT = 14 * 2**20
WHOLE_GRANT = 121 * 2**19

VMEM = pl.BlockSpec(memory_space=pltpu.VMEM)
SMEM = pl.BlockSpec(memory_space=pltpu.SMEM)
ANY = pl.BlockSpec(memory_space=pl.ANY)
F32, BF16 = jnp.float32, jnp.bfloat16


def call(kernel, outs, in_specs, args, scratch=(), grant=GRANT, out_specs=None, aliases=None):
    return pl.pallas_call(
        kernel,
        out_shape=[jax.ShapeDtypeStruct(shape, dtype) for shape, dtype in outs],
        in_specs=in_specs,
        out_specs=out_specs or [VMEM] * len(outs),
        scratch_shapes=list(scratch),
        input_output_aliases=aliases or {},
        compiler_params=pltpu.CompilerParams(vmem_limit_bytes=grant),
    )(*args)


def partner_offset(offset_index):
    return (offset_index // 2 + 1) * (1 if offset_index % 2 == 0 else -1)


def routes(partners):
    found = {}
    for sender in range(2):
        for offset_index in range(partners):
            to = sender + partner_offset(offset_index)
            found.setdefault(to // 2, []).append((sender, offset_index, to % 2))
    far = sorted((hop for hop in found if hop > 0)) + sorted((hop for hop in found if hop < 0), reverse=True)
    return [(hop, found[hop]) for hop in [0] + far]


def side():
    return lax.rem(lax.axis_index("rows"), 2)


def swap(x):
    devices = lax.axis_size("rows")
    return lax.ppermute(x, "rows", [(i, i ^ 1) for i in range(devices)])


def split2(x):
    high = x.astype(BF16)
    return high, (x - high.astype(F32)).astype(BF16)


def dot(a, b):
    return jnp.dot(a, b, preferred_element_type=F32)


def product(m, x):
    half = x.shape[1] // 2
    got = dot(m, jnp.concatenate([x, x], axis=0))
    return got[:, :half] + got[:, half:]


def terms(x):
    return jnp.concatenate(split2(x), axis=1)


def pick_rows(onehot, x):
    half = x.shape[1]
    high = x.astype(BF16)
    rest = x - high.astype(F32)
    mid = rest.astype(BF16)
    low = (rest - mid.astype(F32)).astype(BF16)
    got = dot(onehot, jnp.concatenate([high, mid, low], axis=1))
    return got[:, :half] + (got[:, half : 2 * half] + got[:, 2 * half :])


def on_each_side(body):
    for place in range(2):

        @pl.when(side() == place)
        def _(place=place):
            body(place)


def fill_onehot(rows, onehot):
    lists, length = rows.shape
    width = onehot.shape[1]
    down = lax.broadcasted_iota(jnp.int32, (length, length), 0)
    along = lax.broadcasted_iota(jnp.int32, (length, length), 1)
    lanes = lax.broadcasted_iota(jnp.int32, (length, width), 1)
    for i in range(lists):
        spread = jnp.broadcast_to(rows[i : i + 1, :], (length, length))
        column = jnp.sum(jnp.where(down == along, spread, 0).astype(F32), axis=1, keepdims=True)
        hit = jnp.broadcast_to(column, (length, width)) == lanes.astype(F32)
        onehot[i * length : (i + 1) * length, :] = jnp.where(hit, 1.0, 0.0).astype(BF16)


def halves_kernel(x, keep, give):
    half = keep.shape[1]

    def body(place):
        keep[...] = x[:, place * half : (place + 1) * half]
        give[...] = x[:, (1 - place) * half : (2 - place) * half]

    on_each_side(body)


def fetch_merge_kernel(columns_in, tiles_in, total, columns, tiles, done):
    blocks = tiles.shape[0]
    fetch = [pltpu.make_async_copy(columns_in, columns, done.at[blocks])]
    fetch += [pltpu.make_async_copy(tiles_in.at[i], tiles.at[i], done.at[i]) for i in range(blocks)]
    for copy in fetch:
        copy.start()
    total[...] = jnp.zeros_like(total)
    fetch[0].wait()
    for block in range(blocks):
        fetch[1 + block].wait()
        add_blocks(columns, tiles, total, block)


def add_blocks(columns, tiles, total, block):
    for slot in range(tiles.shape[1]):
        column = columns[block, slot]
        total[block, column] += tiles[block, slot]


def merge_kernel(columns, tiles, total):
    total[...] = jnp.zeros_like(total)
    for block in range(tiles.shape[0]):
        add_blocks(columns, tiles, total, block)


def split_kernel(total, onehot, own, far, out):
    blocks, columns, size, _ = total.shape
    for block in range(blocks):
        at = slice(block * size, (block + 1) * size)
        for column in range(columns):
            to = own if column < blocks else far
            place = (column if column < blocks else column - blocks) * size
            low_place = place + to.shape[1] // 2
            to[at, place : place + size], to[at, low_place : low_place + size] = split2(total[block, column])
    out[...] = dot(onehot[...], far[...]).astype(BF16)


def deal(route, sender, rows, outs):
    for (_, group), out in zip(route, outs):
        length = out.shape[0] // len(group)
        for i, (source, offset_index, _) in enumerate(group):
            if source == sender:
                out[i * length : (i + 1) * length, :] = rows[offset_index * length : (offset_index + 1) * length]


def collect(route, receiver, arrived):
    found = {}
    for (_, group), piece in zip(route, arrived):
        length = piece.shape[0] // len(group)
        for i, (_, offset_index, target) in enumerate(group):
            if target == receiver:
                found[offset_index] = terms(piece[i * length : (i + 1) * length, :])
    return jnp.concatenate([found[i] for i in range(len(found))], axis=0)


def first_kernel(route, mine, other, rows_mine, rows_other, *refs):
    outs = refs[: len(route)]
    onehots = refs[len(route) :]
    fill_onehot(rows_mine, onehots[0])
    fill_onehot(rows_other, onehots[1])
    picked = [pick_rows(onehot[...], state[...]) for onehot, state in zip(onehots, (mine, other))]

    def body(place):
        for role in range(2):
            deal(route, role ^ place, picked[role], outs)

    on_each_side(body)


def own_kernel(route, has_source, first, *refs):
    refs = list(refs)

    def take(count):
        taken = refs[:count]
        del refs[:count]
        return taken

    onehots, owns = take(2), take(2)
    sources = take(2) if has_source else None
    states = take(2)
    if not first:
        fars, arrived = take(2), take(len(route))
    bases, picks = take(2), take(2)

    def body(place):
        now = [state[...] for state in states]
        if not first:
            halos = [collect(route, role ^ place, arrived) for role in range(2)]
            now = [now[role] + product(fars[role][...], halos[role]) for role in range(2)]
        total = [now[role] + product(owns[role][...], terms(now[role])) for role in range(2)]
        if has_source:
            total = [total[role] + sources[role][...] for role in range(2)]
        for role in range(2):
            bases[role][...] = total[role]
            got = dot(onehots[role][...], terms(total[role]))
            half = got.shape[1] // 2
            picks[role][...] = got[:, :half] + got[:, half:]

    if first:
        body(0)
    else:
        on_each_side(body)


def payload_kernel(route, *refs):
    count = len(route)
    picks, outs_of = refs[:2], refs[2:4]
    arrived, outs = refs[4 : 4 + count], refs[4 + count :]

    def body(place):
        halos = [collect(route, role ^ place, arrived) for role in range(2)]
        rows = [picks[role][...] + product(outs_of[role][...], halos[role]) for role in range(2)]
        for role in range(2):
            deal(route, role ^ place, rows[role], outs)

    on_each_side(body)


def give_back_kernel(route, base, far, *refs):
    arrived, out = refs[: len(route)], refs[len(route)]

    def body(place):
        out[...] = base[...] + product(far[...], collect(route, 1 - place, arrived))

    on_each_side(body)


def store_half(half, out, place, done):
    width = half.shape[1]
    copy = pltpu.make_async_copy(half, out.at[:, place * width : (place + 1) * width], done)
    copy.start()
    copy.wait()


def keep_kernel(route, base, far, *refs):
    arrived, (out, half, done) = refs[: len(route)], refs[len(route) :]

    def body(place):
        half[...] = base[...] + product(far[...], collect(route, place, arrived))
        store_half(half, out, place, done)

    on_each_side(body)


def join_kernel(got, begun, out, done):
    on_each_side(lambda place: store_half(got, out, 1 - place, done))


def on_device(
    tracers_init, source, explicit_tiles, implicit_tiles, explicit_cols, implicit_cols, send_rows
):
    devices = lax.axis_size("rows")
    local_rows, panels = tracers_init.shape
    half = panels // 2
    blocks, slots, size, _ = explicit_tiles.shape
    partners, length = send_rows.shape
    halo_rows = partners * length
    columns = blocks + halo_rows // size
    route = routes(partners)
    state_half = ((local_rows, half), F32)
    list_half = ((halo_rows, half), F32)
    pieces_out = [((len(group) * length, half), F32) for _, group in route]

    def halves(x):
        return call(halves_kernel, [state_half] * 2, [VMEM], (x,))

    def merge(tiles, cols):
        return call(merge_kernel, [((blocks, columns, size, size), F32)], [SMEM, VMEM], (cols, tiles))[0]

    def split(total, onehot):
        return call(
            split_kernel,
            [((local_rows, 2 * local_rows), BF16), ((local_rows, 2 * halo_rows), BF16), ((halo_rows, 2 * halo_rows), BF16)],
            [VMEM] * 2,
            (total, onehot),
        )

    def exchange(pieces):
        arrived = [pieces[0]]
        for (hop, _), piece in zip(route[1:], pieces[1:]):
            pairs = [(d, (d + 2 * hop) % devices) for d in range(devices)]
            arrived.append(lax.ppermute(piece, "rows", pairs))
        return arrived

    applies = 2 * STEPS
    for number in range(applies):
        if number == 0:
            rows_other = swap(send_rows)
            state, give = halves(tracers_init)
            state_other = swap(give)
            merged_e = call(
                fetch_merge_kernel,
                [((blocks, columns, size, size), F32)],
                [ANY] * 2,
                (explicit_cols, explicit_tiles),
                [
                    pltpu.SMEM((blocks, slots), jnp.int32),
                    pltpu.VMEM((blocks, slots, size, size), F32),
                    pltpu.SemaphoreType.DMA((blocks + 1,)),
                ],
                WHOLE_GRANT,
            )[0]
            merged_e_other = swap(merged_e)
            *pieces, onehot, onehot_other = call(
                functools.partial(first_kernel, route),
                pieces_out + [((halo_rows, local_rows), BF16)] * 2,
                [VMEM] * 4,
                (state, state_other, send_rows, rows_other),
            )
            states = (state, state_other)
        else:
            pieces = call(
                functools.partial(payload_kernel, route),
                pieces_out,
                [VMEM] * (4 + len(route)),
                (*picks, matrix[0][2], matrix[1][2], *arrived),
            )
        fresh = exchange(pieces)
        if number == 0:
            give_s = halves(source)
            sources = (give_s[0], swap(give_s[1]))
            matrix_e = (split(merged_e, onehot), split(merged_e_other, onehot_other))
            merged_i = merge(implicit_tiles, implicit_cols)
            merged_i_other = swap(merged_i)
        if number == 1:
            matrix_i = (split(merged_i, onehot), split(merged_i_other, onehot_other))
        last_matrix = matrix if number else None
        matrix = matrix_i if number % 2 else matrix_e
        has_source = number % 2 == 0
        args = (onehot, onehot_other, matrix[0][0], matrix[1][0])
        if has_source:
            args += sources
        args += tuple(states)
        if number:
            args += (last_matrix[0][1], last_matrix[1][1], *arrived)
        out = call(
            functools.partial(own_kernel, route, has_source, number == 0),
            [state_half] * 2 + [list_half] * 2,
            [VMEM] * len(args),
            args,
        )
        states, picks = out[:2], out[2:]
        arrived = fresh

    whole = [((local_rows, panels), F32)]
    done = pltpu.SemaphoreType.DMA
    got = swap(
        call(
            functools.partial(give_back_kernel, route),
            [state_half],
            [VMEM] * (2 + len(route)),
            (states[1], matrix[1][1], *arrived),
        )[0]
    )
    begun = call(
        functools.partial(keep_kernel, route),
        whole,
        [VMEM] * (2 + len(route)),
        (states[0], matrix[0][1], *arrived),
        [pltpu.VMEM((local_rows, half), F32), done],
        out_specs=[ANY],
    )
    return call(join_kernel, whole, [VMEM, ANY], (got, *begun), [done], out_specs=[ANY], aliases={1: 0})[0]


def solution(mesh):
    return jax.shard_map(
        on_device,
        mesh=mesh,
        in_specs=(
            P("rows", None),
            P("rows", None),
            P("rows", None, None, None),
            P("rows", None, None, None),
            P("rows", None),
            P("rows", None),
            P("rows", None),
        ),
        out_specs=P("rows", None),
        check_vma=False,
    )
```

time: 98.2 us -> 95.8 us (0.976)
  local copies, waits for them, and re-layouts: 2.37 us -> 0.03 us
  Pallas kernels: 23.5 us -> 21.8 us
  waiting for transfers between devices: 6.3 us -> 7.86 us
    unnamed x14 -> x12, local copies, waits for them, and re-layouts: 2.37 us -> 0.03 us
    ppermute x24, waiting for transfers between devices: 0.88 us -> 2.67 us  [exchange(): arrived.append(lax.ppermute(piece, 'rows', pairs))]
    pallas_call x23, Pallas kernels: 23.5 us -> 21.8 us  [call(): pl.pallas_call(kernel, out_shape=[jax.ShapeDtypeStruct(shape, dtype) for...]
  transfers between devices with their start and end apart: 30 -> 30, of which waited for: 5 -> 6; matrix products, arithmetic and copies ran while one was open for 0% -> 0% of each run, Pallas kernels for 19% -> 16%
where the time goes in v1:
time: 95.8 us; the launch traced here: 95.6 us
  starting transfers between devices  65.5 us (68%)
  Pallas kernels  21.8 us (23%)
  waiting for transfers between devices  7.86 us (8%)
    ppermute x24, starting transfers between devices, exchange(): arrived.append(lax.ppermute(piece, 'rows', pairs))  63.6 us
    pallas_call x23, Pallas kernels, call(): pl.pallas_call(kernel, out_shape=[jax.ShapeDtypeStruct(shape, dtype) for...  21.8 us
    ppermute x6, waiting for transfers between devices, swap(): return lax.ppermute(x, 'rows', [(i, i ^ 1) for i in range(devices)])  5.19 us
    ppermute x24, waiting for transfers between devices, exchange(): arrived.append(lax.ppermute(piece, 'rows', pairs))  2.67 us
  transfers between devices with their start and end apart: 30, of which 6 were waited for; matrix products, arithmetic and copies ran while one was open for 0% of the time, Pallas kernels for 16%

profile of v1, /device:TPU:0, one launch (start us, length us, event | category | flops | bytes accessed | tf_op | source)
XLA Modules:
  0.0 95.6 jit_solution(7881266068727581381)
XLA Ops:
  0.0 3.0 %shard_map.78.total = f32[4,7,128,128]{3,2,1,0:T(8,128)} custom-call(s32[4,8]{1,0:T(4,128)} %columns_in.1, f32[4,8,128,128]{3,2,1,0:T(8,128)} %tiles_in.1), custom_call_target="tpu_custom_call" | custom-call | tf_op jit(solution)/shard_map/pallas_call | solution.py:22
  3.1 0.0 copy-start.2
  3.1 0.0 copy-start.3
  3.1 0.0 copy-start.4
  3.1 0.6 collective-permute-start.3
  3.7 0.9 shard_map.75.total
  4.6 0.1 collective-permute-start.2
  4.7 0.5 collective-permute-start
  5.3 0.1 collective-permute-start.4
  5.4 0.5 collective-permute-start.1
  5.9 4.8 %collective-permute-done.1.rows_other = s32[8,48]{1,0:T(8,128)S(1)} collective-permute-done((s32[8,48]{1,0:T(8,128)S(1)}, s32[8,48]{1,0:T(8,128)S(1)}, u32[]{:S(2)}, u32[]{:S(2)}) %collective-permute-start.1) | collective-permute-done | bytes 1568 | tf_op jit(solution)/shard_map/ppermute | solution.py:53
  10.7 0.7 shard_map.74
  11.3 2.9 %collective-permute-start.5 = (f32[192,128]{1,0:T(8,128)S(1)}, f32[192,128]{1,0:T(8,128)S(1)}, u32[]{:S(2)}, u32[]{:S(2)}) collective-permute-start(f32[192,128]{1,0:T(8,128)S(1)} %get-tuple-element.90), channel_id=1, source_target_pairs={{0,2},{1,3},{2,4},{3,5},{4,6},{5,7},{6,8},{7,9},{8,10},{9,11},{10,... | collective-permute-start | bytes 294920 | tf_op jit(solution)/shard_map/ppermute | solution.py:297
  14.2 4.1 %collective-permute-start.7 = (f32[192,128]{1,0:T(8,128)S(1)}, f32[192,128]{1,0:T(8,128)S(1)}, u32[]{:S(2)}, u32[]{:S(2)}) collective-permute-start(f32[192,128]{1,0:T(8,128)S(1)} %get-tuple-element.92), channel_id=1, source_target_pairs={{0,30},{1,31},{2,0},{3,1},{4,2},{5,3},{6,4},{7,5},{8,6},{9,7},{10,... | collective-permute-start | bytes 294920 | tf_op jit(solution)/shard_map/ppermute | solution.py:297
  18.3 4.7 %collective-permute-start.8 = (f32[144,128]{1,0:T(8,128)S(1)}, f32[144,128]{1,0:T(8,128)S(1)}, u32[]{:S(2)}, u32[]{:S(2)}) collective-permute-start(f32[144,128]{1,0:T(8,128)S(1)} %get-tuple-element.93), channel_id=1, source_target_pairs={{0,28},{1,29},{2,30},{3,31},{4,0},{5,1},{6,2},{7,3},{8,4},{9,5},{1... | collective-permute-start | bytes 221192 | tf_op jit(solution)/shard_map/ppermute | solution.py:297
  23.0 0.8 shard_map.79
  23.8 0.8 shard_map.80
  24.6 1.0 %shard_map.82 = (f32[512,128]{1,0:T(8,128)S(1)}, f32[512,128]{1,0:T(8,128)S(1)}, f32[384,128]{1,0:T(8,128)S(1)}, f32[384,128]{1,0:T(8,128)S(1)}) custom-call(bf16[384,512]{1,0:T(8,128)(2,1)S(1)} %get-tuple-element.77.onehot.refs_0_, bf16[384,512]{1,0:T(8,128)(2,1)S(1)} %get-tuple-element.78.onehot.refs_1_, bf16[512,1024]{1,0:T(8,128)(2,1)S(1)} %get-tuple-element.81.refs_2_, ...), custom_call_target="tpu_custom_call" | custom-call | tf_op jit(solution)/shard_map/pallas_call | solution.py:22
  25.6 0.0 collective-permute-done.6.refs_10_.refs_6_
  25.6 0.0 collective-permute-done.7.refs_11_.refs_7_
  25.6 0.5 shard_map.84
  26.1 0.1 collective-permute-start.9
  26.2 5.6 %collective-permute-start.11 = (f32[192,128]{1,0:T(8,128)S(1)}, f32[192,128]{1,0:T(8,128)S(1)}, u32[]{:S(2)}, u32[]{:S(2)}) collective-permute-start(f32[192,128]{1,0:T(8,128)S(1)} %get-tuple-element.105), channel_id=1, source_target_pairs={{0,30},{1,31},{2,0},{3,1},{4,2},{5,3},{6,4},{7,5},{8,6},{9,7},{10,... | collective-permute-start | bytes 294920 | tf_op jit(solution)/shard_map/ppermute | solution.py:297
  31.8 4.7 %collective-permute-start.12 = (f32[144,128]{1,0:T(8,128)S(1)}, f32[144,128]{1,0:T(8,128)S(1)}, u32[]{:S(2)}, u32[]{:S(2)}) collective-permute-start(f32[144,128]{1,0:T(8,128)S(1)} %get-tuple-element.106), channel_id=1, source_target_pairs={{0,28},{1,29},{2,30},{3,31},{4,0},{5,1},{6,2},{7,3},{8,4},{9,5},{1... | collective-permute-start | bytes 221192 | tf_op jit(solution)/shard_map/ppermute | solution.py:297
  36.5 0.8 shard_map.76
  37.3 0.0 collective-permute-done.2.total
  37.3 0.8 shard_map.77
  38.1 1.5 %shard_map.83 = (f32[512,128]{1,0:T(8,128)S(1)}, f32[512,128]{1,0:T(8,128)S(1)}, f32[384,128]{1,0:T(8,128)S(1)}, f32[384,128]{1,0:T(8,128)S(1)}) custom-call(bf16[384,512]{1,0:T(8,128)(2,1)S(1)} %get-tuple-element.77.onehot.refs_0_, bf16[384,512]{1,0:T(8,128)(2,1)S(1)} %get-tuple-element.78.onehot.refs_1_, bf16[512,1024]{1,0:T(8,128)(2,1)S(1)} %get-tuple-element.79.refs_2_, ...), custom_call_target="tpu_custom_call" | custom-call | tf_op jit(solution)/shard_map/pallas_call | solution.py:22
  39.6 0.0 collective-permute-done.10.refs_12_.refs_6_
  39.6 0.0 collective-permute-done.12.refs_14_.refs_8_
  39.6 0.0 collective-permute-done.11.refs_13_.refs_7_
  39.6 0.5 shard_map.86
  40.1 0.1 collective-permute-start.13
  40.2 5.6 %collective-permute-start.15 = (f32[192,128]{1,0:T(8,128)S(1)}, f32[192,128]{1,0:T(8,128)S(1)}, u32[]{:S(2)}, u32[]{:S(2)}) collective-permute-start(f32[192,128]{1,0:T(8,128)S(1)} %get-tuple-element.116), channel_id=1, source_target_pairs={{0,30},{1,31},{2,0},{3,1},{4,2},{5,3},{6,4},{7,5},{8,6},{9,7},{10,... | collective-permute-start | bytes 294920 | tf_op jit(solution)/shard_map/ppermute | solution.py:297
  45.8 0.0 collective-permute-start.14
  45.8 4.7 %collective-permute-start.16 = (f32[144,128]{1,0:T(8,128)S(1)}, f32[144,128]{1,0:T(8,128)S(1)}, u32[]{:S(2)}, u32[]{:S(2)}) collective-permute-start(f32[144,128]{1,0:T(8,128)S(1)} %get-tuple-element.117), channel_id=1, source_target_pairs={{0,28},{1,29},{2,30},{3,31},{4,0},{5,1},{6,2},{7,3},{8,4},{9,5},{1... | collective-permute-start | bytes 221192 | tf_op jit(solution)/shard_map/ppermute | solution.py:297
  50.5 1.5 %shard_map.85 = (f32[512,128]{1,0:T(8,128)S(1)}, f32[512,128]{1,0:T(8,128)S(1)}, f32[384,128]{1,0:T(8,128)S(1)}, f32[384,128]{1,0:T(8,128)S(1)}) custom-call(bf16[384,512]{1,0:T(8,128)(2,1)S(1)} %get-tuple-element.77.onehot.refs_0_, bf16[384,512]{1,0:T(8,128)(2,1)S(1)} %get-tuple-element.78.onehot.refs_1_, bf16[512,1024]{1,0:T(8,128)(2,1)S(1)} %get-tuple-element.81.refs_2_, ...), custom_call_target="tpu_custom_call" | custom-call | tf_op jit(solution)/shard_map/pallas_call | solution.py:22
  52.0 0.8 collective-permute-done.14.refs_10_.refs_6_
  52.8 0.0 collective-permute-done.15.refs_11_.refs_7_
  52.9 0.7 shard_map.88
  53.5 0.1 collective-permute-start.17
  53.6 5.6 %collective-permute-start.19 = (f32[192,128]{1,0:T(8,128)S(1)}, f32[192,128]{1,0:T(8,128)S(1)}, u32[]{:S(2)}, u32[]{:S(2)}) collective-permute-start(f32[192,128]{1,0:T(8,128)S(1)} %get-tuple-element.125), channel_id=1, source_target_pairs={{0,30},{1,31},{2,0},{3,1},{4,2},{5,3},{6,4},{7,5},{8,6},{9,7},{10,... | collective-permute-start | bytes 294920 | tf_op jit(solution)/shard_map/ppermute | solution.py:297
  59.2 0.0 collective-permute-start.18
  59.2 4.7 %collective-permute-start.20 = (f32[144,128]{1,0:T(8,128)S(1)}, f32[144,128]{1,0:T(8,128)S(1)}, u32[]{:S(2)}, u32[]{:S(2)}) collective-permute-start(f32[144,128]{1,0:T(8,128)S(1)} %get-tuple-element.126), channel_id=1, source_target_pairs={{0,28},{1,29},{2,30},{3,31},{4,0},{5,1},{6,2},{7,3},{8,4},{9,5},{1... | collective-permute-start | bytes 221192 | tf_op jit(solution)/shard_map/ppermute | solution.py:297
  63.9 1.5 %shard_map.87 = (f32[512,128]{1,0:T(8,128)S(1)}, f32[512,128]{1,0:T(8,128)S(1)}, f32[384,128]{1,0:T(8,128)S(1)}, f32[384,128]{1,0:T(8,128)S(1)}) custom-call(bf16[384,512]{1,0:T(8,128)(2,1)S(1)} %get-tuple-element.77.onehot.refs_0_, bf16[384,512]{1,0:T(8,128)(2,1)S(1)} %get-tuple-element.78.onehot.refs_1_, bf16[512,1024]{1,0:T(8,128)(2,1)S(1)} %get-tuple-element.79.refs_2_, ...), custom_call_target="tpu_custom_call" | custom-call | tf_op jit(solution)/shard_map/pallas_call | solution.py:22
  65.4 0.8 collective-permute-done.18.refs_12_.refs_6_
  66.3 0.0 collective-permute-done.17.refs_11_.refs_5_
  66.3 0.5 shard_map.90
  66.8 0.1 collective-permute-start.21
  66.8 5.6 %collective-permute-start.23 = (f32[192,128]{1,0:T(8,128)S(1)}, f32[192,128]{1,0:T(8,128)S(1)}, u32[]{:S(2)}, u32[]{:S(2)}) collective-permute-start(f32[192,128]{1,0:T(8,128)S(1)} %get-tuple-element.134), channel_id=1, source_target_pairs={{0,30},{1,31},{2,0},{3,1},{4,2},{5,3},{6,4},{7,5},{8,6},{9,7},{10,... | collective-permute-start | bytes 294920 | tf_op jit(solution)/shard_map/ppermute | solution.py:297
  72.5 4.7 %collective-permute-start.24 = (f32[144,128]{1,0:T(8,128)S(1)}, f32[144,128]{1,0:T(8,128)S(1)}, u32[]{:S(2)}, u32[]{:S(2)}) collective-permute-start(f32[144,128]{1,0:T(8,128)S(1)} %get-tuple-element.135), channel_id=1, source_target_pairs={{0,28},{1,29},{2,30},{3,31},{4,0},{5,1},{6,2},{7,3},{8,4},{9,5},{1... | collective-permute-start | bytes 221192 | tf_op jit(solution)/shard_map/ppermute | solution.py:297
  77.2 1.5 %shard_map.89 = (f32[512,128]{1,0:T(8,128)S(1)}, f32[512,128]{1,0:T(8,128)S(1)}, f32[384,128]{1,0:T(8,128)S(1)}, f32[384,128]{1,0:T(8,128)S(1)}) custom-call(bf16[384,512]{1,0:T(8,128)(2,1)S(1)} %get-tuple-element.77.onehot.refs_0_, bf16[384,512]{1,0:T(8,128)(2,1)S(1)} %get-tuple-element.78.onehot.refs_1_, bf16[512,1024]{1,0:T(8,128)(2,1)S(1)} %get-tuple-element.81.refs_2_, ...), custom_call_target="tpu_custom_call" | custom-call | tf_op jit(solution)/shard_map/pallas_call | solution.py:22
  78.7 0.8 collective-permute-done.22.refs_10_.refs_6_
  79.5 0.5 shard_map.92
  80.0 0.1 collective-permute-start.25
  80.1 5.6 %collective-permute-start.27 = (f32[192,128]{1,0:T(8,128)S(1)}, f32[192,128]{1,0:T(8,128)S(1)}, u32[]{:S(2)}, u32[]{:S(2)}) collective-permute-start(f32[192,128]{1,0:T(8,128)S(1)} %get-tuple-element.142), channel_id=1, source_target_pairs={{0,30},{1,31},{2,0},{3,1},{4,2},{5,3},{6,4},{7,5},{8,6},{9,7},{10,... | collective-permute-start | bytes 294920 | tf_op jit(solution)/shard_map/ppermute | solution.py:297
  85.7 4.7 %collective-permute-start.28 = (f32[144,128]{1,0:T(8,128)S(1)}, f32[144,128]{1,0:T(8,128)S(1)}, u32[]{:S(2)}, u32[]{:S(2)}) collective-permute-start(f32[144,128]{1,0:T(8,128)S(1)} %get-tuple-element.143), channel_id=1, source_target_pairs={{0,28},{1,29},{2,30},{3,31},{4,0},{5,1},{6,2},{7,3},{8,4},{9,5},{1... | collective-permute-start | bytes 221192 | tf_op jit(solution)/shard_map/ppermute | solution.py:297
  90.4 2.2 %shard_map.91 = (f32[512,128]{1,0:T(8,128)S(1)}, f32[512,128]{1,0:T(8,128)S(1)}, f32[384,128]{1,0:T(8,128)}, f32[384,128]{1,0:T(8,128)}) custom-call(bf16[384,512]{1,0:T(8,128)(2,1)S(1)} %get-tuple-element.77.onehot.refs_0_, bf16[384,512]{1,0:T(8,128)(2,1)S(1)} %get-tuple-element.78.onehot.refs_1_, bf16[512,1024]{1,0:T(8,128)(2,1)S(1)} %get-tuple-element.79.refs_2_, ...), custom_call_target="tpu_custom_call" | custom-call | tf_op jit(solution)/shard_map/pallas_call | solution.py:22
  92.6 0.1 collective-permute-done.26.refs_2_
  92.8 0.4 shard_map.93
  93.2 0.1 collective-permute-start.29
  93.2 1.1 %shard_map.94.begun = f32[512,256]{1,0:T(8,128)} custom-call(f32[512,128]{1,0:T(8,128)S(1)} %get-tuple-element.144.base, bf16[512,768]{1,0:T(8,128)(2,1)S(1)} %get-tuple-element.96.refs_8_.far, f32[96,128]{1,0:T(8,128)S(1)} %get-tuple-element.139.refs_0_, f32[192,128]{1,0:T(8,128)S(1)} %collective-permute-done.25.refs_1_, ...), custom_call_target="tpu_custom_call" | custom-call | tf_op jit(solution)/shard_map/pallas_call | solution.py:22
  94.3 0.4 collective-permute-done.29.got
  94.8 0.7 shard_map.95
  (31 shorter events, 0.1 us)
Async XLA Ops:
  0.0 3.7 %copy-start.5 = (s32[4,8]{1,0:T(4,128)S(1)}, s32[4,8]{1,0:T(4,128)}, u32[]{:S(2)}) copy-start(s32[4,8]{1,0:T(4,128)} %columns.1) | copy-start | bytes 388
  0.0 3.7 %copy-start.1 = (f32[4,8,128,128]{3,2,1,0:T(8,128)S(1)}, f32[4,8,128,128]{3,2,1,0:T(8,128)}, u32[]{:S(2)}) copy-start(f32[4,8,128,128]{3,2,1,0:T(8,128)} %tiles.1) | copy-start | bytes 6291460
  3.1 1.6 %copy-start.2 = (f32[512,256]{1,0:T(8,128)S(1)}, f32[512,256]{1,0:T(8,128)}, u32[]{:S(2)}) copy-start(f32[512,256]{1,0:T(8,128)} %x.2) | copy-start | bytes 1572868
  3.1 2.2 %copy-start.3 = (f32[512,256]{1,0:T(8,128)S(1)}, f32[512,256]{1,0:T(8,128)}, u32[]{:S(2)}) copy-start(f32[512,256]{1,0:T(8,128)} %x.3) | copy-start | bytes 1572868
  3.1 2.3 %copy-start.4 = (s32[8,48]{1,0:T(8,128)S(1)}, s32[8,48]{1,0:T(8,128)}, u32[]{:S(2)}) copy-start(s32[8,48]{1,0:T(8,128)} %rows_mine.1) | copy-start | bytes 4612
  3.1 19.9 %copy-start = (f32[4,7,128,128]{3,2,1,0:T(8,128)S(1)}, f32[4,7,128,128]{3,2,1,0:T(8,128)}, u32[]{:S(2)}) copy-start(f32[4,7,128,128]{3,2,1,0:T(8,128)} %shard_map.78.total) | copy-start | bytes 5505028
  3.1 15.2 %collective-permute-start.3 = (f32[4,7,128,128]{3,2,1,0:T(8,128)}, f32[4,7,128,128]{3,2,1,0:T(8,128)S(1)}, u32[]{:S(2)}, u32[]{:S(2)}) collective-permute-start(f32[4,7,128,128]{3,2,1,0:T(8,128)} %shard_map.78.total), channel_id=1, source_target_pairs={{0,1},{1,0},{2,3},{3,2},{4,5},{5,4},{6,7},{7,6},{8,9},{9,8},{10,11... | collective-permute-start | bytes 5505032 | tf_op jit(solution)/shard_map/ppermute | solution.py:53
  4.6 32.7 %collective-permute-start.2 = (f32[4,7,128,128]{3,2,1,0:T(8,128)S(1)}, f32[4,7,128,128]{3,2,1,0:T(8,128)S(1)}, u32[]{:S(2)}, u32[]{:S(2)}) collective-permute-start(f32[4,7,128,128]{3,2,1,0:T(8,128)S(1)} %shard_map.75.total), channel_id=1, source_target_pairs={{0,1},{1,0},{2,3},{3,2},{4,5},{5,4},{6,7},{7,6},{8,9},{9,8},{10,11... | collective-permute-start | bytes 5505032 | tf_op jit(solution)/shard_map/ppermute | solution.py:53
  4.7 5.9 %collective-permute-start = (f32[512,128]{1,0:T(8,128)S(1)}, f32[512,128]{1,0:T(8,128)S(1)}, u32[]{:S(2)}, u32[]{:S(2)}) collective-permute-start(f32[512,128]{1,0:T(8,128)S(1)} %get-tuple-element.76), channel_id=1, source_target_pairs={{0,1},{1,0},{2,3},{3,2},{4,5},{5,4},{6,7},{7,6},{8,9},{9,8},{10,11... | collective-permute-start | bytes 786440 | tf_op jit(solution)/shard_map/ppermute | solution.py:53
  5.3 13.0 %collective-permute-start.4 = (f32[512,128]{1,0:T(8,128)S(1)}, f32[512,128]{1,0:T(8,128)S(1)}, u32[]{:S(2)}, u32[]{:S(2)}) collective-permute-start(f32[512,128]{1,0:T(8,128)S(1)} %get-tuple-element.84), channel_id=1, source_target_pairs={{0,1},{1,0},{2,3},{3,2},{4,5},{5,4},{6,7},{7,6},{8,9},{9,8},{10,11... | collective-permute-start | bytes 786440 | tf_op jit(solution)/shard_map/ppermute | solution.py:53
  5.4 5.2 %collective-permute-start.1 = (s32[8,48]{1,0:T(8,128)S(1)}, s32[8,48]{1,0:T(8,128)S(1)}, u32[]{:S(2)}, u32[]{:S(2)}) collective-permute-start(s32[8,48]{1,0:T(8,128)S(1)} %copy-done.4), channel_id=1, source_target_pairs={{0,1},{1,0},{2,3},{3,2},{4,5},{5,4},{6,7},{7,6},{8,9},{9,8},{10,11... | collective-permute-start | bytes 4616 | tf_op jit(solution)/shard_map/ppermute | solution.py:53
  11.3 14.3 %collective-permute-start.5 = (f32[192,128]{1,0:T(8,128)S(1)}, f32[192,128]{1,0:T(8,128)S(1)}, u32[]{:S(2)}, u32[]{:S(2)}) collective-permute-start(f32[192,128]{1,0:T(8,128)S(1)} %get-tuple-element.90), channel_id=1, source_target_pairs={{0,2},{1,3},{2,4},{3,5},{4,6},{5,7},{6,8},{7,9},{8,10},{9,11},{10,... | collective-permute-start | bytes 294920 | tf_op jit(solution)/shard_map/ppermute | solution.py:297
  14.2 11.4 %collective-permute-start.7 = (f32[192,128]{1,0:T(8,128)S(1)}, f32[192,128]{1,0:T(8,128)S(1)}, u32[]{:S(2)}, u32[]{:S(2)}) collective-permute-start(f32[192,128]{1,0:T(8,128)S(1)} %get-tuple-element.92), channel_id=1, source_target_pairs={{0,30},{1,31},{2,0},{3,1},{4,2},{5,3},{6,4},{7,5},{8,6},{9,7},{10,... | collective-permute-start | bytes 294920 | tf_op jit(solution)/shard_map/ppermute | solution.py:297
  18.3 7.3 %collective-permute-start.6 = (f32[144,128]{1,0:T(8,128)S(1)}, f32[144,128]{1,0:T(8,128)S(1)}, u32[]{:S(2)}, u32[]{:S(2)}) collective-permute-start(f32[144,128]{1,0:T(8,128)S(1)} %get-tuple-element.91), channel_id=1, source_target_pairs={{0,4},{1,5},{2,6},{3,7},{4,8},{5,9},{6,10},{7,11},{8,12},{9,13},{1... | collective-permute-start | bytes 221192 | tf_op jit(solution)/shard_map/ppermute | solution.py:297
  18.3 7.3 %collective-permute-start.8 = (f32[144,128]{1,0:T(8,128)S(1)}, f32[144,128]{1,0:T(8,128)S(1)}, u32[]{:S(2)}, u32[]{:S(2)}) collective-permute-start(f32[144,128]{1,0:T(8,128)S(1)} %get-tuple-element.93), channel_id=1, source_target_pairs={{0,28},{1,29},{2,30},{3,31},{4,0},{5,1},{6,2},{7,3},{8,4},{9,5},{1... | collective-permute-start | bytes 221192 | tf_op jit(solution)/shard_map/ppermute | solution.py:297
  26.1 13.5 %collective-permute-start.9 = (f32[192,128]{1,0:T(8,128)S(1)}, f32[192,128]{1,0:T(8,128)S(1)}, u32[]{:S(2)}, u32[]{:S(2)}) collective-permute-start(f32[192,128]{1,0:T(8,128)S(1)} %get-tuple-element.103), channel_id=1, source_target_pairs={{0,2},{1,3},{2,4},{3,5},{4,6},{5,7},{6,8},{7,9},{8,10},{9,11},{10,... | collective-permute-start | bytes 294920 | tf_op jit(solution)/shard_map/ppermute | solution.py:297
  26.2 13.4 %collective-permute-start.11 = (f32[192,128]{1,0:T(8,128)S(1)}, f32[192,128]{1,0:T(8,128)S(1)}, u32[]{:S(2)}, u32[]{:S(2)}) collective-permute-start(f32[192,128]{1,0:T(8,128)S(1)} %get-tuple-element.105), channel_id=1, source_target_pairs={{0,30},{1,31},{2,0},{3,1},{4,2},{5,3},{6,4},{7,5},{8,6},{9,7},{10,... | collective-permute-start | bytes 294920 | tf_op jit(solution)/shard_map/ppermute | solution.py:297
  31.8 7.8 %collective-permute-start.10 = (f32[144,128]{1,0:T(8,128)S(1)}, f32[144,128]{1,0:T(8,128)S(1)}, u32[]{:S(2)}, u32[]{:S(2)}) collective-permute-start(f32[144,128]{1,0:T(8,128)S(1)} %get-tuple-element.104), channel_id=1, source_target_pairs={{0,4},{1,5},{2,6},{3,7},{4,8},{5,9},{6,10},{7,11},{8,12},{9,13},{1... | collective-permute-start | bytes 221192 | tf_op jit(solution)/shard_map/ppermute | solution.py:297
  31.8 7.8 %collective-permute-start.12 = (f32[144,128]{1,0:T(8,128)S(1)}, f32[144,128]{1,0:T(8,128)S(1)}, u32[]{:S(2)}, u32[]{:S(2)}) collective-permute-start(f32[144,128]{1,0:T(8,128)S(1)} %get-tuple-element.106), channel_id=1, source_target_pairs={{0,28},{1,29},{2,30},{3,31},{4,0},{5,1},{6,2},{7,3},{8,4},{9,5},{1... | collective-permute-start | bytes 221192 | tf_op jit(solution)/shard_map/ppermute | solution.py:297
  40.1 12.7 %collective-permute-start.13 = (f32[192,128]{1,0:T(8,128)S(1)}, f32[192,128]{1,0:T(8,128)S(1)}, u32[]{:S(2)}, u32[]{:S(2)}) collective-permute-start(f32[192,128]{1,0:T(8,128)S(1)} %get-tuple-element.114), channel_id=1, source_target_pairs={{0,2},{1,3},{2,4},{3,5},{4,6},{5,7},{6,8},{7,9},{8,10},{9,11},{10,... | collective-permute-start | bytes 294920 | tf_op jit(solution)/shard_map/ppermute | solution.py:297
  40.2 12.7 %collective-permute-start.15 = (f32[192,128]{1,0:T(8,128)S(1)}, f32[192,128]{1,0:T(8,128)S(1)}, u32[]{:S(2)}, u32[]{:S(2)}) collective-permute-start(f32[192,128]{1,0:T(8,128)S(1)} %get-tuple-element.116), channel_id=1, source_target_pairs={{0,30},{1,31},{2,0},{3,1},{4,2},{5,3},{6,4},{7,5},{8,6},{9,7},{10,... | collective-permute-start | bytes 294920 | tf_op jit(solution)/shard_map/ppermute | solution.py:297
  45.8 7.0 %collective-permute-start.14 = (f32[144,128]{1,0:T(8,128)S(1)}, f32[144,128]{1,0:T(8,128)S(1)}, u32[]{:S(2)}, u32[]{:S(2)}) collective-permute-start(f32[144,128]{1,0:T(8,128)S(1)} %get-tuple-element.115), channel_id=1, source_target_pairs={{0,4},{1,5},{2,6},{3,7},{4,8},{5,9},{6,10},{7,11},{8,12},{9,13},{1... | collective-permute-start | bytes 221192 | tf_op jit(solution)/shard_map/ppermute | solution.py:297
  45.8 7.0 %collective-permute-start.16 = (f32[144,128]{1,0:T(8,128)S(1)}, f32[144,128]{1,0:T(8,128)S(1)}, u32[]{:S(2)}, u32[]{:S(2)}) collective-permute-start(f32[144,128]{1,0:T(8,128)S(1)} %get-tuple-element.117), channel_id=1, source_target_pairs={{0,28},{1,29},{2,30},{3,31},{4,0},{5,1},{6,2},{7,3},{8,4},{9,5},{1... | collective-permute-start | bytes 221192 | tf_op jit(solution)/shard_map/ppermute | solution.py:297
  53.5 12.7 %collective-permute-start.17 = (f32[192,128]{1,0:T(8,128)S(1)}, f32[192,128]{1,0:T(8,128)S(1)}, u32[]{:S(2)}, u32[]{:S(2)}) collective-permute-start(f32[192,128]{1,0:T(8,128)S(1)} %get-tuple-element.123), channel_id=1, source_target_pairs={{0,2},{1,3},{2,4},{3,5},{4,6},{5,7},{6,8},{7,9},{8,10},{9,11},{10,... | collective-permute-start | bytes 294920 | tf_op jit(solution)/shard_map/ppermute | solution.py:297
  53.6 12.7 %collective-permute-start.19 = (f32[192,128]{1,0:T(8,128)S(1)}, f32[192,128]{1,0:T(8,128)S(1)}, u32[]{:S(2)}, u32[]{:S(2)}) collective-permute-start(f32[192,128]{1,0:T(8,128)S(1)} %get-tuple-element.125), channel_id=1, source_target_pairs={{0,30},{1,31},{2,0},{3,1},{4,2},{5,3},{6,4},{7,5},{8,6},{9,7},{10,... | collective-permute-start | bytes 294920 | tf_op jit(solution)/shard_map/ppermute | solution.py:297
  59.2 7.0 %collective-permute-start.18 = (f32[144,128]{1,0:T(8,128)S(1)}, f32[144,128]{1,0:T(8,128)S(1)}, u32[]{:S(2)}, u32[]{:S(2)}) collective-permute-start(f32[144,128]{1,0:T(8,128)S(1)} %get-tuple-element.124), channel_id=1, source_target_pairs={{0,4},{1,5},{2,6},{3,7},{4,8},{5,9},{6,10},{7,11},{8,12},{9,13},{1... | collective-permute-start | bytes 221192 | tf_op jit(solution)/shard_map/ppermute | solution.py:297
  59.2 7.0 %collective-permute-start.20 = (f32[144,128]{1,0:T(8,128)S(1)}, f32[144,128]{1,0:T(8,128)S(1)}, u32[]{:S(2)}, u32[]{:S(2)}) collective-permute-start(f32[144,128]{1,0:T(8,128)S(1)} %get-tuple-element.126), channel_id=1, source_target_pairs={{0,28},{1,29},{2,30},{3,31},{4,0},{5,1},{6,2},{7,3},{8,4},{9,5},{1... | collective-permute-start | bytes 221192 | tf_op jit(solution)/shard_map/ppermute | solution.py:297
  66.8 12.7 %collective-permute-start.21 = (f32[192,128]{1,0:T(8,128)S(1)}, f32[192,128]{1,0:T(8,128)S(1)}, u32[]{:S(2)}, u32[]{:S(2)}) collective-permute-start(f32[192,128]{1,0:T(8,128)S(1)} %get-tuple-element.132), channel_id=1, source_target_pairs={{0,2},{1,3},{2,4},{3,5},{4,6},{5,7},{6,8},{7,9},{8,10},{9,11},{10,... | collective-permute-start | bytes 294920 | tf_op jit(solution)/shard_map/ppermute | solution.py:297
  66.8 12.7 %collective-permute-start.23 = (f32[192,128]{1,0:T(8,128)S(1)}, f32[192,128]{1,0:T(8,128)S(1)}, u32[]{:S(2)}, u32[]{:S(2)}) collective-permute-start(f32[192,128]{1,0:T(8,128)S(1)} %get-tuple-element.134), channel_id=1, source_target_pairs={{0,30},{1,31},{2,0},{3,1},{4,2},{5,3},{6,4},{7,5},{8,6},{9,7},{10,... | collective-permute-start | bytes 294920 | tf_op jit(solution)/shard_map/ppermute | solution.py:297
  72.5 7.0 %collective-permute-start.22 = (f32[144,128]{1,0:T(8,128)S(1)}, f32[144,128]{1,0:T(8,128)S(1)}, u32[]{:S(2)}, u32[]{:S(2)}) collective-permute-start(f32[144,128]{1,0:T(8,128)S(1)} %get-tuple-element.133), channel_id=1, source_target_pairs={{0,4},{1,5},{2,6},{3,7},{4,8},{5,9},{6,10},{7,11},{8,12},{9,13},{1... | collective-permute-start | bytes 221192 | tf_op jit(solution)/shard_map/ppermute | solution.py:297
  72.5 7.0 %collective-permute-start.24 = (f32[144,128]{1,0:T(8,128)S(1)}, f32[144,128]{1,0:T(8,128)S(1)}, u32[]{:S(2)}, u32[]{:S(2)}) collective-permute-start(f32[144,128]{1,0:T(8,128)S(1)} %get-tuple-element.135), channel_id=1, source_target_pairs={{0,28},{1,29},{2,30},{3,31},{4,0},{5,1},{6,2},{7,3},{8,4},{9,5},{1... | collective-permute-start | bytes 221192 | tf_op jit(solution)/shard_map/ppermute | solution.py:297
  80.0 12.7 %collective-permute-start.25 = (f32[192,128]{1,0:T(8,128)S(1)}, f32[192,128]{1,0:T(8,128)S(1)}, u32[]{:S(2)}, u32[]{:S(2)}) collective-permute-start(f32[192,128]{1,0:T(8,128)S(1)} %get-tuple-element.140), channel_id=1, source_target_pairs={{0,2},{1,3},{2,4},{3,5},{4,6},{5,7},{6,8},{7,9},{8,10},{9,11},{10,... | collective-permute-start | bytes 294920 | tf_op jit(solution)/shard_map/ppermute | solution.py:297
  80.1 12.7 %collective-permute-start.27 = (f32[192,128]{1,0:T(8,128)S(1)}, f32[192,128]{1,0:T(8,128)S(1)}, u32[]{:S(2)}, u32[]{:S(2)}) collective-permute-start(f32[192,128]{1,0:T(8,128)S(1)} %get-tuple-element.142), channel_id=1, source_target_pairs={{0,30},{1,31},{2,0},{3,1},{4,2},{5,3},{6,4},{7,5},{8,6},{9,7},{10,... | collective-permute-start | bytes 294920 | tf_op jit(solution)/shard_map/ppermute | solution.py:297
  85.7 7.0 %collective-permute-start.26 = (f32[144,128]{1,0:T(8,128)S(1)}, f32[144,128]{1,0:T(8,128)S(1)}, u32[]{:S(2)}, u32[]{:S(2)}) collective-permute-start(f32[144,128]{1,0:T(8,128)S(1)} %get-tuple-element.141), channel_id=1, source_target_pairs={{0,4},{1,5},{2,6},{3,7},{4,8},{5,9},{6,10},{7,11},{8,12},{9,13},{1... | collective-permute-start | bytes 221192 | tf_op jit(solution)/shard_map/ppermute | solution.py:297
  85.7 7.0 %collective-permute-start.28 = (f32[144,128]{1,0:T(8,128)S(1)}, f32[144,128]{1,0:T(8,128)S(1)}, u32[]{:S(2)}, u32[]{:S(2)}) collective-permute-start(f32[144,128]{1,0:T(8,128)S(1)} %get-tuple-element.143), channel_id=1, source_target_pairs={{0,28},{1,29},{2,30},{3,31},{4,0},{5,1},{6,2},{7,3},{8,4},{9,5},{1... | collective-permute-start | bytes 221192 | tf_op jit(solution)/shard_map/ppermute | solution.py:297
  93.2 1.6 %collective-permute-start.29 = (f32[512,128]{1,0:T(8,128)S(1)}, f32[512,128]{1,0:T(8,128)S(1)}, u32[]{:S(2)}, u32[]{:S(2)}) collective-permute-start(f32[512,128]{1,0:T(8,128)S(1)} %shard_map.93), channel_id=1, source_target_pairs={{0,1},{1,0},{2,3},{3,2},{4,5},{5,4},{6,7},{7,6},{8,9},{9,8},{10,11... | collective-permute-start | bytes 786440 | tf_op jit(solution)/shard_map/ppermute | solution.py:53

commit v2 on v1

--- a/solution.py
+++ b/solution.py
@@ -34,14 +34,60 @@
     return (offset_index // 2 + 1) * (1 if offset_index % 2 == 0 else -1)
 
 
-def routes(partners):
+def plan(partners, pairs):
     found = {}
     for sender in range(2):
         for offset_index in range(partners):
             to = sender + partner_offset(offset_index)
             found.setdefault(to // 2, []).append((sender, offset_index, to % 2))
-    far = sorted((hop for hop in found if hop > 0)) + sorted((hop for hop in found if hop < 0), reverse=True)
-    return [(hop, found[hop]) for hop in [0] + far]
+    local = found.pop(0)
+    reach = max(found)
+    if reach == 2 and pairs % 4 == 0:
+        order = ((2, (1, 0, 1, 1)), (1, (0, 1, 0, 1)), (2, (0, 1, 0, 0)), (1, (1, 0, 1, 0)))
+    else:
+        order = [(hop, (forward,)) for forward in (1, 0) for hop in range(1, reach + 1)]
+    return local, [(hop, forward, found[-hop], found[hop]) for hop, forward in order]
+
+
+def hop_of(hop, forward, pair):
+    return hop if forward[pair % len(forward)] else -hop
+
+
+def by_pair(table):
+    if len(set(table)) == 1:
+        return table[0]
+    pair = lax.rem(lax.axis_index("rows") // 2, len(table))
+    value = table[0]
+    for i in range(1, len(table)):
+        value = jnp.where(pair == i, table[i], value)
+    return value
+
+
+def sent_forward(step):
+    return by_pair(step[1])
+
+
+def came_forward(step):
+    hop, forward = step[:2]
+    count = len(forward)
+    table = [0] * count
+    for pair in range(count):
+        table[(pair + hop_of(hop, forward, pair)) % count] = forward[pair]
+    return by_pair(table)
+
+
+def blend(backward, forward, is_forward):
+    return backward if backward == forward else backward + is_forward * (forward - backward)
+
+
+def block(index, length):
+    if isinstance(index, int):
+        return slice(index * length, (index + 1) * length)
+    return pl.ds(pl.multiple_of(index * length, 16), length)
+
+
+def role_slot(role):
+    return side() if role == 0 else 1 - side()
 
 
 def side():
@@ -150,39 +196,43 @@
     out[...] = dot(onehot[...], far[...]).astype(BF16)
 
 
-def deal(route, sender, rows, outs):
-    for (_, group), out in zip(route, outs):
-        length = out.shape[0] // len(group)
-        for i, (source, offset_index, _) in enumerate(group):
-            if source == sender:
-                out[i * length : (i + 1) * length, :] = rows[offset_index * length : (offset_index + 1) * length]
-
-
-def collect(route, receiver, arrived):
-    found = {}
-    for (_, group), piece in zip(route, arrived):
-        length = piece.shape[0] // len(group)
-        for i, (_, offset_index, target) in enumerate(group):
-            if target == receiver:
-                found[offset_index] = terms(piece[i * length : (i + 1) * length, :])
-    return jnp.concatenate([found[i] for i in range(len(found))], axis=0)
-
-
-def first_kernel(route, mine, other, rows_mine, rows_other, *refs):
-    outs = refs[: len(route)]
-    onehots = refs[len(route) :]
-    fill_onehot(rows_mine, onehots[0])
-    fill_onehot(rows_other, onehots[1])
-    picked = [pick_rows(onehot[...], state[...]) for onehot, state in zip(onehots, (mine, other))]
-
-    def body(place):
-        for role in range(2):
-            deal(route, role ^ place, picked[role], outs)
-
-    on_each_side(body)
-
-
-def own_kernel(route, has_source, first, *refs):
+def deal(steps, lists, outs):
+    local, far = steps
+    length = outs[0].shape[0] // len(local)
+    for i, (sender, index, _) in enumerate(local):
+        outs[0][block(i, length), :] = lists[sender, block(index, length), :]
+    for step, out in zip(far, outs[1:]):
+        is_forward = sent_forward(step)
+        for i, (backward, forward) in enumerate(zip(*step[2:])):
+            sender = blend(backward[0], forward[0], is_forward)
+            index = blend(backward[1], forward[1], is_forward)
+            out[block(i, length), :] = lists[sender, block(index, length), :]
+
+
+def collect(steps, arrived, halo):
+    local, far = steps
+    length = arrived[0].shape[0] // len(local)
+    for i, (_, index, receiver) in enumerate(local):
+        halo[receiver, block(index, length), :] = terms(arrived[0][block(i, length), :])
+    for step, piece in zip(far, arrived[1:]):
+        is_forward = came_forward(step)
+        for i, (backward, forward) in enumerate(zip(*step[2:])):
+            receiver = blend(backward[2], forward[2], is_forward)
+            index = blend(backward[1], forward[1], is_forward)
+            halo[receiver, block(index, length), :] = terms(piece[block(i, length), :])
+
+
+def first_kernel(steps, mine, other, rows_mine, rows_other, *refs):
+    *outs, onehot_mine, onehot_other, lists = refs
+    for role, (rows, onehot, state) in enumerate(
+        ((rows_mine, onehot_mine, mine), (rows_other, onehot_other, other))
+    ):
+        fill_onehot(rows, onehot)
+        lists[role_slot(role)] = pick_rows(onehot[...], state[...])
+    deal(steps, lists, outs)
+
+
+def own_kernel(steps, has_source, first, last, *refs):
     refs = list(refs)
 
     def take(count):
@@ -194,50 +244,41 @@
     sources = take(2) if has_source else None
     states = take(2)
     if not first:
-        fars, arrived = take(2), take(len(route))
-    bases, picks = take(2), take(2)
-
-    def body(place):
-        now = [state[...] for state in states]
-        if not first:
-            halos = [collect(route, role ^ place, arrived) for role in range(2)]
-            now = [now[role] + product(fars[role][...], halos[role]) for role in range(2)]
-        total = [now[role] + product(owns[role][...], terms(now[role])) for role in range(2)]
-        if has_source:
-            total = [total[role] + sources[role][...] for role in range(2)]
-        for role in range(2):
-            bases[role][...] = total[role]
+        fars, arrived = take(2), take(1 + len(steps[1]))
+    bases = take(2)
+    picks = None if last else take(2)
+    now = [state[...] for state in states]
+    if not first:
+        (halo,) = refs
+        collect(steps, arrived, halo)
+        now = [now[role] + product(fars[role][...], halo[role_slot(role)]) for role in range(2)]
+    total = [now[role] + product(owns[role][...], terms(now[role])) for role in range(2)]
+    if has_source:
+        total = [total[role] + sources[role][...] for role in range(2)]
+    for role in range(2):
+        bases[role][...] = total[role]
+        if not last:
             got = dot(onehots[role][...], terms(total[role]))
             half = got.shape[1] // 2
             picks[role][...] = got[:, :half] + got[:, half:]
 
-    if first:
-        body(0)
-    else:
-        on_each_side(body)
-
-
-def payload_kernel(route, *refs):
-    count = len(route)
+
+def payload_kernel(steps, *refs):
+    count = 1 + len(steps[1])
     picks, outs_of = refs[:2], refs[2:4]
-    arrived, outs = refs[4 : 4 + count], refs[4 + count :]
-
-    def body(place):
-        halos = [collect(route, role ^ place, arrived) for role in range(2)]
-        rows = [picks[role][...] + product(outs_of[role][...], halos[role]) for role in range(2)]
-        for role in range(2):
-            deal(route, role ^ place, rows[role], outs)
-
-    on_each_side(body)
-
-
-def give_back_kernel(route, base, far, *refs):
-    arrived, out = refs[: len(route)], refs[len(route)]
-
-    def body(place):
-        out[...] = base[...] + product(far[...], collect(route, 1 - place, arrived))
-
-    on_each_side(body)
+    arrived, outs = refs[4 : 4 + count], refs[4 + count : 4 + 2 * count]
+    halo, lists = refs[4 + 2 * count :]
+    collect(steps, arrived, halo)
+    rows = [picks[role][...] + product(outs_of[role][...], halo[role_slot(role)]) for role in range(2)]
+    for role in range(2):
+        lists[role_slot(role)] = rows[role]
+    deal(steps, lists, outs)
+
+
+def give_back_kernel(steps, base, far, *refs):
+    *arrived, out, halo = refs
+    collect(steps, arrived, halo)
+    out[...] = base[...] + product(far[...], halo[role_slot(1)])
 
 
 def store_half(half, out, place, done):
@@ -247,14 +288,11 @@
     copy.wait()
 
 
-def keep_kernel(route, base, far, *refs):
-    arrived, (out, half, done) = refs[: len(route)], refs[len(route) :]
-
-    def body(place):
-        half[...] = base[...] + product(far[...], collect(route, place, arrived))
-        store_half(half, out, place, done)
-
-    on_each_side(body)
+def keep_kernel(steps, base, far, *refs):
+    *arrived, out, half, done, halo = refs
+    collect(steps, arrived, halo)
+    half[...] = base[...] + product(far[...], halo[role_slot(0)])
+    on_each_side(lambda place: store_half(half, out, place, done))
 
 
 def join_kernel(got, begun, out, done):
@@ -271,10 +309,13 @@
     partners, length = send_rows.shape
     halo_rows = partners * length
     columns = blocks + halo_rows // size
-    route = routes(partners)
+    local, far = steps = plan(partners, devices // 2)
+    count = 1 + len(far)
     state_half = ((local_rows, half), F32)
     list_half = ((halo_rows, half), F32)
-    pieces_out = [((len(group) * length, half), F32) for _, group in route]
+    pieces_out = [((len(lists) * length, half), F32) for lists in (local, *(step[2] for step in far))]
+    halo_scratch = pltpu.VMEM((2, halo_rows, panels), BF16)
+    lists_scratch = pltpu.VMEM((2, halo_rows, half), F32)
 
     def halves(x):
         return call(halves_kernel, [state_half] * 2, [VMEM], (x,))
@@ -292,8 +333,8 @@
 
     def exchange(pieces):
         arrived = [pieces[0]]
-        for (hop, _), piece in zip(route[1:], pieces[1:]):
-            pairs = [(d, (d + 2 * hop) % devices) for d in range(devices)]
+        for (hop, forward, _, _), piece in zip(far, pieces[1:]):
+            pairs = [(d, (d + 2 * hop_of(hop, forward, d // 2)) % devices) for d in range(devices)]
             arrived.append(lax.ppermute(piece, "rows", pairs))
         return arrived
 
@@ -317,25 +358,28 @@
             )[0]
             merged_e_other = swap(merged_e)
             *pieces, onehot, onehot_other = call(
-                functools.partial(first_kernel, route),
+                functools.partial(first_kernel, steps),
                 pieces_out + [((halo_rows, local_rows), BF16)] * 2,
                 [VMEM] * 4,
                 (state, state_other, send_rows, rows_other),
+                [lists_scratch],
             )
             states = (state, state_other)
+            later_tiles, later_cols = implicit_tiles, implicit_cols
         else:
             pieces = call(
-                functools.partial(payload_kernel, route),
+                functools.partial(payload_kernel, steps),
                 pieces_out,
-                [VMEM] * (4 + len(route)),
+                [VMEM] * (4 + count),
                 (*picks, matrix[0][2], matrix[1][2], *arrived),
+                [halo_scratch, lists_scratch],
             )
         fresh = exchange(pieces)
         if number == 0:
             give_s = halves(source)
             sources = (give_s[0], swap(give_s[1]))
             matrix_e = (split(merged_e, onehot), split(merged_e_other, onehot_other))
-            merged_i = merge(implicit_tiles, implicit_cols)
+            merged_i = merge(later_tiles, later_cols)
             merged_i_other = swap(merged_i)
         if number == 1:
             matrix_i = (split(merged_i, onehot), split(merged_i_other, onehot_other))
@@ -349,10 +393,11 @@
         if number:
             args += (last_matrix[0][1], last_matrix[1][1], *arrived)
         out = call(
-            functools.partial(own_kernel, route, has_source, number == 0),
-            [state_half] * 2 + [list_half] * 2,
+            functools.partial(own_kernel, steps, has_source, number == 0, number == applies - 1),
+            [state_half] * 2 + [list_half] * (2 if number < applies - 1 else 0),
             [VMEM] * len(args),
             args,
+            [halo_scratch] if number else [],
         )
         states, picks = out[:2], out[2:]
         arrived = fresh
@@ -361,18 +406,19 @@
     done = pltpu.SemaphoreType.DMA
     got = swap(
         call(
-            functools.partial(give_back_kernel, route),
+            functools.partial(give_back_kernel, steps),
             [state_half],
-            [VMEM] * (2 + len(route)),
+            [VMEM] * (2 + count),
             (states[1], matrix[1][1], *arrived),
+            [halo_scratch],
         )[0]
     )
     begun = call(
-        functools.partial(keep_kernel, route),
+        functools.partial(keep_kernel, steps),
         whole,
-        [VMEM] * (2 + len(route)),
+        [VMEM] * (2 + count),
         (states[0], matrix[0][1], *arrived),
-        [pltpu.VMEM((local_rows, half), F32), done],
+        [pltpu.VMEM((local_rows, half), F32), done, halo_scratch],
         out_specs=[ANY],
     )
     return call(join_kernel, whole, [VMEM, ANY], (got, *begun), [done], out_specs=[ANY], aliases={1: 0})[0]

time: 95.8 us -> 89.7 us (0.936)
  starting transfers between devices: 65.5 us -> 58.9 us
    ppermute x24, starting transfers between devices: 63.6 us -> 57.1 us  [exchange(): arrived.append(lax.ppermute(piece, 'rows', pairs))]
  transfers between devices with their start and end apart: 30 -> 30, of which waited for: 6 -> 6; matrix products, arithmetic and copies ran while one was open for 0% -> 0% of each run, Pallas kernels for 16% -> 17%
where the time goes in v2:
time: 89.7 us; the launch traced here: 89.6 us
  starting transfers between devices  58.9 us (66%)
  Pallas kernels  21.5 us (24%)
  waiting for transfers between devices  8.65 us (10%)
    ppermute x24, starting transfers between devices, exchange(): arrived.append(lax.ppermute(piece, 'rows', pairs))  57.1 us
    pallas_call x23, Pallas kernels, call(): pl.pallas_call(kernel, out_shape=[jax.ShapeDtypeStruct(shape, dtype) for...  21.5 us
    ppermute x6, waiting for transfers between devices, swap(): return lax.ppermute(x, 'rows', [(i, i ^ 1) for i in range(devices)])  5.15 us
    ppermute x24, waiting for transfers between devices, exchange(): arrived.append(lax.ppermute(piece, 'rows', pairs))  3.5 us
    ppermute x6, starting transfers between devices, swap(): return lax.ppermute(x, 'rows', [(i, i ^ 1) for i in range(devices)])  1.83 us
  transfers between devices with their start and end apart: 30, of which 6 were waited for; matrix products, arithmetic and copies ran while one was open for 0% of the time, Pallas kernels for 17%

profile of v2, /device:TPU:0, one launch (start us, length us, event | category | flops | bytes accessed | tf_op | source)
XLA Modules:
  0.0 89.6 jit_solution(5511865005056204428)
XLA Ops:
  0.0 3.0 %shard_map.78.total = f32[4,7,128,128]{3,2,1,0:T(8,128)} custom-call(s32[4,8]{1,0:T(4,128)} %columns_in.1, f32[4,8,128,128]{3,2,1,0:T(8,128)} %tiles_in.1), custom_call_target="tpu_custom_call" | custom-call | tf_op jit(solution)/shard_map/pallas_call | solution.py:22
  3.1 0.0 copy-start.2
  3.1 0.0 copy-start.3
  3.1 0.0 copy-start.4
  3.1 0.6 collective-permute-start.3
  3.7 0.9 %shard_map.75.total = f32[4,7,128,128]{3,2,1,0:T(8,128)S(1)} custom-call(s32[4,8]{1,0:T(4,128)S(1)} %copy-done.5, f32[4,8,128,128]{3,2,1,0:T(8,128)S(1)} %copy-done.1), custom_call_target="tpu_custom_call" | custom-call | tf_op jit(solution)/shard_map/pallas_call | solution.py:22
  4.6 0.1 collective-permute-start.2
  4.7 0.5 collective-permute-start
  5.3 0.1 collective-permute-start.4
  5.4 0.5 collective-permute-start.1
  5.9 4.8 %collective-permute-done.1.rows_other = s32[8,48]{1,0:T(8,128)S(1)} collective-permute-done((s32[8,48]{1,0:T(8,128)S(1)}, s32[8,48]{1,0:T(8,128)S(1)}, u32[]{:S(2)}, u32[]{:S(2)}) %collective-permute-start.1) | collective-permute-done | bytes 1568 | tf_op jit(solution)/shard_map/ppermute | solution.py:99
  10.7 0.7 shard_map.74
  11.4 6.9 %collective-permute-start.6 = (f32[192,128]{1,0:T(8,128)S(1)}, f32[192,128]{1,0:T(8,128)S(1)}, u32[]{:S(2)}, u32[]{:S(2)}) collective-permute-start(f32[192,128]{1,0:T(8,128)S(1)} %get-tuple-element.91), channel_id=1, source_target_pairs={{0,30},{1,31},{2,4},{3,5},{4,2},{5,3},{6,8},{7,9},{8,6},{9,7},{10,... | collective-permute-start | bytes 294920 | tf_op jit(solution)/shard_map/ppermute | solution.py:338
  18.3 0.0 collective-permute-start.8
  18.3 0.0 collective-permute-done.4.refs_5_
  18.3 0.0 collective-permute-start.5
  18.3 0.0 collective-permute-done.3.total
  18.3 4.7 %collective-permute-start.7 = (f32[144,128]{1,0:T(8,128)S(1)}, f32[144,128]{1,0:T(8,128)S(1)}, u32[]{:S(2)}, u32[]{:S(2)}) collective-permute-start(f32[144,128]{1,0:T(8,128)S(1)} %get-tuple-element.92), channel_id=1, source_target_pairs={{0,28},{1,29},{2,6},{3,7},{4,0},{5,1},{6,2},{7,3},{8,4},{9,5},{10,... | collective-permute-start | bytes 221192 | tf_op jit(solution)/shard_map/ppermute | solution.py:338
  23.0 0.8 shard_map.79
  23.8 0.8 shard_map.80
  24.6 1.0 %shard_map.82 = (f32[512,128]{1,0:T(8,128)S(1)}, f32[512,128]{1,0:T(8,128)S(1)}, f32[384,128]{1,0:T(8,128)S(1)}, f32[384,128]{1,0:T(8,128)S(1)}) custom-call(bf16[384,512]{1,0:T(8,128)(2,1)S(1)} %get-tuple-element.77.onehot.refs_0_, bf16[384,512]{1,0:T(8,128)(2,1)S(1)} %get-tuple-element.78.onehot.refs_1_, bf16[512,1024]{1,0:T(8,128)(2,1)S(1)} %get-tuple-element.81.refs_2_, ...), custom_call_target="tpu_custom_call" | custom-call | tf_op jit(solution)/shard_map/pallas_call | solution.py:22
  25.6 0.0 collective-permute-done.5.refs_9_.refs_5_
  25.6 0.0 collective-permute-done.8.refs_12_.refs_8_
  25.6 0.6 shard_map.84
  26.2 4.3 %collective-permute-start.10 = (f32[192,128]{1,0:T(8,128)S(1)}, f32[192,128]{1,0:T(8,128)S(1)}, u32[]{:S(2)}, u32[]{:S(2)}) collective-permute-start(f32[192,128]{1,0:T(8,128)S(1)} %get-tuple-element.104), channel_id=1, source_target_pairs={{0,30},{1,31},{2,4},{3,5},{4,2},{5,3},{6,8},{7,9},{8,6},{9,7},{10,... | collective-permute-start | bytes 294920 | tf_op jit(solution)/shard_map/ppermute | solution.py:338
  30.6 0.0 collective-permute-start.12
  30.6 0.0 collective-permute-start.9
  30.6 4.7 %collective-permute-start.11 = (f32[144,128]{1,0:T(8,128)S(1)}, f32[144,128]{1,0:T(8,128)S(1)}, u32[]{:S(2)}, u32[]{:S(2)}) collective-permute-start(f32[144,128]{1,0:T(8,128)S(1)} %get-tuple-element.105), channel_id=1, source_target_pairs={{0,28},{1,29},{2,6},{3,7},{4,0},{5,1},{6,2},{7,3},{8,4},{9,5},{10,... | collective-permute-start | bytes 221192 | tf_op jit(solution)/shard_map/ppermute | solution.py:338
  35.3 0.8 shard_map.76
  36.1 0.0 collective-permute-done.2.total
  36.1 0.8 shard_map.77
  36.9 1.5 %shard_map.83 = (f32[512,128]{1,0:T(8,128)S(1)}, f32[512,128]{1,0:T(8,128)S(1)}, f32[384,128]{1,0:T(8,128)S(1)}, f32[384,128]{1,0:T(8,128)S(1)}) custom-call(bf16[384,512]{1,0:T(8,128)(2,1)S(1)} %get-tuple-element.77.onehot.refs_0_, bf16[384,512]{1,0:T(8,128)(2,1)S(1)} %get-tuple-element.78.onehot.refs_1_, bf16[512,1024]{1,0:T(8,128)(2,1)S(1)} %get-tuple-element.79.refs_2_, ...), custom_call_target="tpu_custom_call" | custom-call | tf_op jit(solution)/shard_map/pallas_call | solution.py:22
  38.4 0.0 collective-permute-done.11.refs_13_.refs_7_
  38.4 0.0 collective-permute-done.10.refs_12_.refs_6_
  38.4 0.6 shard_map.86
  39.0 3.8 %collective-permute-start.14 = (f32[192,128]{1,0:T(8,128)S(1)}, f32[192,128]{1,0:T(8,128)S(1)}, u32[]{:S(2)}, u32[]{:S(2)}) collective-permute-start(f32[192,128]{1,0:T(8,128)S(1)} %get-tuple-element.115), channel_id=1, source_target_pairs={{0,30},{1,31},{2,4},{3,5},{4,2},{5,3},{6,8},{7,9},{8,6},{9,7},{10,... | collective-permute-start | bytes 294920 | tf_op jit(solution)/shard_map/ppermute | solution.py:338
  42.8 0.0 collective-permute-start.13
  42.8 4.7 %collective-permute-start.15 = (f32[144,128]{1,0:T(8,128)S(1)}, f32[144,128]{1,0:T(8,128)S(1)}, u32[]{:S(2)}, u32[]{:S(2)}) collective-permute-start(f32[144,128]{1,0:T(8,128)S(1)} %get-tuple-element.116), channel_id=1, source_target_pairs={{0,28},{1,29},{2,6},{3,7},{4,0},{5,1},{6,2},{7,3},{8,4},{9,5},{10,... | collective-permute-start | bytes 221192 | tf_op jit(solution)/shard_map/ppermute | solution.py:338
  47.6 1.5 %shard_map.85 = (f32[512,128]{1,0:T(8,128)S(1)}, f32[512,128]{1,0:T(8,128)S(1)}, f32[384,128]{1,0:T(8,128)S(1)}, f32[384,128]{1,0:T(8,128)S(1)}) custom-call(bf16[384,512]{1,0:T(8,128)(2,1)S(1)} %get-tuple-element.77.onehot.refs_0_, bf16[384,512]{1,0:T(8,128)(2,1)S(1)} %get-tuple-element.78.onehot.refs_1_, bf16[512,1024]{1,0:T(8,128)(2,1)S(1)} %get-tuple-element.81.refs_2_, ...), custom_call_target="tpu_custom_call" | custom-call | tf_op jit(solution)/shard_map/pallas_call | solution.py:22
  49.1 0.8 collective-permute-done.13.refs_9_.refs_5_
  49.9 0.6 shard_map.88
  50.5 4.6 %collective-permute-start.18 = (f32[192,128]{1,0:T(8,128)S(1)}, f32[192,128]{1,0:T(8,128)S(1)}, u32[]{:S(2)}, u32[]{:S(2)}) collective-permute-start(f32[192,128]{1,0:T(8,128)S(1)} %get-tuple-element.124), channel_id=1, source_target_pairs={{0,30},{1,31},{2,4},{3,5},{4,2},{5,3},{6,8},{7,9},{8,6},{9,7},{10,... | collective-permute-start | bytes 294920 | tf_op jit(solution)/shard_map/ppermute | solution.py:338
  55.1 4.7 %collective-permute-start.19 = (f32[144,128]{1,0:T(8,128)S(1)}, f32[144,128]{1,0:T(8,128)S(1)}, u32[]{:S(2)}, u32[]{:S(2)}) collective-permute-start(f32[144,128]{1,0:T(8,128)S(1)} %get-tuple-element.125), channel_id=1, source_target_pairs={{0,28},{1,29},{2,6},{3,7},{4,0},{5,1},{6,2},{7,3},{8,4},{9,5},{10,... | collective-permute-start | bytes 221192 | tf_op jit(solution)/shard_map/ppermute | solution.py:338
  59.8 1.5 %shard_map.87 = (f32[512,128]{1,0:T(8,128)S(1)}, f32[512,128]{1,0:T(8,128)S(1)}, f32[384,128]{1,0:T(8,128)S(1)}, f32[384,128]{1,0:T(8,128)S(1)}) custom-call(bf16[384,512]{1,0:T(8,128)(2,1)S(1)} %get-tuple-element.77.onehot.refs_0_, bf16[384,512]{1,0:T(8,128)(2,1)S(1)} %get-tuple-element.78.onehot.refs_1_, bf16[512,1024]{1,0:T(8,128)(2,1)S(1)} %get-tuple-element.79.refs_2_, ...), custom_call_target="tpu_custom_call" | custom-call | tf_op jit(solution)/shard_map/pallas_call | solution.py:22
  61.3 0.8 collective-permute-done.17.refs_11_.refs_5_
  62.1 0.0 collective-permute-done.19.refs_13_.refs_7_
  62.1 0.0 collective-permute-done.18.refs_12_.refs_6_
  62.1 0.6 shard_map.90
  62.8 4.6 %collective-permute-start.22 = (f32[192,128]{1,0:T(8,128)S(1)}, f32[192,128]{1,0:T(8,128)S(1)}, u32[]{:S(2)}, u32[]{:S(2)}) collective-permute-start(f32[192,128]{1,0:T(8,128)S(1)} %get-tuple-element.133), channel_id=1, source_target_pairs={{0,30},{1,31},{2,4},{3,5},{4,2},{5,3},{6,8},{7,9},{8,6},{9,7},{10,... | collective-permute-start | bytes 294920 | tf_op jit(solution)/shard_map/ppermute | solution.py:338
  67.3 4.7 %collective-permute-start.23 = (f32[144,128]{1,0:T(8,128)S(1)}, f32[144,128]{1,0:T(8,128)S(1)}, u32[]{:S(2)}, u32[]{:S(2)}) collective-permute-start(f32[144,128]{1,0:T(8,128)S(1)} %get-tuple-element.134), channel_id=1, source_target_pairs={{0,28},{1,29},{2,6},{3,7},{4,0},{5,1},{6,2},{7,3},{8,4},{9,5},{10,... | collective-permute-start | bytes 221192 | tf_op jit(solution)/shard_map/ppermute | solution.py:338
  72.1 1.5 %shard_map.89 = (f32[512,128]{1,0:T(8,128)S(1)}, f32[512,128]{1,0:T(8,128)S(1)}, f32[384,128]{1,0:T(8,128)S(1)}, f32[384,128]{1,0:T(8,128)S(1)}) custom-call(bf16[384,512]{1,0:T(8,128)(2,1)S(1)} %get-tuple-element.77.onehot.refs_0_, bf16[384,512]{1,0:T(8,128)(2,1)S(1)} %get-tuple-element.78.onehot.refs_1_, bf16[512,1024]{1,0:T(8,128)(2,1)S(1)} %get-tuple-element.81.refs_2_, ...), custom_call_target="tpu_custom_call" | custom-call | tf_op jit(solution)/shard_map/pallas_call | solution.py:22
  73.6 0.8 collective-permute-done.21.refs_9_.refs_5_
  74.4 0.0 collective-permute-done.23.refs_11_.refs_7_
  74.4 0.6 shard_map.92
  75.0 4.6 %collective-permute-start.26 = (f32[192,128]{1,0:T(8,128)S(1)}, f32[192,128]{1,0:T(8,128)S(1)}, u32[]{:S(2)}, u32[]{:S(2)}) collective-permute-start(f32[192,128]{1,0:T(8,128)S(1)} %get-tuple-element.141), channel_id=1, source_target_pairs={{0,30},{1,31},{2,4},{3,5},{4,2},{5,3},{6,8},{7,9},{8,6},{9,7},{10,... | collective-permute-start | bytes 294920 | tf_op jit(solution)/shard_map/ppermute | solution.py:338
  79.6 4.7 %collective-permute-start.27 = (f32[144,128]{1,0:T(8,128)S(1)}, f32[144,128]{1,0:T(8,128)S(1)}, u32[]{:S(2)}, u32[]{:S(2)}) collective-permute-start(f32[144,128]{1,0:T(8,128)S(1)} %get-tuple-element.142), channel_id=1, source_target_pairs={{0,28},{1,29},{2,6},{3,7},{4,0},{5,1},{6,2},{7,3},{8,4},{9,5},{10,... | collective-permute-start | bytes 221192 | tf_op jit(solution)/shard_map/ppermute | solution.py:338
  84.3 1.2 %shard_map.91 = (f32[512,128]{1,0:T(8,128)S(1)}, f32[512,128]{1,0:T(8,128)S(1)}) custom-call(bf16[384,512]{1,0:T(8,128)(2,1)S(1)} %get-tuple-element.77.onehot.refs_0_, bf16[384,512]{1,0:T(8,128)(2,1)S(1)} %get-tuple-element.78.onehot.refs_1_, bf16[512,1024]{1,0:T(8,128)(2,1)S(1)} %get-tuple-element.79.refs_2_, ...), custom_call_target="tpu_custom_call" | custom-call | tf_op jit(solution)/shard_map/pallas_call | solution.py:22
  85.6 1.1 %collective-permute-done.25.refs_1_ = f32[144,128]{1,0:T(8,128)S(1)} collective-permute-done((f32[144,128]{1,0:T(8,128)S(1)}, f32[144,128]{1,0:T(8,128)S(1)}, u32[]{:S(2)}, u32[]{:S(2)}) %collective-permute-start.25) | collective-permute-done | bytes 73760 | tf_op jit(solution)/shard_map/ppermute | solution.py:338
  86.6 0.0 collective-permute-done.27.refs_3_
  86.7 0.4 shard_map.93
  87.1 0.1 collective-permute-start.29
  87.2 1.1 %shard_map.94.begun = f32[512,256]{1,0:T(8,128)} custom-call(f32[512,128]{1,0:T(8,128)S(1)} %get-tuple-element.144.base, bf16[512,768]{1,0:T(8,128)(2,1)S(1)} %get-tuple-element.96.refs_8_.far, f32[96,128]{1,0:T(8,128)S(1)} %get-tuple-element.139.refs_0_, f32[144,128]{1,0:T(8,128)S(1)} %collective-permute-done.25.refs_1_, ...), custom_call_target="tpu_custom_call" | custom-call | tf_op jit(solution)/shard_map/pallas_call | solution.py:22
  88.3 0.4 collective-permute-done.29.got
  88.7 0.7 shard_map.95
  (31 shorter events, 0.1 us)
Async XLA Ops:
  0.0 3.7 %copy-start.5 = (s32[4,8]{1,0:T(4,128)S(1)}, s32[4,8]{1,0:T(4,128)}, u32[]{:S(2)}) copy-start(s32[4,8]{1,0:T(4,128)} %columns.1) | copy-start | bytes 388
  0.0 3.7 %copy-start.1 = (f32[4,8,128,128]{3,2,1,0:T(8,128)S(1)}, f32[4,8,128,128]{3,2,1,0:T(8,128)}, u32[]{:S(2)}) copy-start(f32[4,8,128,128]{3,2,1,0:T(8,128)} %tiles.1) | copy-start | bytes 6291460
  3.1 1.6 %copy-start.2 = (f32[512,256]{1,0:T(8,128)S(1)}, f32[512,256]{1,0:T(8,128)}, u32[]{:S(2)}) copy-start(f32[512,256]{1,0:T(8,128)} %x.2) | copy-start | bytes 1572868
  3.1 2.2 %copy-start.3 = (f32[512,256]{1,0:T(8,128)S(1)}, f32[512,256]{1,0:T(8,128)}, u32[]{:S(2)}) copy-start(f32[512,256]{1,0:T(8,128)} %x.3) | copy-start | bytes 1572868
  3.1 2.3 %copy-start.4 = (s32[8,48]{1,0:T(8,128)S(1)}, s32[8,48]{1,0:T(8,128)}, u32[]{:S(2)}) copy-start(s32[8,48]{1,0:T(8,128)} %rows_mine.1) | copy-start | bytes 4612
  3.1 19.9 %copy-start = (f32[4,7,128,128]{3,2,1,0:T(8,128)S(1)}, f32[4,7,128,128]{3,2,1,0:T(8,128)}, u32[]{:S(2)}) copy-start(f32[4,7,128,128]{3,2,1,0:T(8,128)} %shard_map.78.total) | copy-start | bytes 5505028
  3.1 15.2 %collective-permute-start.3 = (f32[4,7,128,128]{3,2,1,0:T(8,128)}, f32[4,7,128,128]{3,2,1,0:T(8,128)S(1)}, u32[]{:S(2)}, u32[]{:S(2)}) collective-permute-start(f32[4,7,128,128]{3,2,1,0:T(8,128)} %shard_map.78.total), channel_id=1, source_target_pairs={{0,1},{1,0},{2,3},{3,2},{4,5},{5,4},{6,7},{7,6},{8,9},{9,8},{10,11... | collective-permute-start | bytes 5505032 | tf_op jit(solution)/shard_map/ppermute | solution.py:99
  4.6 31.5 %collective-permute-start.2 = (f32[4,7,128,128]{3,2,1,0:T(8,128)S(1)}, f32[4,7,128,128]{3,2,1,0:T(8,128)S(1)}, u32[]{:S(2)}, u32[]{:S(2)}) collective-permute-start(f32[4,7,128,128]{3,2,1,0:T(8,128)S(1)} %shard_map.75.total), channel_id=1, source_target_pairs={{0,1},{1,0},{2,3},{3,2},{4,5},{5,4},{6,7},{7,6},{8,9},{9,8},{10,11... | collective-permute-start | bytes 5505032 | tf_op jit(solution)/shard_map/ppermute | solution.py:99
  4.7 5.9 %collective-permute-start = (f32[512,128]{1,0:T(8,128)S(1)}, f32[512,128]{1,0:T(8,128)S(1)}, u32[]{:S(2)}, u32[]{:S(2)}) collective-permute-start(f32[512,128]{1,0:T(8,128)S(1)} %get-tuple-element.76), channel_id=1, source_target_pairs={{0,1},{1,0},{2,3},{3,2},{4,5},{5,4},{6,7},{7,6},{8,9},{9,8},{10,11... | collective-permute-start | bytes 786440 | tf_op jit(solution)/shard_map/ppermute | solution.py:99
  5.3 13.0 %collective-permute-start.4 = (f32[512,128]{1,0:T(8,128)S(1)}, f32[512,128]{1,0:T(8,128)S(1)}, u32[]{:S(2)}, u32[]{:S(2)}) collective-permute-start(f32[512,128]{1,0:T(8,128)S(1)} %get-tuple-element.84), channel_id=1, source_target_pairs={{0,1},{1,0},{2,3},{3,2},{4,5},{5,4},{6,7},{7,6},{8,9},{9,8},{10,11... | collective-permute-start | bytes 786440 | tf_op jit(solution)/shard_map/ppermute | solution.py:99
  5.4 5.2 %collective-permute-start.1 = (s32[8,48]{1,0:T(8,128)S(1)}, s32[8,48]{1,0:T(8,128)S(1)}, u32[]{:S(2)}, u32[]{:S(2)}) collective-permute-start(s32[8,48]{1,0:T(8,128)S(1)} %copy-done.4), channel_id=1, source_target_pairs={{0,1},{1,0},{2,3},{3,2},{4,5},{5,4},{6,7},{7,6},{8,9},{9,8},{10,11... | collective-permute-start | bytes 4616 | tf_op jit(solution)/shard_map/ppermute | solution.py:99
  11.4 14.2 %collective-permute-start.6 = (f32[192,128]{1,0:T(8,128)S(1)}, f32[192,128]{1,0:T(8,128)S(1)}, u32[]{:S(2)}, u32[]{:S(2)}) collective-permute-start(f32[192,128]{1,0:T(8,128)S(1)} %get-tuple-element.91), channel_id=1, source_target_pairs={{0,30},{1,31},{2,4},{3,5},{4,2},{5,3},{6,8},{7,9},{8,6},{9,7},{10,... | collective-permute-start | bytes 294920 | tf_op jit(solution)/shard_map/ppermute | solution.py:338
  18.3 7.3 %collective-permute-start.8 = (f32[192,128]{1,0:T(8,128)S(1)}, f32[192,128]{1,0:T(8,128)S(1)}, u32[]{:S(2)}, u32[]{:S(2)}) collective-permute-start(f32[192,128]{1,0:T(8,128)S(1)} %get-tuple-element.93), channel_id=1, source_target_pairs={{0,2},{1,3},{2,0},{3,1},{4,6},{5,7},{6,4},{7,5},{8,10},{9,11},{10,... | collective-permute-start | bytes 294920 | tf_op jit(solution)/shard_map/ppermute | solution.py:338
  18.3 7.3 %collective-permute-start.5 = (f32[144,128]{1,0:T(8,128)S(1)}, f32[144,128]{1,0:T(8,128)S(1)}, u32[]{:S(2)}, u32[]{:S(2)}) collective-permute-start(f32[144,128]{1,0:T(8,128)S(1)} %get-tuple-element.90), channel_id=1, source_target_pairs={{0,4},{1,5},{2,30},{3,31},{4,8},{5,9},{6,10},{7,11},{8,12},{9,13},... | collective-permute-start | bytes 221192 | tf_op jit(solution)/shard_map/ppermute | solution.py:338
  18.3 7.3 %collective-permute-start.7 = (f32[144,128]{1,0:T(8,128)S(1)}, f32[144,128]{1,0:T(8,128)S(1)}, u32[]{:S(2)}, u32[]{:S(2)}) collective-permute-start(f32[144,128]{1,0:T(8,128)S(1)} %get-tuple-element.92), channel_id=1, source_target_pairs={{0,28},{1,29},{2,6},{3,7},{4,0},{5,1},{6,2},{7,3},{8,4},{9,5},{10,... | collective-permute-start | bytes 221192 | tf_op jit(solution)/shard_map/ppermute | solution.py:338
  26.2 12.2 %collective-permute-start.10 = (f32[192,128]{1,0:T(8,128)S(1)}, f32[192,128]{1,0:T(8,128)S(1)}, u32[]{:S(2)}, u32[]{:S(2)}) collective-permute-start(f32[192,128]{1,0:T(8,128)S(1)} %get-tuple-element.104), channel_id=1, source_target_pairs={{0,30},{1,31},{2,4},{3,5},{4,2},{5,3},{6,8},{7,9},{8,6},{9,7},{10,... | collective-permute-start | bytes 294920 | tf_op jit(solution)/shard_map/ppermute | solution.py:338
  30.6 7.9 %collective-permute-start.12 = (f32[192,128]{1,0:T(8,128)S(1)}, f32[192,128]{1,0:T(8,128)S(1)}, u32[]{:S(2)}, u32[]{:S(2)}) collective-permute-start(f32[192,128]{1,0:T(8,128)S(1)} %get-tuple-element.106), channel_id=1, source_target_pairs={{0,2},{1,3},{2,0},{3,1},{4,6},{5,7},{6,4},{7,5},{8,10},{9,11},{10,... | collective-permute-start | bytes 294920 | tf_op jit(solution)/shard_map/ppermute | solution.py:338
  30.6 7.8 %collective-permute-start.9 = (f32[144,128]{1,0:T(8,128)S(1)}, f32[144,128]{1,0:T(8,128)S(1)}, u32[]{:S(2)}, u32[]{:S(2)}) collective-permute-start(f32[144,128]{1,0:T(8,128)S(1)} %get-tuple-element.103), channel_id=1, source_target_pairs={{0,4},{1,5},{2,30},{3,31},{4,8},{5,9},{6,10},{7,11},{8,12},{9,13},... | collective-permute-start | bytes 221192 | tf_op jit(solution)/shard_map/ppermute | solution.py:338
  30.6 7.8 %collective-permute-start.11 = (f32[144,128]{1,0:T(8,128)S(1)}, f32[144,128]{1,0:T(8,128)S(1)}, u32[]{:S(2)}, u32[]{:S(2)}) collective-permute-start(f32[144,128]{1,0:T(8,128)S(1)} %get-tuple-element.105), channel_id=1, source_target_pairs={{0,28},{1,29},{2,6},{3,7},{4,0},{5,1},{6,2},{7,3},{8,4},{9,5},{10,... | collective-permute-start | bytes 221192 | tf_op jit(solution)/shard_map/ppermute | solution.py:338
  39.0 10.8 %collective-permute-start.14 = (f32[192,128]{1,0:T(8,128)S(1)}, f32[192,128]{1,0:T(8,128)S(1)}, u32[]{:S(2)}, u32[]{:S(2)}) collective-permute-start(f32[192,128]{1,0:T(8,128)S(1)} %get-tuple-element.115), channel_id=1, source_target_pairs={{0,30},{1,31},{2,4},{3,5},{4,2},{5,3},{6,8},{7,9},{8,6},{9,7},{10,... | collective-permute-start | bytes 294920 | tf_op jit(solution)/shard_map/ppermute | solution.py:338
  42.8 7.1 %collective-permute-start.16 = (f32[192,128]{1,0:T(8,128)S(1)}, f32[192,128]{1,0:T(8,128)S(1)}, u32[]{:S(2)}, u32[]{:S(2)}) collective-permute-start(f32[192,128]{1,0:T(8,128)S(1)} %get-tuple-element.117), channel_id=1, source_target_pairs={{0,2},{1,3},{2,0},{3,1},{4,6},{5,7},{6,4},{7,5},{8,10},{9,11},{10,... | collective-permute-start | bytes 294920 | tf_op jit(solution)/shard_map/ppermute | solution.py:338
  42.8 7.0 %collective-permute-start.13 = (f32[144,128]{1,0:T(8,128)S(1)}, f32[144,128]{1,0:T(8,128)S(1)}, u32[]{:S(2)}, u32[]{:S(2)}) collective-permute-start(f32[144,128]{1,0:T(8,128)S(1)} %get-tuple-element.114), channel_id=1, source_target_pairs={{0,4},{1,5},{2,30},{3,31},{4,8},{5,9},{6,10},{7,11},{8,12},{9,13},... | collective-permute-start | bytes 221192 | tf_op jit(solution)/shard_map/ppermute | solution.py:338
  42.8 7.0 %collective-permute-start.15 = (f32[144,128]{1,0:T(8,128)S(1)}, f32[144,128]{1,0:T(8,128)S(1)}, u32[]{:S(2)}, u32[]{:S(2)}) collective-permute-start(f32[144,128]{1,0:T(8,128)S(1)} %get-tuple-element.116), channel_id=1, source_target_pairs={{0,28},{1,29},{2,6},{3,7},{4,0},{5,1},{6,2},{7,3},{8,4},{9,5},{10,... | collective-permute-start | bytes 221192 | tf_op jit(solution)/shard_map/ppermute | solution.py:338
  50.5 11.6 %collective-permute-start.18 = (f32[192,128]{1,0:T(8,128)S(1)}, f32[192,128]{1,0:T(8,128)S(1)}, u32[]{:S(2)}, u32[]{:S(2)}) collective-permute-start(f32[192,128]{1,0:T(8,128)S(1)} %get-tuple-element.124), channel_id=1, source_target_pairs={{0,30},{1,31},{2,4},{3,5},{4,2},{5,3},{6,8},{7,9},{8,6},{9,7},{10,... | collective-permute-start | bytes 294920 | tf_op jit(solution)/shard_map/ppermute | solution.py:338
  55.1 7.1 %collective-permute-start.20 = (f32[192,128]{1,0:T(8,128)S(1)}, f32[192,128]{1,0:T(8,128)S(1)}, u32[]{:S(2)}, u32[]{:S(2)}) collective-permute-start(f32[192,128]{1,0:T(8,128)S(1)} %get-tuple-element.126), channel_id=1, source_target_pairs={{0,2},{1,3},{2,0},{3,1},{4,6},{5,7},{6,4},{7,5},{8,10},{9,11},{10,... | collective-permute-start | bytes 294920 | tf_op jit(solution)/shard_map/ppermute | solution.py:338
  55.1 7.0 %collective-permute-start.17 = (f32[144,128]{1,0:T(8,128)S(1)}, f32[144,128]{1,0:T(8,128)S(1)}, u32[]{:S(2)}, u32[]{:S(2)}) collective-permute-start(f32[144,128]{1,0:T(8,128)S(1)} %get-tuple-element.123), channel_id=1, source_target_pairs={{0,4},{1,5},{2,30},{3,31},{4,8},{5,9},{6,10},{7,11},{8,12},{9,13},... | collective-permute-start | bytes 221192 | tf_op jit(solution)/shard_map/ppermute | solution.py:338
  55.1 7.0 %collective-permute-start.19 = (f32[144,128]{1,0:T(8,128)S(1)}, f32[144,128]{1,0:T(8,128)S(1)}, u32[]{:S(2)}, u32[]{:S(2)}) collective-permute-start(f32[144,128]{1,0:T(8,128)S(1)} %get-tuple-element.125), channel_id=1, source_target_pairs={{0,28},{1,29},{2,6},{3,7},{4,0},{5,1},{6,2},{7,3},{8,4},{9,5},{10,... | collective-permute-start | bytes 221192 | tf_op jit(solution)/shard_map/ppermute | solution.py:338
  62.8 11.6 %collective-permute-start.22 = (f32[192,128]{1,0:T(8,128)S(1)}, f32[192,128]{1,0:T(8,128)S(1)}, u32[]{:S(2)}, u32[]{:S(2)}) collective-permute-start(f32[192,128]{1,0:T(8,128)S(1)} %get-tuple-element.133), channel_id=1, source_target_pairs={{0,30},{1,31},{2,4},{3,5},{4,2},{5,3},{6,8},{7,9},{8,6},{9,7},{10,... | collective-permute-start | bytes 294920 | tf_op jit(solution)/shard_map/ppermute | solution.py:338
  67.3 7.1 %collective-permute-start.24 = (f32[192,128]{1,0:T(8,128)S(1)}, f32[192,128]{1,0:T(8,128)S(1)}, u32[]{:S(2)}, u32[]{:S(2)}) collective-permute-start(f32[192,128]{1,0:T(8,128)S(1)} %get-tuple-element.135), channel_id=1, source_target_pairs={{0,2},{1,3},{2,0},{3,1},{4,6},{5,7},{6,4},{7,5},{8,10},{9,11},{10,... | collective-permute-start | bytes 294920 | tf_op jit(solution)/shard_map/ppermute | solution.py:338
  67.3 7.0 %collective-permute-start.21 = (f32[144,128]{1,0:T(8,128)S(1)}, f32[144,128]{1,0:T(8,128)S(1)}, u32[]{:S(2)}, u32[]{:S(2)}) collective-permute-start(f32[144,128]{1,0:T(8,128)S(1)} %get-tuple-element.132), channel_id=1, source_target_pairs={{0,4},{1,5},{2,30},{3,31},{4,8},{5,9},{6,10},{7,11},{8,12},{9,13},... | collective-permute-start | bytes 221192 | tf_op jit(solution)/shard_map/ppermute | solution.py:338
  67.3 7.0 %collective-permute-start.23 = (f32[144,128]{1,0:T(8,128)S(1)}, f32[144,128]{1,0:T(8,128)S(1)}, u32[]{:S(2)}, u32[]{:S(2)}) collective-permute-start(f32[144,128]{1,0:T(8,128)S(1)} %get-tuple-element.134), channel_id=1, source_target_pairs={{0,28},{1,29},{2,6},{3,7},{4,0},{5,1},{6,2},{7,3},{8,4},{9,5},{10,... | collective-permute-start | bytes 221192 | tf_op jit(solution)/shard_map/ppermute | solution.py:338
  75.0 11.6 %collective-permute-start.26 = (f32[192,128]{1,0:T(8,128)S(1)}, f32[192,128]{1,0:T(8,128)S(1)}, u32[]{:S(2)}, u32[]{:S(2)}) collective-permute-start(f32[192,128]{1,0:T(8,128)S(1)} %get-tuple-element.141), channel_id=1, source_target_pairs={{0,30},{1,31},{2,4},{3,5},{4,2},{5,3},{6,8},{7,9},{8,6},{9,7},{10,... | collective-permute-start | bytes 294920 | tf_op jit(solution)/shard_map/ppermute | solution.py:338
  79.6 7.1 %collective-permute-start.28 = (f32[192,128]{1,0:T(8,128)S(1)}, f32[192,128]{1,0:T(8,128)S(1)}, u32[]{:S(2)}, u32[]{:S(2)}) collective-permute-start(f32[192,128]{1,0:T(8,128)S(1)} %get-tuple-element.143), channel_id=1, source_target_pairs={{0,2},{1,3},{2,0},{3,1},{4,6},{5,7},{6,4},{7,5},{8,10},{9,11},{10,... | collective-permute-start | bytes 294920 | tf_op jit(solution)/shard_map/ppermute | solution.py:338
  79.6 7.0 %collective-permute-start.25 = (f32[144,128]{1,0:T(8,128)S(1)}, f32[144,128]{1,0:T(8,128)S(1)}, u32[]{:S(2)}, u32[]{:S(2)}) collective-permute-start(f32[144,128]{1,0:T(8,128)S(1)} %get-tuple-element.140), channel_id=1, source_target_pairs={{0,4},{1,5},{2,30},{3,31},{4,8},{5,9},{6,10},{7,11},{8,12},{9,13},... | collective-permute-start | bytes 221192 | tf_op jit(solution)/shard_map/ppermute | solution.py:338
  79.6 7.0 %collective-permute-start.27 = (f32[144,128]{1,0:T(8,128)S(1)}, f32[144,128]{1,0:T(8,128)S(1)}, u32[]{:S(2)}, u32[]{:S(2)}) collective-permute-start(f32[144,128]{1,0:T(8,128)S(1)} %get-tuple-element.142), channel_id=1, source_target_pairs={{0,28},{1,29},{2,6},{3,7},{4,0},{5,1},{6,2},{7,3},{8,4},{9,5},{10,... | collective-permute-start | bytes 221192 | tf_op jit(solution)/shard_map/ppermute | solution.py:338
  87.1 1.6 %collective-permute-start.29 = (f32[512,128]{1,0:T(8,128)S(1)}, f32[512,128]{1,0:T(8,128)S(1)}, u32[]{:S(2)}, u32[]{:S(2)}) collective-permute-start(f32[512,128]{1,0:T(8,128)S(1)} %shard_map.93), channel_id=1, source_target_pairs={{0,1},{1,0},{2,3},{3,2},{4,5},{5,4},{6,7},{7,6},{8,9},{9,8},{10,11... | collective-permute-start | bytes 786440 | tf_op jit(solution)/shard_map/ppermute | solution.py:99

commit v3 on v2

--- a/solution.py
+++ b/solution.py
@@ -10,7 +10,7 @@
 
 STEPS = 3
 GRANT = 14 * 2**20
-WHOLE_GRANT = 121 * 2**19
+COST = 2 * 10**9
 
 VMEM = pl.BlockSpec(memory_space=pltpu.VMEM)
 SMEM = pl.BlockSpec(memory_space=pltpu.SMEM)
@@ -18,7 +18,7 @@
 F32, BF16 = jnp.float32, jnp.bfloat16
 
 
-def call(kernel, outs, in_specs, args, scratch=(), grant=GRANT, out_specs=None, aliases=None):
+def call(kernel, outs, in_specs, args, scratch=(), grant=GRANT, out_specs=None, aliases=None, cost=COST):
     return pl.pallas_call(
         kernel,
         out_shape=[jax.ShapeDtypeStruct(shape, dtype) for shape, dtype in outs],
@@ -26,6 +26,7 @@
         out_specs=out_specs or [VMEM] * len(outs),
         scratch_shapes=list(scratch),
         input_output_aliases=aliases or {},
+        cost_estimate=pl.CostEstimate(flops=cost, bytes_accessed=0, transcendentals=0),
         compiler_params=pltpu.CompilerParams(vmem_limit_bytes=grant),
     )(*args)
 
@@ -157,19 +158,6 @@
         give[...] = x[:, (1 - place) * half : (2 - place) * half]
 
     on_each_side(body)
-
-
-def fetch_merge_kernel(columns_in, tiles_in, total, columns, tiles, done):
-    blocks = tiles.shape[0]
-    fetch = [pltpu.make_async_copy(columns_in, columns, done.at[blocks])]
-    fetch += [pltpu.make_async_copy(tiles_in.at[i], tiles.at[i], done.at[i]) for i in range(blocks)]
-    for copy in fetch:
-        copy.start()
-    total[...] = jnp.zeros_like(total)
-    fetch[0].wait()
-    for block in range(blocks):
-        fetch[1 + block].wait()
-        add_blocks(columns, tiles, total, block)
 
 
 def add_blocks(columns, tiles, total, block):
@@ -305,7 +293,7 @@
     devices = lax.axis_size("rows")
     local_rows, panels = tracers_init.shape
     half = panels // 2
-    blocks, slots, size, _ = explicit_tiles.shape
+    blocks, _, size, _ = explicit_tiles.shape
     partners, length = send_rows.shape
     halo_rows = partners * length
     columns = blocks + halo_rows // size
@@ -344,18 +332,7 @@
             rows_other = swap(send_rows)
             state, give = halves(tracers_init)
             state_other = swap(give)
-            merged_e = call(
-                fetch_merge_kernel,
-                [((blocks, columns, size, size), F32)],
-                [ANY] * 2,
-                (explicit_cols, explicit_tiles),
-                [
-                    pltpu.SMEM((blocks, slots), jnp.int32),
-                    pltpu.VMEM((blocks, slots, size, size), F32),
-                    pltpu.SemaphoreType.DMA((blocks + 1,)),
-                ],
-                WHOLE_GRANT,
-            )[0]
+            merged_e = merge(explicit_tiles, explicit_cols)
             merged_e_other = swap(merged_e)
             *pieces, onehot, onehot_other = call(
                 functools.partial(first_kernel, steps),

time: 89.7 us -> 82.4 us (0.919)
  starting transfers between devices: 58.9 us -> 35 us
  waiting for transfers between devices: 8.65 us -> 24.9 us
  local copies, waits for them, and re-layouts: 0.03 us -> 2.4 us
  Pallas kernels: 21.5 us -> 19.4 us
    ppermute x24, starting transfers between devices: 57.1 us -> 32.9 us  [exchange(): arrived.append(lax.ppermute(piece, 'rows', pairs))]
    ppermute x24, waiting for transfers between devices: 3.5 us -> 20.8 us  [exchange(): arrived.append(lax.ppermute(piece, 'rows', pairs))]
    unnamed x12 -> x14, local copies, waits for them, and re-layouts: 0.03 us -> 2.4 us
    pallas_call x23, Pallas kernels: 21.5 us -> 19.4 us  [call(): pl.pallas_call(kernel, out_shape=[jax.ShapeDtypeStruct(shape, dtype) for...]
    ppermute x6, waiting for transfers between devices: 5.15 us -> 4.11 us  [swap(): return lax.ppermute(x, 'rows', [(i, i ^ 1) for i in range(devices)])]
  transfers between devices with their start and end apart: 30 -> 30, of which waited for: 6 -> 18; matrix products, arithmetic and copies ran while one was open for 0% -> 0% of each run, Pallas kernels for 17% -> 18%
where the time goes in v3:
time: 82.4 us; the launch traced here: 82.2 us
  starting transfers between devices  35 us (42%)
  waiting for transfers between devices  24.9 us (30%)
  Pallas kernels  19.4 us (24%)
  local copies, waits for them, and re-layouts  2.4 us (3%)
    ppermute x24, starting transfers between devices, exchange(): arrived.append(lax.ppermute(piece, 'rows', pairs))  32.9 us
    ppermute x24, waiting for transfers between devices, exchange(): arrived.append(lax.ppermute(piece, 'rows', pairs))  20.8 us
    pallas_call x23, Pallas kernels, call(): pl.pallas_call(kernel, out_shape=[jax.ShapeDtypeStruct(shape, dtype) for...  19.4 us
    ppermute x6, waiting for transfers between devices, swap(): return lax.ppermute(x, 'rows', [(i, i ^ 1) for i in range(devices)])  4.11 us
    unnamed x14, local copies, waits for them, and re-layouts  2.4 us
    ppermute x6, starting transfers between devices, swap(): return lax.ppermute(x, 'rows', [(i, i ^ 1) for i in range(devices)])  2.17 us
  transfers between devices with their start and end apart: 30, of which 18 were waited for; matrix products, arithmetic and copies ran while one was open for 0% of the time, Pallas kernels for 18%

profile of v3, /device:TPU:0, one launch (start us, length us, event | category | flops | bytes accessed | tf_op | source)
XLA Modules:
  0.0 82.2 jit_solution(4809552237332351958)
XLA Ops:
  0.0 1.6 %copy-done = f32[4,8,128,128]{3,2,1,0:T(8,128)S(1)} copy-done((f32[4,8,128,128]{3,2,1,0:T(8,128)S(1)}, f32[4,8,128,128]{3,2,1,0:T(8,128)}, u32[]{:S(2)}) %copy-start) | copy-done | bytes 2097176
  1.6 0.7 copy-done.5
  2.3 0.9 %shard_map.78.total = f32[4,7,128,128]{3,2,1,0:T(8,128)S(1)} custom-call(s32[4,8]{1,0:T(4,128)S(1)} %copy-done.5, f32[4,8,128,128]{3,2,1,0:T(8,128)S(1)} %copy-done), custom_call_target="tpu_custom_call" | custom-call | flops 2000000000 | tf_op jit(solution)/shard_map/pallas_call | solution.py:22
  3.2 0.6 collective-permute-start.3
  3.9 0.9 %shard_map.75.total = f32[4,7,128,128]{3,2,1,0:T(8,128)S(1)} custom-call(s32[4,8]{1,0:T(4,128)S(1)} %copy-done.6, f32[4,8,128,128]{3,2,1,0:T(8,128)S(1)} %copy-done.1), custom_call_target="tpu_custom_call" | custom-call | flops 2000000000 | tf_op jit(solution)/shard_map/pallas_call | solution.py:22
  4.8 0.6 collective-permute-start.2
  5.4 0.1 collective-permute-start
  5.5 0.5 collective-permute-start.1
  6.0 0.4 collective-permute-start.4
  6.4 3.7 %collective-permute-done.1.rows_other = s32[8,48]{1,0:T(8,128)S(1)} collective-permute-done((s32[8,48]{1,0:T(8,128)S(1)}, s32[8,48]{1,0:T(8,128)S(1)}, u32[]{:S(2)}, u32[]{:S(2)}) %collective-permute-start.1) | collective-permute-done | bytes 1568 | tf_op jit(solution)/shard_map/ppermute | solution.py:100
  10.2 0.7 shard_map.74
  10.9 0.8 shard_map.76
  11.7 0.8 shard_map.79
  12.5 2.9 %collective-permute-start.5 = (f32[144,128]{1,0:T(8,128)S(1)}, f32[144,128]{1,0:T(8,128)S(1)}, u32[]{:S(2)}, u32[]{:S(2)}) collective-permute-start(f32[144,128]{1,0:T(8,128)S(1)} %get-tuple-element.90), channel_id=1, source_target_pairs={{0,4},{1,5},{2,30},{3,31},{4,8},{5,9},{6,10},{7,11},{8,12},{9,13},... | collective-permute-start | bytes 221192 | tf_op jit(solution)/shard_map/ppermute | solution.py:326
  15.4 4.1 %collective-permute-start.6 = (f32[192,128]{1,0:T(8,128)S(1)}, f32[192,128]{1,0:T(8,128)S(1)}, u32[]{:S(2)}, u32[]{:S(2)}) collective-permute-start(f32[192,128]{1,0:T(8,128)S(1)} %get-tuple-element.91), channel_id=1, source_target_pairs={{0,30},{1,31},{2,4},{3,5},{4,2},{5,3},{6,8},{7,9},{8,6},{9,7},{10,... | collective-permute-start | bytes 294920 | tf_op jit(solution)/shard_map/ppermute | solution.py:326
  19.5 1.8 %collective-permute-start.7 = (f32[144,128]{1,0:T(8,128)S(1)}, f32[144,128]{1,0:T(8,128)S(1)}, u32[]{:S(2)}, u32[]{:S(2)}) collective-permute-start(f32[144,128]{1,0:T(8,128)S(1)} %get-tuple-element.92), channel_id=1, source_target_pairs={{0,28},{1,29},{2,6},{3,7},{4,0},{5,1},{6,2},{7,3},{8,4},{9,5},{10,... | collective-permute-start | bytes 221192 | tf_op jit(solution)/shard_map/ppermute | solution.py:326
  21.3 0.8 shard_map.80
  22.1 1.0 %shard_map.82 = (f32[512,128]{1,0:T(8,128)S(1)}, f32[512,128]{1,0:T(8,128)S(1)}, f32[384,128]{1,0:T(8,128)S(1)}, f32[384,128]{1,0:T(8,128)S(1)}) custom-call(bf16[384,512]{1,0:T(8,128)(2,1)S(1)} %get-tuple-element.77.onehot.refs_0_, bf16[384,512]{1,0:T(8,128)(2,1)S(1)} %get-tuple-element.78.onehot.refs_1_, bf16[512,1024]{1,0:T(8,128)(2,1)S(1)} %get-tuple-element.81.refs_2_, ...), custom_call_target="tpu_custom_call" | custom-call | flops 2000000000 | tf_op jit(solution)/shard_map/pallas_call | solution.py:22
  23.2 2.2 %collective-permute-done.7.refs_11_.refs_7_ = f32[144,128]{1,0:T(8,128)S(1)} collective-permute-done((f32[144,128]{1,0:T(8,128)S(1)}, f32[144,128]{1,0:T(8,128)S(1)}, u32[]{:S(2)}, u32[]{:S(2)}) %collective-permute-start.7) | collective-permute-done | bytes 73760 | tf_op jit(solution)/shard_map/ppermute | solution.py:326
  25.3 1.4 %collective-permute-done.8.refs_12_.refs_8_ = f32[192,128]{1,0:T(8,128)S(1)} collective-permute-done((f32[192,128]{1,0:T(8,128)S(1)}, f32[192,128]{1,0:T(8,128)S(1)}, u32[]{:S(2)}, u32[]{:S(2)}) %collective-permute-start.8) | collective-permute-done | bytes 98336 | tf_op jit(solution)/shard_map/ppermute | solution.py:326
  26.7 0.6 shard_map.84
  27.4 0.3 collective-permute-start.9
  27.7 3.9 %collective-permute-start.10 = (f32[192,128]{1,0:T(8,128)S(1)}, f32[192,128]{1,0:T(8,128)S(1)}, u32[]{:S(2)}, u32[]{:S(2)}) collective-permute-start(f32[192,128]{1,0:T(8,128)S(1)} %get-tuple-element.104), channel_id=1, source_target_pairs={{0,30},{1,31},{2,4},{3,5},{4,2},{5,3},{6,8},{7,9},{8,6},{9,7},{10,... | collective-permute-start | bytes 294920 | tf_op jit(solution)/shard_map/ppermute | solution.py:326
  31.6 0.6 collective-permute-start.11
  32.1 0.8 shard_map.77
  32.9 1.5 %shard_map.83 = (f32[512,128]{1,0:T(8,128)S(1)}, f32[512,128]{1,0:T(8,128)S(1)}, f32[384,128]{1,0:T(8,128)S(1)}, f32[384,128]{1,0:T(8,128)S(1)}) custom-call(bf16[384,512]{1,0:T(8,128)(2,1)S(1)} %get-tuple-element.77.onehot.refs_0_, bf16[384,512]{1,0:T(8,128)(2,1)S(1)} %get-tuple-element.78.onehot.refs_1_, bf16[512,1024]{1,0:T(8,128)(2,1)S(1)} %get-tuple-element.79.refs_2_, ...), custom_call_target="tpu_custom_call" | custom-call | flops 2000000000 | tf_op jit(solution)/shard_map/pallas_call | solution.py:22
  34.5 2.2 %collective-permute-done.11.refs_13_.refs_7_ = f32[144,128]{1,0:T(8,128)S(1)} collective-permute-done((f32[144,128]{1,0:T(8,128)S(1)}, f32[144,128]{1,0:T(8,128)S(1)}, u32[]{:S(2)}, u32[]{:S(2)}) %collective-permute-start.11) | collective-permute-done | bytes 73760 | tf_op jit(solution)/shard_map/ppermute | solution.py:326
  36.7 0.6 shard_map.86
  37.4 1.5 %collective-permute-start.13 = (f32[144,128]{1,0:T(8,128)S(1)}, f32[144,128]{1,0:T(8,128)S(1)}, u32[]{:S(2)}, u32[]{:S(2)}) collective-permute-start(f32[144,128]{1,0:T(8,128)S(1)} %get-tuple-element.114), channel_id=1, source_target_pairs={{0,4},{1,5},{2,30},{3,31},{4,8},{5,9},{6,10},{7,11},{8,12},{9,13},... | collective-permute-start | bytes 221192 | tf_op jit(solution)/shard_map/ppermute | solution.py:326
  38.9 2.7 %collective-permute-start.14 = (f32[192,128]{1,0:T(8,128)S(1)}, f32[192,128]{1,0:T(8,128)S(1)}, u32[]{:S(2)}, u32[]{:S(2)}) collective-permute-start(f32[192,128]{1,0:T(8,128)S(1)} %get-tuple-element.115), channel_id=1, source_target_pairs={{0,30},{1,31},{2,4},{3,5},{4,2},{5,3},{6,8},{7,9},{8,6},{9,7},{10,... | collective-permute-start | bytes 294920 | tf_op jit(solution)/shard_map/ppermute | solution.py:326
  41.6 0.6 collective-permute-start.15
  42.1 1.5 %shard_map.85 = (f32[512,128]{1,0:T(8,128)S(1)}, f32[512,128]{1,0:T(8,128)S(1)}, f32[384,128]{1,0:T(8,128)S(1)}, f32[384,128]{1,0:T(8,128)S(1)}) custom-call(bf16[384,512]{1,0:T(8,128)(2,1)S(1)} %get-tuple-element.77.onehot.refs_0_, bf16[384,512]{1,0:T(8,128)(2,1)S(1)} %get-tuple-element.78.onehot.refs_1_, bf16[512,1024]{1,0:T(8,128)(2,1)S(1)} %get-tuple-element.81.refs_2_, ...), custom_call_target="tpu_custom_call" | custom-call | flops 2000000000 | tf_op jit(solution)/shard_map/pallas_call | solution.py:22
  43.7 0.8 collective-permute-done.13.refs_9_.refs_5_
  44.5 1.5 %collective-permute-done.15.refs_11_.refs_7_ = f32[144,128]{1,0:T(8,128)S(1)} collective-permute-done((f32[144,128]{1,0:T(8,128)S(1)}, f32[144,128]{1,0:T(8,128)S(1)}, u32[]{:S(2)}, u32[]{:S(2)}) %collective-permute-start.15) | collective-permute-done | bytes 73760 | tf_op jit(solution)/shard_map/ppermute | solution.py:326
  45.9 1.2 %collective-permute-done.14.refs_10_.refs_6_ = f32[192,128]{1,0:T(8,128)S(1)} collective-permute-done((f32[192,128]{1,0:T(8,128)S(1)}, f32[192,128]{1,0:T(8,128)S(1)}, u32[]{:S(2)}, u32[]{:S(2)}) %collective-permute-start.14) | collective-permute-done | bytes 98336 | tf_op jit(solution)/shard_map/ppermute | solution.py:326
  47.1 0.6 shard_map.88
  47.7 1.6 %collective-permute-start.17 = (f32[144,128]{1,0:T(8,128)S(1)}, f32[144,128]{1,0:T(8,128)S(1)}, u32[]{:S(2)}, u32[]{:S(2)}) collective-permute-start(f32[144,128]{1,0:T(8,128)S(1)} %get-tuple-element.123), channel_id=1, source_target_pairs={{0,4},{1,5},{2,30},{3,31},{4,8},{5,9},{6,10},{7,11},{8,12},{9,13},... | collective-permute-start | bytes 221192 | tf_op jit(solution)/shard_map/ppermute | solution.py:326
  49.4 2.3 %collective-permute-start.18 = (f32[192,128]{1,0:T(8,128)S(1)}, f32[192,128]{1,0:T(8,128)S(1)}, u32[]{:S(2)}, u32[]{:S(2)}) collective-permute-start(f32[192,128]{1,0:T(8,128)S(1)} %get-tuple-element.124), channel_id=1, source_target_pairs={{0,30},{1,31},{2,4},{3,5},{4,2},{5,3},{6,8},{7,9},{8,6},{9,7},{10,... | collective-permute-start | bytes 294920 | tf_op jit(solution)/shard_map/ppermute | solution.py:326
  51.6 0.9 %collective-permute-start.19 = (f32[144,128]{1,0:T(8,128)S(1)}, f32[144,128]{1,0:T(8,128)S(1)}, u32[]{:S(2)}, u32[]{:S(2)}) collective-permute-start(f32[144,128]{1,0:T(8,128)S(1)} %get-tuple-element.125), channel_id=1, source_target_pairs={{0,28},{1,29},{2,6},{3,7},{4,0},{5,1},{6,2},{7,3},{8,4},{9,5},{10,... | collective-permute-start | bytes 221192 | tf_op jit(solution)/shard_map/ppermute | solution.py:326
  52.5 1.5 %shard_map.87 = (f32[512,128]{1,0:T(8,128)S(1)}, f32[512,128]{1,0:T(8,128)S(1)}, f32[384,128]{1,0:T(8,128)S(1)}, f32[384,128]{1,0:T(8,128)S(1)}) custom-call(bf16[384,512]{1,0:T(8,128)(2,1)S(1)} %get-tuple-element.77.onehot.refs_0_, bf16[384,512]{1,0:T(8,128)(2,1)S(1)} %get-tuple-element.78.onehot.refs_1_, bf16[512,1024]{1,0:T(8,128)(2,1)S(1)} %get-tuple-element.79.refs_2_, ...), custom_call_target="tpu_custom_call" | custom-call | flops 2000000000 | tf_op jit(solution)/shard_map/pallas_call | solution.py:22
  54.1 0.8 collective-permute-done.17.refs_11_.refs_5_
  54.8 1.1 %collective-permute-done.19.refs_13_.refs_7_ = f32[144,128]{1,0:T(8,128)S(1)} collective-permute-done((f32[144,128]{1,0:T(8,128)S(1)}, f32[144,128]{1,0:T(8,128)S(1)}, u32[]{:S(2)}, u32[]{:S(2)}) %collective-permute-start.19) | collective-permute-done | bytes 73760 | tf_op jit(solution)/shard_map/ppermute | solution.py:326
  56.0 1.7 %collective-permute-done.18.refs_12_.refs_6_ = f32[192,128]{1,0:T(8,128)S(1)} collective-permute-done((f32[192,128]{1,0:T(8,128)S(1)}, f32[192,128]{1,0:T(8,128)S(1)}, u32[]{:S(2)}, u32[]{:S(2)}) %collective-permute-start.18) | collective-permute-done | bytes 98336 | tf_op jit(solution)/shard_map/ppermute | solution.py:326
  57.7 0.6 shard_map.90
  58.3 1.6 %collective-permute-start.21 = (f32[144,128]{1,0:T(8,128)S(1)}, f32[144,128]{1,0:T(8,128)S(1)}, u32[]{:S(2)}, u32[]{:S(2)}) collective-permute-start(f32[144,128]{1,0:T(8,128)S(1)} %get-tuple-element.132), channel_id=1, source_target_pairs={{0,4},{1,5},{2,30},{3,31},{4,8},{5,9},{6,10},{7,11},{8,12},{9,13},... | collective-permute-start | bytes 221192 | tf_op jit(solution)/shard_map/ppermute | solution.py:326
  59.8 2.4 %collective-permute-start.22 = (f32[192,128]{1,0:T(8,128)S(1)}, f32[192,128]{1,0:T(8,128)S(1)}, u32[]{:S(2)}, u32[]{:S(2)}) collective-permute-start(f32[192,128]{1,0:T(8,128)S(1)} %get-tuple-element.133), channel_id=1, source_target_pairs={{0,30},{1,31},{2,4},{3,5},{4,2},{5,3},{6,8},{7,9},{8,6},{9,7},{10,... | collective-permute-start | bytes 294920 | tf_op jit(solution)/shard_map/ppermute | solution.py:326
  62.3 0.8 collective-permute-start.23
  63.1 0.1 collective-permute-start.24
  63.2 1.5 %shard_map.89 = (f32[512,128]{1,0:T(8,128)S(1)}, f32[512,128]{1,0:T(8,128)S(1)}, f32[384,128]{1,0:T(8,128)S(1)}, f32[384,128]{1,0:T(8,128)S(1)}) custom-call(bf16[384,512]{1,0:T(8,128)(2,1)S(1)} %get-tuple-element.77.onehot.refs_0_, bf16[384,512]{1,0:T(8,128)(2,1)S(1)} %get-tuple-element.78.onehot.refs_1_, bf16[512,1024]{1,0:T(8,128)(2,1)S(1)} %get-tuple-element.81.refs_2_, ...), custom_call_target="tpu_custom_call" | custom-call | flops 2000000000 | tf_op jit(solution)/shard_map/pallas_call | solution.py:22
  64.7 0.7 collective-permute-done.21.refs_9_.refs_5_
  65.4 1.2 %collective-permute-done.23.refs_11_.refs_7_ = f32[144,128]{1,0:T(8,128)S(1)} collective-permute-done((f32[144,128]{1,0:T(8,128)S(1)}, f32[144,128]{1,0:T(8,128)S(1)}, u32[]{:S(2)}, u32[]{:S(2)}) %collective-permute-start.23) | collective-permute-done | bytes 73760 | tf_op jit(solution)/shard_map/ppermute | solution.py:326
  66.6 2.6 %collective-permute-done.22.refs_10_.refs_6_ = f32[192,128]{1,0:T(8,128)S(1)} collective-permute-done((f32[192,128]{1,0:T(8,128)S(1)}, f32[192,128]{1,0:T(8,128)S(1)}, u32[]{:S(2)}, u32[]{:S(2)}) %collective-permute-start.22) | collective-permute-done | bytes 98336 | tf_op jit(solution)/shard_map/ppermute | solution.py:326
  69.3 0.6 shard_map.92
  69.9 0.6 collective-permute-start.25
  70.5 3.0 %collective-permute-start.26 = (f32[192,128]{1,0:T(8,128)S(1)}, f32[192,128]{1,0:T(8,128)S(1)}, u32[]{:S(2)}, u32[]{:S(2)}) collective-permute-start(f32[192,128]{1,0:T(8,128)S(1)} %get-tuple-element.141), channel_id=1, source_target_pairs={{0,30},{1,31},{2,4},{3,5},{4,2},{5,3},{6,8},{7,9},{8,6},{9,7},{10,... | collective-permute-start | bytes 294920 | tf_op jit(solution)/shard_map/ppermute | solution.py:326
  73.4 1.2 %collective-permute-start.27 = (f32[144,128]{1,0:T(8,128)S(1)}, f32[144,128]{1,0:T(8,128)S(1)}, u32[]{:S(2)}, u32[]{:S(2)}) collective-permute-start(f32[144,128]{1,0:T(8,128)S(1)} %get-tuple-element.142), channel_id=1, source_target_pairs={{0,28},{1,29},{2,6},{3,7},{4,0},{5,1},{6,2},{7,3},{8,4},{9,5},{10,... | collective-permute-start | bytes 221192 | tf_op jit(solution)/shard_map/ppermute | solution.py:326
  74.7 1.3 %shard_map.91 = (f32[512,128]{1,0:T(8,128)S(1)}, f32[512,128]{1,0:T(8,128)S(1)}) custom-call(bf16[384,512]{1,0:T(8,128)(2,1)S(1)} %get-tuple-element.77.onehot.refs_0_, bf16[384,512]{1,0:T(8,128)(2,1)S(1)} %get-tuple-element.78.onehot.refs_1_, bf16[512,1024]{1,0:T(8,128)(2,1)S(1)} %get-tuple-element.79.refs_2_, ...), custom_call_target="tpu_custom_call" | custom-call | flops 2000000000 | tf_op jit(solution)/shard_map/pallas_call | solution.py:22
  75.9 1.1 %collective-permute-done.25.refs_1_ = f32[144,128]{1,0:T(8,128)S(1)} collective-permute-done((f32[144,128]{1,0:T(8,128)S(1)}, f32[144,128]{1,0:T(8,128)S(1)}, u32[]{:S(2)}, u32[]{:S(2)}) %collective-permute-start.25) | collective-permute-done | bytes 73760 | tf_op jit(solution)/shard_map/ppermute | solution.py:326
  77.0 1.9 %collective-permute-done.27.refs_3_ = f32[144,128]{1,0:T(8,128)S(1)} collective-permute-done((f32[144,128]{1,0:T(8,128)S(1)}, f32[144,128]{1,0:T(8,128)S(1)}, u32[]{:S(2)}, u32[]{:S(2)}) %collective-permute-start.27) | collective-permute-done | bytes 73760 | tf_op jit(solution)/shard_map/ppermute | solution.py:326
  78.8 0.4 collective-permute-done.28.refs_4_
  79.3 0.4 shard_map.93
  79.8 1.2 %shard_map.94.begun = f32[512,256]{1,0:T(8,128)} custom-call(f32[512,128]{1,0:T(8,128)S(1)} %get-tuple-element.144.base, bf16[512,768]{1,0:T(8,128)(2,1)S(1)} %get-tuple-element.96.refs_8_.far, f32[96,128]{1,0:T(8,128)S(1)} %get-tuple-element.139.refs_0_, f32[144,128]{1,0:T(8,128)S(1)} %collective-permute-done.25.refs_1_, ...), custom_call_target="tpu_custom_call" | custom-call | flops 2000000000 | tf_op jit(solution)/shard_map/pallas_call | solution.py:22
  80.9 0.4 collective-permute-done.29.got
  81.3 0.7 shard_map.95
  (33 shorter events, 0.5 us)
Async XLA Ops:
  0.0 1.6 %copy-start = (f32[4,8,128,128]{3,2,1,0:T(8,128)S(1)}, f32[4,8,128,128]{3,2,1,0:T(8,128)}, u32[]{:S(2)}) copy-start(f32[4,8,128,128]{3,2,1,0:T(8,128)} %tiles.3) | copy-start | bytes 6291460
  1.6 0.7 copy-start.5
  2.3 1.6 %copy-start.1 = (f32[4,8,128,128]{3,2,1,0:T(8,128)S(1)}, f32[4,8,128,128]{3,2,1,0:T(8,128)}, u32[]{:S(2)}) copy-start(f32[4,8,128,128]{3,2,1,0:T(8,128)} %tiles.2) | copy-start | bytes 6291460
  2.3 1.6 %copy-start.6 = (s32[4,8]{1,0:T(4,128)S(1)}, s32[4,8]{1,0:T(4,128)}, u32[]{:S(2)}) copy-start(s32[4,8]{1,0:T(4,128)} %columns.2) | copy-start | bytes 388
  3.2 2.2 %copy-start.2 = (f32[512,256]{1,0:T(8,128)S(1)}, f32[512,256]{1,0:T(8,128)}, u32[]{:S(2)}) copy-start(f32[512,256]{1,0:T(8,128)} %x.2) | copy-start | bytes 1572868
  3.2 16.3 %collective-permute-start.3 = (f32[4,7,128,128]{3,2,1,0:T(8,128)S(1)}, f32[4,7,128,128]{3,2,1,0:T(8,128)S(1)}, u32[]{:S(2)}, u32[]{:S(2)}) collective-permute-start(f32[4,7,128,128]{3,2,1,0:T(8,128)S(1)} %shard_map.78.total), channel_id=1, source_target_pairs={{0,1},{1,0},{2,3},{3,2},{4,5},{5,4},{6,7},{7,6},{8,9},{9,8},{10,11... | collective-permute-start | bytes 5505032 | tf_op jit(solution)/shard_map/ppermute | solution.py:100
  4.8 0.7 copy-start.4
  4.8 1.2 %copy-start.3 = (f32[512,256]{1,0:T(8,128)S(1)}, f32[512,256]{1,0:T(8,128)}, u32[]{:S(2)}) copy-start(f32[512,256]{1,0:T(8,128)} %x.3) | copy-start | bytes 1572868
  4.8 27.3 %collective-permute-start.2 = (f32[4,7,128,128]{3,2,1,0:T(8,128)S(1)}, f32[4,7,128,128]{3,2,1,0:T(8,128)S(1)}, u32[]{:S(2)}, u32[]{:S(2)}) collective-permute-start(f32[4,7,128,128]{3,2,1,0:T(8,128)S(1)} %shard_map.75.total), channel_id=1, source_target_pairs={{0,1},{1,0},{2,3},{3,2},{4,5},{5,4},{6,7},{7,6},{8,9},{9,8},{10,11... | collective-permute-start | bytes 5505032 | tf_op jit(solution)/shard_map/ppermute | solution.py:100
  5.4 4.8 %collective-permute-start = (f32[512,128]{1,0:T(8,128)S(1)}, f32[512,128]{1,0:T(8,128)S(1)}, u32[]{:S(2)}, u32[]{:S(2)}) collective-permute-start(f32[512,128]{1,0:T(8,128)S(1)} %get-tuple-element.76), channel_id=1, source_target_pairs={{0,1},{1,0},{2,3},{3,2},{4,5},{5,4},{6,7},{7,6},{8,9},{9,8},{10,11... | collective-permute-start | bytes 786440 | tf_op jit(solution)/shard_map/ppermute | solution.py:100
  5.5 4.7 %collective-permute-start.1 = (s32[8,48]{1,0:T(8,128)S(1)}, s32[8,48]{1,0:T(8,128)S(1)}, u32[]{:S(2)}, u32[]{:S(2)}) collective-permute-start(s32[8,48]{1,0:T(8,128)S(1)} %copy-done.4), channel_id=1, source_target_pairs={{0,1},{1,0},{2,3},{3,2},{4,5},{5,4},{6,7},{7,6},{8,9},{9,8},{10,11... | collective-permute-start | bytes 4616 | tf_op jit(solution)/shard_map/ppermute | solution.py:100
  6.0 16.0 %collective-permute-start.4 = (f32[512,128]{1,0:T(8,128)S(1)}, f32[512,128]{1,0:T(8,128)S(1)}, u32[]{:S(2)}, u32[]{:S(2)}) collective-permute-start(f32[512,128]{1,0:T(8,128)S(1)} %get-tuple-element.84), channel_id=1, source_target_pairs={{0,1},{1,0},{2,3},{3,2},{4,5},{5,4},{6,7},{7,6},{8,9},{9,8},{10,11... | collective-permute-start | bytes 786440 | tf_op jit(solution)/shard_map/ppermute | solution.py:100
  12.5 10.7 %collective-permute-start.5 = (f32[144,128]{1,0:T(8,128)S(1)}, f32[144,128]{1,0:T(8,128)S(1)}, u32[]{:S(2)}, u32[]{:S(2)}) collective-permute-start(f32[144,128]{1,0:T(8,128)S(1)} %get-tuple-element.90), channel_id=1, source_target_pairs={{0,4},{1,5},{2,30},{3,31},{4,8},{5,9},{6,10},{7,11},{8,12},{9,13},... | collective-permute-start | bytes 221192 | tf_op jit(solution)/shard_map/ppermute | solution.py:326
  15.4 10.0 %collective-permute-start.6 = (f32[192,128]{1,0:T(8,128)S(1)}, f32[192,128]{1,0:T(8,128)S(1)}, u32[]{:S(2)}, u32[]{:S(2)}) collective-permute-start(f32[192,128]{1,0:T(8,128)S(1)} %get-tuple-element.91), channel_id=1, source_target_pairs={{0,30},{1,31},{2,4},{3,5},{4,2},{5,3},{6,8},{7,9},{8,6},{9,7},{10,... | collective-permute-start | bytes 294920 | tf_op jit(solution)/shard_map/ppermute | solution.py:326
  19.5 5.8 %collective-permute-start.7 = (f32[144,128]{1,0:T(8,128)S(1)}, f32[144,128]{1,0:T(8,128)S(1)}, u32[]{:S(2)}, u32[]{:S(2)}) collective-permute-start(f32[144,128]{1,0:T(8,128)S(1)} %get-tuple-element.92), channel_id=1, source_target_pairs={{0,28},{1,29},{2,6},{3,7},{4,0},{5,1},{6,2},{7,3},{8,4},{9,5},{10,... | collective-permute-start | bytes 221192 | tf_op jit(solution)/shard_map/ppermute | solution.py:326
  22.1 4.7 %collective-permute-start.8 = (f32[192,128]{1,0:T(8,128)S(1)}, f32[192,128]{1,0:T(8,128)S(1)}, u32[]{:S(2)}, u32[]{:S(2)}) collective-permute-start(f32[192,128]{1,0:T(8,128)S(1)} %get-tuple-element.93), channel_id=1, source_target_pairs={{0,2},{1,3},{2,0},{3,1},{4,6},{5,7},{6,4},{7,5},{8,10},{9,11},{10,... | collective-permute-start | bytes 294920 | tf_op jit(solution)/shard_map/ppermute | solution.py:326
  27.4 7.1 %collective-permute-start.9 = (f32[144,128]{1,0:T(8,128)S(1)}, f32[144,128]{1,0:T(8,128)S(1)}, u32[]{:S(2)}, u32[]{:S(2)}) collective-permute-start(f32[144,128]{1,0:T(8,128)S(1)} %get-tuple-element.103), channel_id=1, source_target_pairs={{0,4},{1,5},{2,30},{3,31},{4,8},{5,9},{6,10},{7,11},{8,12},{9,13},... | collective-permute-start | bytes 221192 | tf_op jit(solution)/shard_map/ppermute | solution.py:326
  27.7 9.0 %collective-permute-start.10 = (f32[192,128]{1,0:T(8,128)S(1)}, f32[192,128]{1,0:T(8,128)S(1)}, u32[]{:S(2)}, u32[]{:S(2)}) collective-permute-start(f32[192,128]{1,0:T(8,128)S(1)} %get-tuple-element.104), channel_id=1, source_target_pairs={{0,30},{1,31},{2,4},{3,5},{4,2},{5,3},{6,8},{7,9},{8,6},{9,7},{10,... | collective-permute-start | bytes 294920 | tf_op jit(solution)/shard_map/ppermute | solution.py:326
  31.6 5.1 %collective-permute-start.11 = (f32[144,128]{1,0:T(8,128)S(1)}, f32[144,128]{1,0:T(8,128)S(1)}, u32[]{:S(2)}, u32[]{:S(2)}) collective-permute-start(f32[144,128]{1,0:T(8,128)S(1)} %get-tuple-element.105), channel_id=1, source_target_pairs={{0,28},{1,29},{2,6},{3,7},{4,0},{5,1},{6,2},{7,3},{8,4},{9,5},{10,... | collective-permute-start | bytes 221192 | tf_op jit(solution)/shard_map/ppermute | solution.py:326
  32.1 4.6 %collective-permute-start.12 = (f32[192,128]{1,0:T(8,128)S(1)}, f32[192,128]{1,0:T(8,128)S(1)}, u32[]{:S(2)}, u32[]{:S(2)}) collective-permute-start(f32[192,128]{1,0:T(8,128)S(1)} %get-tuple-element.106), channel_id=1, source_target_pairs={{0,2},{1,3},{2,0},{3,1},{4,6},{5,7},{6,4},{7,5},{8,10},{9,11},{10,... | collective-permute-start | bytes 294920 | tf_op jit(solution)/shard_map/ppermute | solution.py:326
  37.4 7.1 %collective-permute-start.13 = (f32[144,128]{1,0:T(8,128)S(1)}, f32[144,128]{1,0:T(8,128)S(1)}, u32[]{:S(2)}, u32[]{:S(2)}) collective-permute-start(f32[144,128]{1,0:T(8,128)S(1)} %get-tuple-element.114), channel_id=1, source_target_pairs={{0,4},{1,5},{2,30},{3,31},{4,8},{5,9},{6,10},{7,11},{8,12},{9,13},... | collective-permute-start | bytes 221192 | tf_op jit(solution)/shard_map/ppermute | solution.py:326
  38.9 8.3 %collective-permute-start.14 = (f32[192,128]{1,0:T(8,128)S(1)}, f32[192,128]{1,0:T(8,128)S(1)}, u32[]{:S(2)}, u32[]{:S(2)}) collective-permute-start(f32[192,128]{1,0:T(8,128)S(1)} %get-tuple-element.115), channel_id=1, source_target_pairs={{0,30},{1,31},{2,4},{3,5},{4,2},{5,3},{6,8},{7,9},{8,6},{9,7},{10,... | collective-permute-start | bytes 294920 | tf_op jit(solution)/shard_map/ppermute | solution.py:326
  41.6 4.4 %collective-permute-start.15 = (f32[144,128]{1,0:T(8,128)S(1)}, f32[144,128]{1,0:T(8,128)S(1)}, u32[]{:S(2)}, u32[]{:S(2)}) collective-permute-start(f32[144,128]{1,0:T(8,128)S(1)} %get-tuple-element.116), channel_id=1, source_target_pairs={{0,28},{1,29},{2,6},{3,7},{4,0},{5,1},{6,2},{7,3},{8,4},{9,5},{10,... | collective-permute-start | bytes 221192 | tf_op jit(solution)/shard_map/ppermute | solution.py:326
  42.1 5.0 %collective-permute-start.16 = (f32[192,128]{1,0:T(8,128)S(1)}, f32[192,128]{1,0:T(8,128)S(1)}, u32[]{:S(2)}, u32[]{:S(2)}) collective-permute-start(f32[192,128]{1,0:T(8,128)S(1)} %get-tuple-element.117), channel_id=1, source_target_pairs={{0,2},{1,3},{2,0},{3,1},{4,6},{5,7},{6,4},{7,5},{8,10},{9,11},{10,... | collective-permute-start | bytes 294920 | tf_op jit(solution)/shard_map/ppermute | solution.py:326
  47.7 7.1 %collective-permute-start.17 = (f32[144,128]{1,0:T(8,128)S(1)}, f32[144,128]{1,0:T(8,128)S(1)}, u32[]{:S(2)}, u32[]{:S(2)}) collective-permute-start(f32[144,128]{1,0:T(8,128)S(1)} %get-tuple-element.123), channel_id=1, source_target_pairs={{0,4},{1,5},{2,30},{3,31},{4,8},{5,9},{6,10},{7,11},{8,12},{9,13},... | collective-permute-start | bytes 221192 | tf_op jit(solution)/shard_map/ppermute | solution.py:326
  49.4 8.3 %collective-permute-start.18 = (f32[192,128]{1,0:T(8,128)S(1)}, f32[192,128]{1,0:T(8,128)S(1)}, u32[]{:S(2)}, u32[]{:S(2)}) collective-permute-start(f32[192,128]{1,0:T(8,128)S(1)} %get-tuple-element.124), channel_id=1, source_target_pairs={{0,30},{1,31},{2,4},{3,5},{4,2},{5,3},{6,8},{7,9},{8,6},{9,7},{10,... | collective-permute-start | bytes 294920 | tf_op jit(solution)/shard_map/ppermute | solution.py:326
  51.6 4.4 %collective-permute-start.19 = (f32[144,128]{1,0:T(8,128)S(1)}, f32[144,128]{1,0:T(8,128)S(1)}, u32[]{:S(2)}, u32[]{:S(2)}) collective-permute-start(f32[144,128]{1,0:T(8,128)S(1)} %get-tuple-element.125), channel_id=1, source_target_pairs={{0,28},{1,29},{2,6},{3,7},{4,0},{5,1},{6,2},{7,3},{8,4},{9,5},{10,... | collective-permute-start | bytes 221192 | tf_op jit(solution)/shard_map/ppermute | solution.py:326
  52.5 5.2 %collective-permute-start.20 = (f32[192,128]{1,0:T(8,128)S(1)}, f32[192,128]{1,0:T(8,128)S(1)}, u32[]{:S(2)}, u32[]{:S(2)}) collective-permute-start(f32[192,128]{1,0:T(8,128)S(1)} %get-tuple-element.126), channel_id=1, source_target_pairs={{0,2},{1,3},{2,0},{3,1},{4,6},{5,7},{6,4},{7,5},{8,10},{9,11},{10,... | collective-permute-start | bytes 294920 | tf_op jit(solution)/shard_map/ppermute | solution.py:326
  58.3 7.1 %collective-permute-start.21 = (f32[144,128]{1,0:T(8,128)S(1)}, f32[144,128]{1,0:T(8,128)S(1)}, u32[]{:S(2)}, u32[]{:S(2)}) collective-permute-start(f32[144,128]{1,0:T(8,128)S(1)} %get-tuple-element.132), channel_id=1, source_target_pairs={{0,4},{1,5},{2,30},{3,31},{4,8},{5,9},{6,10},{7,11},{8,12},{9,13},... | collective-permute-start | bytes 221192 | tf_op jit(solution)/shard_map/ppermute | solution.py:326
  59.8 9.4 %collective-permute-start.22 = (f32[192,128]{1,0:T(8,128)S(1)}, f32[192,128]{1,0:T(8,128)S(1)}, u32[]{:S(2)}, u32[]{:S(2)}) collective-permute-start(f32[192,128]{1,0:T(8,128)S(1)} %get-tuple-element.133), channel_id=1, source_target_pairs={{0,30},{1,31},{2,4},{3,5},{4,2},{5,3},{6,8},{7,9},{8,6},{9,7},{10,... | collective-permute-start | bytes 294920 | tf_op jit(solution)/shard_map/ppermute | solution.py:326
  62.3 4.4 %collective-permute-start.23 = (f32[144,128]{1,0:T(8,128)S(1)}, f32[144,128]{1,0:T(8,128)S(1)}, u32[]{:S(2)}, u32[]{:S(2)}) collective-permute-start(f32[144,128]{1,0:T(8,128)S(1)} %get-tuple-element.134), channel_id=1, source_target_pairs={{0,28},{1,29},{2,6},{3,7},{4,0},{5,1},{6,2},{7,3},{8,4},{9,5},{10,... | collective-permute-start | bytes 221192 | tf_op jit(solution)/shard_map/ppermute | solution.py:326
  63.1 6.2 %collective-permute-start.24 = (f32[192,128]{1,0:T(8,128)S(1)}, f32[192,128]{1,0:T(8,128)S(1)}, u32[]{:S(2)}, u32[]{:S(2)}) collective-permute-start(f32[192,128]{1,0:T(8,128)S(1)} %get-tuple-element.135), channel_id=1, source_target_pairs={{0,2},{1,3},{2,0},{3,1},{4,6},{5,7},{6,4},{7,5},{8,10},{9,11},{10,... | collective-permute-start | bytes 294920 | tf_op jit(solution)/shard_map/ppermute | solution.py:326
  69.9 7.1 %collective-permute-start.25 = (f32[144,128]{1,0:T(8,128)S(1)}, f32[144,128]{1,0:T(8,128)S(1)}, u32[]{:S(2)}, u32[]{:S(2)}) collective-permute-start(f32[144,128]{1,0:T(8,128)S(1)} %get-tuple-element.140), channel_id=1, source_target_pairs={{0,4},{1,5},{2,30},{3,31},{4,8},{5,9},{6,10},{7,11},{8,12},{9,13},... | collective-permute-start | bytes 221192 | tf_op jit(solution)/shard_map/ppermute | solution.py:326
  70.5 8.4 %collective-permute-start.26 = (f32[192,128]{1,0:T(8,128)S(1)}, f32[192,128]{1,0:T(8,128)S(1)}, u32[]{:S(2)}, u32[]{:S(2)}) collective-permute-start(f32[192,128]{1,0:T(8,128)S(1)} %get-tuple-element.141), channel_id=1, source_target_pairs={{0,30},{1,31},{2,4},{3,5},{4,2},{5,3},{6,8},{7,9},{8,6},{9,7},{10,... | collective-permute-start | bytes 294920 | tf_op jit(solution)/shard_map/ppermute | solution.py:326
  73.4 5.4 %collective-permute-start.27 = (f32[144,128]{1,0:T(8,128)S(1)}, f32[144,128]{1,0:T(8,128)S(1)}, u32[]{:S(2)}, u32[]{:S(2)}) collective-permute-start(f32[144,128]{1,0:T(8,128)S(1)} %get-tuple-element.142), channel_id=1, source_target_pairs={{0,28},{1,29},{2,6},{3,7},{4,0},{5,1},{6,2},{7,3},{8,4},{9,5},{10,... | collective-permute-start | bytes 221192 | tf_op jit(solution)/shard_map/ppermute | solution.py:326
  74.6 4.6 %collective-permute-start.28 = (f32[192,128]{1,0:T(8,128)S(1)}, f32[192,128]{1,0:T(8,128)S(1)}, u32[]{:S(2)}, u32[]{:S(2)}) collective-permute-start(f32[192,128]{1,0:T(8,128)S(1)} %get-tuple-element.143), channel_id=1, source_target_pairs={{0,2},{1,3},{2,0},{3,1},{4,6},{5,7},{6,4},{7,5},{8,10},{9,11},{10,... | collective-permute-start | bytes 294920 | tf_op jit(solution)/shard_map/ppermute | solution.py:326
  79.7 1.6 %collective-permute-start.29 = (f32[512,128]{1,0:T(8,128)S(1)}, f32[512,128]{1,0:T(8,128)S(1)}, u32[]{:S(2)}, u32[]{:S(2)}) collective-permute-start(f32[512,128]{1,0:T(8,128)S(1)} %shard_map.93), channel_id=1, source_target_pairs={{0,1},{1,0},{2,3},{3,2},{4,5},{5,4},{6,7},{7,6},{8,9},{9,8},{10,11... | collective-permute-start | bytes 786440 | tf_op jit(solution)/shard_map/ppermute | solution.py:100

commit v4 on v3

--- a/solution.py
+++ b/solution.py
@@ -10,7 +10,7 @@
 
 STEPS = 3
 GRANT = 14 * 2**20
-COST = 2 * 10**9
+COST = 10**9
 
 VMEM = pl.BlockSpec(memory_space=pltpu.VMEM)
 SMEM = pl.BlockSpec(memory_space=pltpu.SMEM)
@@ -305,8 +305,8 @@
     halo_scratch = pltpu.VMEM((2, halo_rows, panels), BF16)
     lists_scratch = pltpu.VMEM((2, halo_rows, half), F32)
 
-    def halves(x):
-        return call(halves_kernel, [state_half] * 2, [VMEM], (x,))
+    def halves(x, cost):
+        return call(halves_kernel, [state_half] * 2, [VMEM], (x,), cost=cost)
 
     def merge(tiles, cols):
         return call(merge_kernel, [((blocks, columns, size, size), F32)], [SMEM, VMEM], (cols, tiles))[0]
@@ -330,7 +330,7 @@
     for number in range(applies):
         if number == 0:
             rows_other = swap(send_rows)
-            state, give = halves(tracers_init)
+            state, give = halves(tracers_init, COST)
             state_other = swap(give)
             merged_e = merge(explicit_tiles, explicit_cols)
             merged_e_other = swap(merged_e)
@@ -353,7 +353,7 @@
             )
         fresh = exchange(pieces)
         if number == 0:
-            give_s = halves(source)
+            give_s = halves(source, COST // 100)
             sources = (give_s[0], swap(give_s[1]))
             matrix_e = (split(merged_e, onehot), split(merged_e_other, onehot_other))
             merged_i = merge(later_tiles, later_cols)

time: 82.4 us -> 85.4 us (1.036)
  starting transfers between devices: 35 us -> 50.5 us
  waiting for transfers between devices: 24.9 us -> 12.5 us
    ppermute x24, starting transfers between devices: 32.9 us -> 48.4 us  [exchange(): arrived.append(lax.ppermute(piece, 'rows', pairs))]
    ppermute x24, waiting for transfers between devices: 20.8 us -> 8.37 us  [exchange(): arrived.append(lax.ppermute(piece, 'rows', pairs))]
  transfers between devices with their start and end apart: 30 -> 30, of which waited for: 18 -> 9; matrix products, arithmetic and copies ran while one was open for 0% -> 0% of each run, Pallas kernels for 18% -> 17%
where the time goes in v4:
time: 85.4 us; the launch traced here: 85.2 us
  starting transfers between devices  50.5 us (59%)
  Pallas kernels  19.4 us (23%)
  waiting for transfers between devices  12.5 us (15%)
  local copies, waits for them, and re-layouts  2.4 us (3%)
    ppermute x24, starting transfers between devices, exchange(): arrived.append(lax.ppermute(piece, 'rows', pairs))  48.4 us
    pallas_call x23, Pallas kernels, call(): pl.pallas_call(kernel, out_shape=[jax.ShapeDtypeStruct(shape, dtype) for...  19.4 us
    ppermute x24, waiting for transfers between devices, exchange(): arrived.append(lax.ppermute(piece, 'rows', pairs))  8.37 us
    ppermute x6, waiting for transfers between devices, swap(): return lax.ppermute(x, 'rows', [(i, i ^ 1) for i in range(devices)])  4.11 us
    unnamed x14, local copies, waits for them, and re-layouts  2.4 us
    ppermute x6, starting transfers between devices, swap(): return lax.ppermute(x, 'rows', [(i, i ^ 1) for i in range(devices)])  2.17 us
  transfers between devices with their start and end apart: 30, of which 9 were waited for; matrix products, arithmetic and copies ran while one was open for 0% of the time, Pallas kernels for 17%

profile of v4, /device:TPU:0, one launch (start us, length us, event | category | flops | bytes accessed | tf_op | source)
XLA Modules:
  0.0 85.2 jit_solution(1795269470902033215)
XLA Ops:
  0.0 1.6 %copy-done = f32[4,8,128,128]{3,2,1,0:T(8,128)S(1)} copy-done((f32[4,8,128,128]{3,2,1,0:T(8,128)S(1)}, f32[4,8,128,128]{3,2,1,0:T(8,128)}, u32[]{:S(2)}) %copy-start) | copy-done | bytes 2097176
  1.6 0.7 copy-done.3
  2.3 0.9 %shard_map.78.total = f32[4,7,128,128]{3,2,1,0:T(8,128)S(1)} custom-call(s32[4,8]{1,0:T(4,128)S(1)} %copy-done.3, f32[4,8,128,128]{3,2,1,0:T(8,128)S(1)} %copy-done), custom_call_target="tpu_custom_call" | custom-call | flops 1000000000 | tf_op jit(solution)/shard_map/pallas_call | solution.py:22
  3.2 0.0 copy-start.5
  3.2 0.6 collective-permute-start.3
  3.8 0.1 copy-done.1
  3.9 0.9 %shard_map.75.total = f32[4,7,128,128]{3,2,1,0:T(8,128)S(1)} custom-call(s32[4,8]{1,0:T(4,128)S(1)} %copy-done.4, f32[4,8,128,128]{3,2,1,0:T(8,128)S(1)} %copy-done.1), custom_call_target="tpu_custom_call" | custom-call | flops 1000000000 | tf_op jit(solution)/shard_map/pallas_call | solution.py:22
  4.8 0.0 copy-start.6
  4.8 0.0 copy-start.2
  4.8 0.6 collective-permute-start.2
  5.4 0.1 collective-permute-start
  5.5 0.5 collective-permute-start.1
  6.0 0.4 collective-permute-start.4
  6.4 3.7 %collective-permute-done.1.rows_other = s32[8,48]{1,0:T(8,128)S(1)} collective-permute-done((s32[8,48]{1,0:T(8,128)S(1)}, s32[8,48]{1,0:T(8,128)S(1)}, u32[]{:S(2)}, u32[]{:S(2)}) %collective-permute-start.1) | collective-permute-done | bytes 1568 | tf_op jit(solution)/shard_map/ppermute | solution.py:100
  10.2 0.0 collective-permute-done.other.refs_7_
  10.2 0.7 shard_map.74
  10.9 2.9 %collective-permute-start.5 = (f32[144,128]{1,0:T(8,128)S(1)}, f32[144,128]{1,0:T(8,128)S(1)}, u32[]{:S(2)}, u32[]{:S(2)}) collective-permute-start(f32[144,128]{1,0:T(8,128)S(1)} %get-tuple-element.90), channel_id=1, source_target_pairs={{0,4},{1,5},{2,30},{3,31},{4,8},{5,9},{6,10},{7,11},{8,12},{9,13},... | collective-permute-start | bytes 221192 | tf_op jit(solution)/shard_map/ppermute | solution.py:326
  13.8 4.1 %collective-permute-start.6 = (f32[192,128]{1,0:T(8,128)S(1)}, f32[192,128]{1,0:T(8,128)S(1)}, u32[]{:S(2)}, u32[]{:S(2)}) collective-permute-start(f32[192,128]{1,0:T(8,128)S(1)} %get-tuple-element.91), channel_id=1, source_target_pairs={{0,30},{1,31},{2,4},{3,5},{4,2},{5,3},{6,8},{7,9},{8,6},{9,7},{10,... | collective-permute-start | bytes 294920 | tf_op jit(solution)/shard_map/ppermute | solution.py:326
  18.0 0.8 shard_map.76
  18.7 0.8 shard_map.79
  19.5 0.0 collective-permute-done.3.total
  19.5 0.5 collective-permute-start.8
  20.0 0.8 shard_map.80
  20.8 0.0 collective-permute-done.4.refs_5_
  20.8 1.7 %collective-permute-start.7 = (f32[144,128]{1,0:T(8,128)S(1)}, f32[144,128]{1,0:T(8,128)S(1)}, u32[]{:S(2)}, u32[]{:S(2)}) collective-permute-start(f32[144,128]{1,0:T(8,128)S(1)} %get-tuple-element.92), channel_id=1, source_target_pairs={{0,28},{1,29},{2,6},{3,7},{4,0},{5,1},{6,2},{7,3},{8,4},{9,5},{10,... | collective-permute-start | bytes 221192 | tf_op jit(solution)/shard_map/ppermute | solution.py:326
  22.5 1.0 %shard_map.82 = (f32[512,128]{1,0:T(8,128)S(1)}, f32[512,128]{1,0:T(8,128)S(1)}, f32[384,128]{1,0:T(8,128)S(1)}, f32[384,128]{1,0:T(8,128)S(1)}) custom-call(bf16[384,512]{1,0:T(8,128)(2,1)S(1)} %get-tuple-element.77.onehot.refs_0_, bf16[384,512]{1,0:T(8,128)(2,1)S(1)} %get-tuple-element.78.onehot.refs_1_, bf16[512,1024]{1,0:T(8,128)(2,1)S(1)} %get-tuple-element.81.refs_2_, ...), custom_call_target="tpu_custom_call" | custom-call | flops 1000000000 | tf_op jit(solution)/shard_map/pallas_call | solution.py:22
  23.5 1.7 %collective-permute-done.7.refs_11_.refs_7_ = f32[144,128]{1,0:T(8,128)S(1)} collective-permute-done((f32[144,128]{1,0:T(8,128)S(1)}, f32[144,128]{1,0:T(8,128)S(1)}, u32[]{:S(2)}, u32[]{:S(2)}) %collective-permute-start.7) | collective-permute-done | bytes 73760 | tf_op jit(solution)/shard_map/ppermute | solution.py:326
  25.2 0.0 collective-permute-done.6.refs_10_.refs_6_
  25.2 0.0 collective-permute-done.8.refs_12_.refs_8_
  25.2 0.6 shard_map.84
  25.8 2.4 %collective-permute-start.9 = (f32[144,128]{1,0:T(8,128)S(1)}, f32[144,128]{1,0:T(8,128)S(1)}, u32[]{:S(2)}, u32[]{:S(2)}) collective-permute-start(f32[144,128]{1,0:T(8,128)S(1)} %get-tuple-element.103), channel_id=1, source_target_pairs={{0,4},{1,5},{2,30},{3,31},{4,8},{5,9},{6,10},{7,11},{8,12},{9,13},... | collective-permute-start | bytes 221192 | tf_op jit(solution)/shard_map/ppermute | solution.py:326
  28.2 3.4 %collective-permute-start.10 = (f32[192,128]{1,0:T(8,128)S(1)}, f32[192,128]{1,0:T(8,128)S(1)}, u32[]{:S(2)}, u32[]{:S(2)}) collective-permute-start(f32[192,128]{1,0:T(8,128)S(1)} %get-tuple-element.104), channel_id=1, source_target_pairs={{0,30},{1,31},{2,4},{3,5},{4,2},{5,3},{6,8},{7,9},{8,6},{9,7},{10,... | collective-permute-start | bytes 294920 | tf_op jit(solution)/shard_map/ppermute | solution.py:326
  31.6 0.8 shard_map.77
  32.4 1.5 %shard_map.83 = (f32[512,128]{1,0:T(8,128)S(1)}, f32[512,128]{1,0:T(8,128)S(1)}, f32[384,128]{1,0:T(8,128)S(1)}, f32[384,128]{1,0:T(8,128)S(1)}) custom-call(bf16[384,512]{1,0:T(8,128)(2,1)S(1)} %get-tuple-element.77.onehot.refs_0_, bf16[384,512]{1,0:T(8,128)(2,1)S(1)} %get-tuple-element.78.onehot.refs_1_, bf16[512,1024]{1,0:T(8,128)(2,1)S(1)} %get-tuple-element.79.refs_2_, ...), custom_call_target="tpu_custom_call" | custom-call | flops 1000000000 | tf_op jit(solution)/shard_map/pallas_call | solution.py:22
  33.9 3.1 %collective-permute-done.11.refs_13_.refs_7_ = f32[144,128]{1,0:T(8,128)S(1)} collective-permute-done((f32[144,128]{1,0:T(8,128)S(1)}, f32[144,128]{1,0:T(8,128)S(1)}, u32[]{:S(2)}, u32[]{:S(2)}) %collective-permute-start.11) | collective-permute-done | bytes 73760 | tf_op jit(solution)/shard_map/ppermute | solution.py:326
  37.0 0.6 shard_map.86
  37.6 3.0 %collective-permute-start.14 = (f32[192,128]{1,0:T(8,128)S(1)}, f32[192,128]{1,0:T(8,128)S(1)}, u32[]{:S(2)}, u32[]{:S(2)}) collective-permute-start(f32[192,128]{1,0:T(8,128)S(1)} %get-tuple-element.115), channel_id=1, source_target_pairs={{0,30},{1,31},{2,4},{3,5},{4,2},{5,3},{6,8},{7,9},{8,6},{9,7},{10,... | collective-permute-start | bytes 294920 | tf_op jit(solution)/shard_map/ppermute | solution.py:326
  40.6 0.3 collective-permute-start.13
  40.9 4.4 %collective-permute-start.15 = (f32[144,128]{1,0:T(8,128)S(1)}, f32[144,128]{1,0:T(8,128)S(1)}, u32[]{:S(2)}, u32[]{:S(2)}) collective-permute-start(f32[144,128]{1,0:T(8,128)S(1)} %get-tuple-element.116), channel_id=1, source_target_pairs={{0,28},{1,29},{2,6},{3,7},{4,0},{5,1},{6,2},{7,3},{8,4},{9,5},{10,... | collective-permute-start | bytes 221192 | tf_op jit(solution)/shard_map/ppermute | solution.py:326
  45.3 1.5 %shard_map.85 = (f32[512,128]{1,0:T(8,128)S(1)}, f32[512,128]{1,0:T(8,128)S(1)}, f32[384,128]{1,0:T(8,128)S(1)}, f32[384,128]{1,0:T(8,128)S(1)}) custom-call(bf16[384,512]{1,0:T(8,128)(2,1)S(1)} %get-tuple-element.77.onehot.refs_0_, bf16[384,512]{1,0:T(8,128)(2,1)S(1)} %get-tuple-element.78.onehot.refs_1_, bf16[512,1024]{1,0:T(8,128)(2,1)S(1)} %get-tuple-element.81.refs_2_, ...), custom_call_target="tpu_custom_call" | custom-call | flops 1000000000 | tf_op jit(solution)/shard_map/pallas_call | solution.py:22
  46.9 0.8 collective-permute-done.13.refs_9_.refs_5_
  47.7 0.6 shard_map.88
  48.3 3.8 %collective-permute-start.18 = (f32[192,128]{1,0:T(8,128)S(1)}, f32[192,128]{1,0:T(8,128)S(1)}, u32[]{:S(2)}, u32[]{:S(2)}) collective-permute-start(f32[192,128]{1,0:T(8,128)S(1)} %get-tuple-element.124), channel_id=1, source_target_pairs={{0,30},{1,31},{2,4},{3,5},{4,2},{5,3},{6,8},{7,9},{8,6},{9,7},{10,... | collective-permute-start | bytes 294920 | tf_op jit(solution)/shard_map/ppermute | solution.py:326
  52.1 4.7 %collective-permute-start.19 = (f32[144,128]{1,0:T(8,128)S(1)}, f32[144,128]{1,0:T(8,128)S(1)}, u32[]{:S(2)}, u32[]{:S(2)}) collective-permute-start(f32[144,128]{1,0:T(8,128)S(1)} %get-tuple-element.125), channel_id=1, source_target_pairs={{0,28},{1,29},{2,6},{3,7},{4,0},{5,1},{6,2},{7,3},{8,4},{9,5},{10,... | collective-permute-start | bytes 221192 | tf_op jit(solution)/shard_map/ppermute | solution.py:326
  56.8 1.5 %shard_map.87 = (f32[512,128]{1,0:T(8,128)S(1)}, f32[512,128]{1,0:T(8,128)S(1)}, f32[384,128]{1,0:T(8,128)S(1)}, f32[384,128]{1,0:T(8,128)S(1)}) custom-call(bf16[384,512]{1,0:T(8,128)(2,1)S(1)} %get-tuple-element.77.onehot.refs_0_, bf16[384,512]{1,0:T(8,128)(2,1)S(1)} %get-tuple-element.78.onehot.refs_1_, bf16[512,1024]{1,0:T(8,128)(2,1)S(1)} %get-tuple-element.79.refs_2_, ...), custom_call_target="tpu_custom_call" | custom-call | flops 1000000000 | tf_op jit(solution)/shard_map/pallas_call | solution.py:22
  58.3 0.8 collective-permute-done.17.refs_11_.refs_5_
  59.2 0.6 shard_map.90
  59.8 3.5 %collective-permute-start.22 = (f32[192,128]{1,0:T(8,128)S(1)}, f32[192,128]{1,0:T(8,128)S(1)}, u32[]{:S(2)}, u32[]{:S(2)}) collective-permute-start(f32[192,128]{1,0:T(8,128)S(1)} %get-tuple-element.133), channel_id=1, source_target_pairs={{0,30},{1,31},{2,4},{3,5},{4,2},{5,3},{6,8},{7,9},{8,6},{9,7},{10,... | collective-permute-start | bytes 294920 | tf_op jit(solution)/shard_map/ppermute | solution.py:326
  63.3 0.5 collective-permute-start.21
  63.8 4.2 %collective-permute-start.23 = (f32[144,128]{1,0:T(8,128)S(1)}, f32[144,128]{1,0:T(8,128)S(1)}, u32[]{:S(2)}, u32[]{:S(2)}) collective-permute-start(f32[144,128]{1,0:T(8,128)S(1)} %get-tuple-element.134), channel_id=1, source_target_pairs={{0,28},{1,29},{2,6},{3,7},{4,0},{5,1},{6,2},{7,3},{8,4},{9,5},{10,... | collective-permute-start | bytes 221192 | tf_op jit(solution)/shard_map/ppermute | solution.py:326
  68.0 1.5 %shard_map.89 = (f32[512,128]{1,0:T(8,128)S(1)}, f32[512,128]{1,0:T(8,128)S(1)}, f32[384,128]{1,0:T(8,128)S(1)}, f32[384,128]{1,0:T(8,128)S(1)}) custom-call(bf16[384,512]{1,0:T(8,128)(2,1)S(1)} %get-tuple-element.77.onehot.refs_0_, bf16[384,512]{1,0:T(8,128)(2,1)S(1)} %get-tuple-element.78.onehot.refs_1_, bf16[512,1024]{1,0:T(8,128)(2,1)S(1)} %get-tuple-element.81.refs_2_, ...), custom_call_target="tpu_custom_call" | custom-call | flops 1000000000 | tf_op jit(solution)/shard_map/pallas_call | solution.py:22
  69.6 0.8 collective-permute-done.21.refs_9_.refs_5_
  70.4 0.1 collective-permute-done.23.refs_11_.refs_7_
  70.5 0.6 shard_map.92
  71.1 4.1 %collective-permute-start.26 = (f32[192,128]{1,0:T(8,128)S(1)}, f32[192,128]{1,0:T(8,128)S(1)}, u32[]{:S(2)}, u32[]{:S(2)}) collective-permute-start(f32[192,128]{1,0:T(8,128)S(1)} %get-tuple-element.141), channel_id=1, source_target_pairs={{0,30},{1,31},{2,4},{3,5},{4,2},{5,3},{6,8},{7,9},{8,6},{9,7},{10,... | collective-permute-start | bytes 294920 | tf_op jit(solution)/shard_map/ppermute | solution.py:326
  75.2 0.1 collective-permute-start.25
  75.3 4.6 %collective-permute-start.27 = (f32[144,128]{1,0:T(8,128)S(1)}, f32[144,128]{1,0:T(8,128)S(1)}, u32[]{:S(2)}, u32[]{:S(2)}) collective-permute-start(f32[144,128]{1,0:T(8,128)S(1)} %get-tuple-element.142), channel_id=1, source_target_pairs={{0,28},{1,29},{2,6},{3,7},{4,0},{5,1},{6,2},{7,3},{8,4},{9,5},{10,... | collective-permute-start | bytes 221192 | tf_op jit(solution)/shard_map/ppermute | solution.py:326
  79.9 1.2 %shard_map.91 = (f32[512,128]{1,0:T(8,128)S(1)}, f32[512,128]{1,0:T(8,128)S(1)}) custom-call(bf16[384,512]{1,0:T(8,128)(2,1)S(1)} %get-tuple-element.77.onehot.refs_0_, bf16[384,512]{1,0:T(8,128)(2,1)S(1)} %get-tuple-element.78.onehot.refs_1_, bf16[512,1024]{1,0:T(8,128)(2,1)S(1)} %get-tuple-element.79.refs_2_, ...), custom_call_target="tpu_custom_call" | custom-call | flops 1000000000 | tf_op jit(solution)/shard_map/pallas_call | solution.py:22
  81.2 1.1 %collective-permute-done.25.refs_1_ = f32[144,128]{1,0:T(8,128)S(1)} collective-permute-done((f32[144,128]{1,0:T(8,128)S(1)}, f32[144,128]{1,0:T(8,128)S(1)}, u32[]{:S(2)}, u32[]{:S(2)}) %collective-permute-start.25) | collective-permute-done | bytes 73760 | tf_op jit(solution)/shard_map/ppermute | solution.py:326
  82.2 0.4 shard_map.93
  82.7 0.1 collective-permute-start.29
  82.8 1.2 %shard_map.94.begun = f32[512,256]{1,0:T(8,128)} custom-call(f32[512,128]{1,0:T(8,128)S(1)} %get-tuple-element.144.base, bf16[512,768]{1,0:T(8,128)(2,1)S(1)} %get-tuple-element.96.refs_8_.far, f32[96,128]{1,0:T(8,128)S(1)} %get-tuple-element.139.refs_0_, f32[144,128]{1,0:T(8,128)S(1)} %collective-permute-done.25.refs_1_, ...), custom_call_target="tpu_custom_call" | custom-call | flops 1000000000 | tf_op jit(solution)/shard_map/pallas_call | solution.py:22
  83.9 0.4 collective-permute-done.29.got
  84.3 0.7 shard_map.95
  (33 shorter events, 0.1 us)
Async XLA Ops:
  0.0 1.6 %copy-start = (f32[4,8,128,128]{3,2,1,0:T(8,128)S(1)}, f32[4,8,128,128]{3,2,1,0:T(8,128)}, u32[]{:S(2)}) copy-start(f32[4,8,128,128]{3,2,1,0:T(8,128)} %tiles.3) | copy-start | bytes 6291460
  1.6 0.7 copy-start.3
  2.3 1.6 %copy-start.1 = (f32[4,8,128,128]{3,2,1,0:T(8,128)S(1)}, f32[4,8,128,128]{3,2,1,0:T(8,128)}, u32[]{:S(2)}) copy-start(f32[4,8,128,128]{3,2,1,0:T(8,128)} %tiles.2) | copy-start | bytes 6291460
  2.3 1.6 %copy-start.4 = (s32[4,8]{1,0:T(4,128)S(1)}, s32[4,8]{1,0:T(4,128)}, u32[]{:S(2)}) copy-start(s32[4,8]{1,0:T(4,128)} %columns.2) | copy-start | bytes 388
  3.2 2.2 %copy-start.5 = (f32[512,256]{1,0:T(8,128)S(1)}, f32[512,256]{1,0:T(8,128)}, u32[]{:S(2)}) copy-start(f32[512,256]{1,0:T(8,128)} %x.2) | copy-start | bytes 1572868
  3.2 16.3 %collective-permute-start.3 = (f32[4,7,128,128]{3,2,1,0:T(8,128)S(1)}, f32[4,7,128,128]{3,2,1,0:T(8,128)S(1)}, u32[]{:S(2)}, u32[]{:S(2)}) collective-permute-start(f32[4,7,128,128]{3,2,1,0:T(8,128)S(1)} %shard_map.78.total), channel_id=1, source_target_pairs={{0,1},{1,0},{2,3},{3,2},{4,5},{5,4},{6,7},{7,6},{8,9},{9,8},{10,11... | collective-permute-start | bytes 5505032 | tf_op jit(solution)/shard_map/ppermute | solution.py:100
  4.8 0.7 copy-start.6
  4.8 1.2 %copy-start.2 = (f32[512,256]{1,0:T(8,128)S(1)}, f32[512,256]{1,0:T(8,128)}, u32[]{:S(2)}) copy-start(f32[512,256]{1,0:T(8,128)} %x.3) | copy-start | bytes 1572868
  4.8 26.8 %collective-permute-start.2 = (f32[4,7,128,128]{3,2,1,0:T(8,128)S(1)}, f32[4,7,128,128]{3,2,1,0:T(8,128)S(1)}, u32[]{:S(2)}, u32[]{:S(2)}) collective-permute-start(f32[4,7,128,128]{3,2,1,0:T(8,128)S(1)} %shard_map.75.total), channel_id=1, source_target_pairs={{0,1},{1,0},{2,3},{3,2},{4,5},{5,4},{6,7},{7,6},{8,9},{9,8},{10,11... | collective-permute-start | bytes 5505032 | tf_op jit(solution)/shard_map/ppermute | solution.py:100
  5.4 4.8 %collective-permute-start = (f32[512,128]{1,0:T(8,128)S(1)}, f32[512,128]{1,0:T(8,128)S(1)}, u32[]{:S(2)}, u32[]{:S(2)}) collective-permute-start(f32[512,128]{1,0:T(8,128)S(1)} %get-tuple-element.76), channel_id=1, source_target_pairs={{0,1},{1,0},{2,3},{3,2},{4,5},{5,4},{6,7},{7,6},{8,9},{9,8},{10,11... | collective-permute-start | bytes 786440 | tf_op jit(solution)/shard_map/ppermute | solution.py:100
  5.5 4.7 %collective-permute-start.1 = (s32[8,48]{1,0:T(8,128)S(1)}, s32[8,48]{1,0:T(8,128)S(1)}, u32[]{:S(2)}, u32[]{:S(2)}) collective-permute-start(s32[8,48]{1,0:T(8,128)S(1)} %copy-done.6), channel_id=1, source_target_pairs={{0,1},{1,0},{2,3},{3,2},{4,5},{5,4},{6,7},{7,6},{8,9},{9,8},{10,11... | collective-permute-start | bytes 4616 | tf_op jit(solution)/shard_map/ppermute | solution.py:100
  6.0 14.7 %collective-permute-start.4 = (f32[512,128]{1,0:T(8,128)S(1)}, f32[512,128]{1,0:T(8,128)S(1)}, u32[]{:S(2)}, u32[]{:S(2)}) collective-permute-start(f32[512,128]{1,0:T(8,128)S(1)} %get-tuple-element.84), channel_id=1, source_target_pairs={{0,1},{1,0},{2,3},{3,2},{4,5},{5,4},{6,7},{7,6},{8,9},{9,8},{10,11... | collective-permute-start | bytes 786440 | tf_op jit(solution)/shard_map/ppermute | solution.py:100
  10.9 12.5 %collective-permute-start.5 = (f32[144,128]{1,0:T(8,128)S(1)}, f32[144,128]{1,0:T(8,128)S(1)}, u32[]{:S(2)}, u32[]{:S(2)}) collective-permute-start(f32[144,128]{1,0:T(8,128)S(1)} %get-tuple-element.90), channel_id=1, source_target_pairs={{0,4},{1,5},{2,30},{3,31},{4,8},{5,9},{6,10},{7,11},{8,12},{9,13},... | collective-permute-start | bytes 221192 | tf_op jit(solution)/shard_map/ppermute | solution.py:326
  13.8 11.4 %collective-permute-start.6 = (f32[192,128]{1,0:T(8,128)S(1)}, f32[192,128]{1,0:T(8,128)S(1)}, u32[]{:S(2)}, u32[]{:S(2)}) collective-permute-start(f32[192,128]{1,0:T(8,128)S(1)} %get-tuple-element.91), channel_id=1, source_target_pairs={{0,30},{1,31},{2,4},{3,5},{4,2},{5,3},{6,8},{7,9},{8,6},{9,7},{10,... | collective-permute-start | bytes 294920 | tf_op jit(solution)/shard_map/ppermute | solution.py:326
  19.5 5.7 %collective-permute-start.8 = (f32[192,128]{1,0:T(8,128)S(1)}, f32[192,128]{1,0:T(8,128)S(1)}, u32[]{:S(2)}, u32[]{:S(2)}) collective-permute-start(f32[192,128]{1,0:T(8,128)S(1)} %get-tuple-element.93), channel_id=1, source_target_pairs={{0,2},{1,3},{2,0},{3,1},{4,6},{5,7},{6,4},{7,5},{8,10},{9,11},{10,... | collective-permute-start | bytes 294920 | tf_op jit(solution)/shard_map/ppermute | solution.py:326
  20.8 4.4 %collective-permute-start.7 = (f32[144,128]{1,0:T(8,128)S(1)}, f32[144,128]{1,0:T(8,128)S(1)}, u32[]{:S(2)}, u32[]{:S(2)}) collective-permute-start(f32[144,128]{1,0:T(8,128)S(1)} %get-tuple-element.92), channel_id=1, source_target_pairs={{0,28},{1,29},{2,6},{3,7},{4,0},{5,1},{6,2},{7,3},{8,4},{9,5},{10,... | collective-permute-start | bytes 221192 | tf_op jit(solution)/shard_map/ppermute | solution.py:326
  25.8 8.2 %collective-permute-start.9 = (f32[144,128]{1,0:T(8,128)S(1)}, f32[144,128]{1,0:T(8,128)S(1)}, u32[]{:S(2)}, u32[]{:S(2)}) collective-permute-start(f32[144,128]{1,0:T(8,128)S(1)} %get-tuple-element.103), channel_id=1, source_target_pairs={{0,4},{1,5},{2,30},{3,31},{4,8},{5,9},{6,10},{7,11},{8,12},{9,13},... | collective-permute-start | bytes 221192 | tf_op jit(solution)/shard_map/ppermute | solution.py:326
  28.2 8.8 %collective-permute-start.10 = (f32[192,128]{1,0:T(8,128)S(1)}, f32[192,128]{1,0:T(8,128)S(1)}, u32[]{:S(2)}, u32[]{:S(2)}) collective-permute-start(f32[192,128]{1,0:T(8,128)S(1)} %get-tuple-element.104), channel_id=1, source_target_pairs={{0,30},{1,31},{2,4},{3,5},{4,2},{5,3},{6,8},{7,9},{8,6},{9,7},{10,... | collective-permute-start | bytes 294920 | tf_op jit(solution)/shard_map/ppermute | solution.py:326
  31.6 5.4 %collective-permute-start.11 = (f32[144,128]{1,0:T(8,128)S(1)}, f32[144,128]{1,0:T(8,128)S(1)}, u32[]{:S(2)}, u32[]{:S(2)}) collective-permute-start(f32[144,128]{1,0:T(8,128)S(1)} %get-tuple-element.105), channel_id=1, source_target_pairs={{0,28},{1,29},{2,6},{3,7},{4,0},{5,1},{6,2},{7,3},{8,4},{9,5},{10,... | collective-permute-start | bytes 221192 | tf_op jit(solution)/shard_map/ppermute | solution.py:326
  31.6 5.4 %collective-permute-start.12 = (f32[192,128]{1,0:T(8,128)S(1)}, f32[192,128]{1,0:T(8,128)S(1)}, u32[]{:S(2)}, u32[]{:S(2)}) collective-permute-start(f32[192,128]{1,0:T(8,128)S(1)} %get-tuple-element.106), channel_id=1, source_target_pairs={{0,2},{1,3},{2,0},{3,1},{4,6},{5,7},{6,4},{7,5},{8,10},{9,11},{10,... | collective-permute-start | bytes 294920 | tf_op jit(solution)/shard_map/ppermute | solution.py:326
  37.6 10.0 %collective-permute-start.14 = (f32[192,128]{1,0:T(8,128)S(1)}, f32[192,128]{1,0:T(8,128)S(1)}, u32[]{:S(2)}, u32[]{:S(2)}) collective-permute-start(f32[192,128]{1,0:T(8,128)S(1)} %get-tuple-element.115), channel_id=1, source_target_pairs={{0,30},{1,31},{2,4},{3,5},{4,2},{5,3},{6,8},{7,9},{8,6},{9,7},{10,... | collective-permute-start | bytes 294920 | tf_op jit(solution)/shard_map/ppermute | solution.py:326
  40.6 7.1 %collective-permute-start.16 = (f32[192,128]{1,0:T(8,128)S(1)}, f32[192,128]{1,0:T(8,128)S(1)}, u32[]{:S(2)}, u32[]{:S(2)}) collective-permute-start(f32[192,128]{1,0:T(8,128)S(1)} %get-tuple-element.117), channel_id=1, source_target_pairs={{0,2},{1,3},{2,0},{3,1},{4,6},{5,7},{6,4},{7,5},{8,10},{9,11},{10,... | collective-permute-start | bytes 294920 | tf_op jit(solution)/shard_map/ppermute | solution.py:326
  40.6 7.0 %collective-permute-start.13 = (f32[144,128]{1,0:T(8,128)S(1)}, f32[144,128]{1,0:T(8,128)S(1)}, u32[]{:S(2)}, u32[]{:S(2)}) collective-permute-start(f32[144,128]{1,0:T(8,128)S(1)} %get-tuple-element.114), channel_id=1, source_target_pairs={{0,4},{1,5},{2,30},{3,31},{4,8},{5,9},{6,10},{7,11},{8,12},{9,13},... | collective-permute-start | bytes 221192 | tf_op jit(solution)/shard_map/ppermute | solution.py:326
  40.9 6.7 %collective-permute-start.15 = (f32[144,128]{1,0:T(8,128)S(1)}, f32[144,128]{1,0:T(8,128)S(1)}, u32[]{:S(2)}, u32[]{:S(2)}) collective-permute-start(f32[144,128]{1,0:T(8,128)S(1)} %get-tuple-element.116), channel_id=1, source_target_pairs={{0,28},{1,29},{2,6},{3,7},{4,0},{5,1},{6,2},{7,3},{8,4},{9,5},{10,... | collective-permute-start | bytes 221192 | tf_op jit(solution)/shard_map/ppermute | solution.py:326
  48.3 10.9 %collective-permute-start.18 = (f32[192,128]{1,0:T(8,128)S(1)}, f32[192,128]{1,0:T(8,128)S(1)}, u32[]{:S(2)}, u32[]{:S(2)}) collective-permute-start(f32[192,128]{1,0:T(8,128)S(1)} %get-tuple-element.124), channel_id=1, source_target_pairs={{0,30},{1,31},{2,4},{3,5},{4,2},{5,3},{6,8},{7,9},{8,6},{9,7},{10,... | collective-permute-start | bytes 294920 | tf_op jit(solution)/shard_map/ppermute | solution.py:326
  52.1 7.1 %collective-permute-start.20 = (f32[192,128]{1,0:T(8,128)S(1)}, f32[192,128]{1,0:T(8,128)S(1)}, u32[]{:S(2)}, u32[]{:S(2)}) collective-permute-start(f32[192,128]{1,0:T(8,128)S(1)} %get-tuple-element.126), channel_id=1, source_target_pairs={{0,2},{1,3},{2,0},{3,1},{4,6},{5,7},{6,4},{7,5},{8,10},{9,11},{10,... | collective-permute-start | bytes 294920 | tf_op jit(solution)/shard_map/ppermute | solution.py:326
  52.1 7.0 %collective-permute-start.17 = (f32[144,128]{1,0:T(8,128)S(1)}, f32[144,128]{1,0:T(8,128)S(1)}, u32[]{:S(2)}, u32[]{:S(2)}) collective-permute-start(f32[144,128]{1,0:T(8,128)S(1)} %get-tuple-element.123), channel_id=1, source_target_pairs={{0,4},{1,5},{2,30},{3,31},{4,8},{5,9},{6,10},{7,11},{8,12},{9,13},... | collective-permute-start | bytes 221192 | tf_op jit(solution)/shard_map/ppermute | solution.py:326
  52.1 7.0 %collective-permute-start.19 = (f32[144,128]{1,0:T(8,128)S(1)}, f32[144,128]{1,0:T(8,128)S(1)}, u32[]{:S(2)}, u32[]{:S(2)}) collective-permute-start(f32[144,128]{1,0:T(8,128)S(1)} %get-tuple-element.125), channel_id=1, source_target_pairs={{0,28},{1,29},{2,6},{3,7},{4,0},{5,1},{6,2},{7,3},{8,4},{9,5},{10,... | collective-permute-start | bytes 221192 | tf_op jit(solution)/shard_map/ppermute | solution.py:326
  59.8 10.7 %collective-permute-start.22 = (f32[192,128]{1,0:T(8,128)S(1)}, f32[192,128]{1,0:T(8,128)S(1)}, u32[]{:S(2)}, u32[]{:S(2)}) collective-permute-start(f32[192,128]{1,0:T(8,128)S(1)} %get-tuple-element.133), channel_id=1, source_target_pairs={{0,30},{1,31},{2,4},{3,5},{4,2},{5,3},{6,8},{7,9},{8,6},{9,7},{10,... | collective-permute-start | bytes 294920 | tf_op jit(solution)/shard_map/ppermute | solution.py:326
  63.3 7.2 %collective-permute-start.24 = (f32[192,128]{1,0:T(8,128)S(1)}, f32[192,128]{1,0:T(8,128)S(1)}, u32[]{:S(2)}, u32[]{:S(2)}) collective-permute-start(f32[192,128]{1,0:T(8,128)S(1)} %get-tuple-element.135), channel_id=1, source_target_pairs={{0,2},{1,3},{2,0},{3,1},{4,6},{5,7},{6,4},{7,5},{8,10},{9,11},{10,... | collective-permute-start | bytes 294920 | tf_op jit(solution)/shard_map/ppermute | solution.py:326
  63.3 7.0 %collective-permute-start.21 = (f32[144,128]{1,0:T(8,128)S(1)}, f32[144,128]{1,0:T(8,128)S(1)}, u32[]{:S(2)}, u32[]{:S(2)}) collective-permute-start(f32[144,128]{1,0:T(8,128)S(1)} %get-tuple-element.132), channel_id=1, source_target_pairs={{0,4},{1,5},{2,30},{3,31},{4,8},{5,9},{6,10},{7,11},{8,12},{9,13},... | collective-permute-start | bytes 221192 | tf_op jit(solution)/shard_map/ppermute | solution.py:326
  63.8 6.6 %collective-permute-start.23 = (f32[144,128]{1,0:T(8,128)S(1)}, f32[144,128]{1,0:T(8,128)S(1)}, u32[]{:S(2)}, u32[]{:S(2)}) collective-permute-start(f32[144,128]{1,0:T(8,128)S(1)} %get-tuple-element.134), channel_id=1, source_target_pairs={{0,28},{1,29},{2,6},{3,7},{4,0},{5,1},{6,2},{7,3},{8,4},{9,5},{10,... | collective-permute-start | bytes 221192 | tf_op jit(solution)/shard_map/ppermute | solution.py:326
  71.1 11.2 %collective-permute-start.26 = (f32[192,128]{1,0:T(8,128)S(1)}, f32[192,128]{1,0:T(8,128)S(1)}, u32[]{:S(2)}, u32[]{:S(2)}) collective-permute-start(f32[192,128]{1,0:T(8,128)S(1)} %get-tuple-element.141), channel_id=1, source_target_pairs={{0,30},{1,31},{2,4},{3,5},{4,2},{5,3},{6,8},{7,9},{8,6},{9,7},{10,... | collective-permute-start | bytes 294920 | tf_op jit(solution)/shard_map/ppermute | solution.py:326
  75.2 7.1 %collective-permute-start.28 = (f32[192,128]{1,0:T(8,128)S(1)}, f32[192,128]{1,0:T(8,128)S(1)}, u32[]{:S(2)}, u32[]{:S(2)}) collective-permute-start(f32[192,128]{1,0:T(8,128)S(1)} %get-tuple-element.143), channel_id=1, source_target_pairs={{0,2},{1,3},{2,0},{3,1},{4,6},{5,7},{6,4},{7,5},{8,10},{9,11},{10,... | collective-permute-start | bytes 294920 | tf_op jit(solution)/shard_map/ppermute | solution.py:326
  75.2 7.0 %collective-permute-start.25 = (f32[144,128]{1,0:T(8,128)S(1)}, f32[144,128]{1,0:T(8,128)S(1)}, u32[]{:S(2)}, u32[]{:S(2)}) collective-permute-start(f32[144,128]{1,0:T(8,128)S(1)} %get-tuple-element.140), channel_id=1, source_target_pairs={{0,4},{1,5},{2,30},{3,31},{4,8},{5,9},{6,10},{7,11},{8,12},{9,13},... | collective-permute-start | bytes 221192 | tf_op jit(solution)/shard_map/ppermute | solution.py:326
  75.3 6.9 %collective-permute-start.27 = (f32[144,128]{1,0:T(8,128)S(1)}, f32[144,128]{1,0:T(8,128)S(1)}, u32[]{:S(2)}, u32[]{:S(2)}) collective-permute-start(f32[144,128]{1,0:T(8,128)S(1)} %get-tuple-element.142), channel_id=1, source_target_pairs={{0,28},{1,29},{2,6},{3,7},{4,0},{5,1},{6,2},{7,3},{8,4},{9,5},{10,... | collective-permute-start | bytes 221192 | tf_op jit(solution)/shard_map/ppermute | solution.py:326
  82.7 1.6 %collective-permute-start.29 = (f32[512,128]{1,0:T(8,128)S(1)}, f32[512,128]{1,0:T(8,128)S(1)}, u32[]{:S(2)}, u32[]{:S(2)}) collective-permute-start(f32[512,128]{1,0:T(8,128)S(1)} %shard_map.93), channel_id=1, source_target_pairs={{0,1},{1,0},{2,3},{3,2},{4,5},{5,4},{6,7},{7,6},{8,9},{9,8},{10,11... | collective-permute-start | bytes 786440 | tf_op jit(solution)/shard_map/ppermute | solution.py:100

commit v5 on v4

--- a/solution.py
+++ b/solution.py
@@ -54,9 +54,11 @@
     return hop if forward[pair % len(forward)] else -hop
 
 
-def by_pair(table):
+def by_pair(table, pair):
     if len(set(table)) == 1:
         return table[0]
+    if pair is not None:
+        return table[pair % len(table)]
     pair = lax.rem(lax.axis_index("rows") // 2, len(table))
     value = table[0]
     for i in range(1, len(table)):
@@ -64,17 +66,26 @@
     return value
 
 
-def sent_forward(step):
-    return by_pair(step[1])
-
-
-def came_forward(step):
+def sent_forward(step, pair):
+    return by_pair(step[1], pair)
+
+
+def came_forward(step, pair):
     hop, forward = step[:2]
     count = len(forward)
     table = [0] * count
+    for sender in range(count):
+        table[(sender + hop_of(hop, forward, sender)) % count] = forward[sender]
+    return by_pair(table, pair)
+
+
+def on_each_pair(steps, body):
+    count = max(len(step[1]) for step in steps[1])
     for pair in range(count):
-        table[(pair + hop_of(hop, forward, pair)) % count] = forward[pair]
-    return by_pair(table)
+
+        @pl.when(lax.rem(lax.axis_index("rows") // 2, count) == pair)
+        def _(pair=pair):
+            body(pair)
 
 
 def blend(backward, forward, is_forward):
@@ -184,26 +195,26 @@
     out[...] = dot(onehot[...], far[...]).astype(BF16)
 
 
-def deal(steps, lists, outs):
+def deal(steps, lists, outs, pair=None):
     local, far = steps
     length = outs[0].shape[0] // len(local)
     for i, (sender, index, _) in enumerate(local):
         outs[0][block(i, length), :] = lists[sender, block(index, length), :]
     for step, out in zip(far, outs[1:]):
-        is_forward = sent_forward(step)
+        is_forward = sent_forward(step, pair)
         for i, (backward, forward) in enumerate(zip(*step[2:])):
             sender = blend(backward[0], forward[0], is_forward)
             index = blend(backward[1], forward[1], is_forward)
             out[block(i, length), :] = lists[sender, block(index, length), :]
 
 
-def collect(steps, arrived, halo):
+def collect(steps, arrived, halo, pair=None):
     local, far = steps
     length = arrived[0].shape[0] // len(local)
     for i, (_, index, receiver) in enumerate(local):
         halo[receiver, block(index, length), :] = terms(arrived[0][block(i, length), :])
     for step, piece in zip(far, arrived[1:]):
-        is_forward = came_forward(step)
+        is_forward = came_forward(step, pair)
         for i, (backward, forward) in enumerate(zip(*step[2:])):
             receiver = blend(backward[2], forward[2], is_forward)
             index = blend(backward[1], forward[1], is_forward)
@@ -217,7 +228,7 @@
     ):
         fill_onehot(rows, onehot)
         lists[role_slot(role)] = pick_rows(onehot[...], state[...])
-    deal(steps, lists, outs)
+    on_each_pair(steps, lambda pair: deal(steps, lists, outs, pair))
 
 
 def own_kernel(steps, has_source, first, last, *refs):
@@ -256,11 +267,15 @@
     picks, outs_of = refs[:2], refs[2:4]
     arrived, outs = refs[4 : 4 + count], refs[4 + count : 4 + 2 * count]
     halo, lists = refs[4 + 2 * count :]
-    collect(steps, arrived, halo)
-    rows = [picks[role][...] + product(outs_of[role][...], halo[role_slot(role)]) for role in range(2)]
-    for role in range(2):
-        lists[role_slot(role)] = rows[role]
-    deal(steps, lists, outs)
+
+    def body(place, pair):
+        collect(steps, arrived, halo, pair)
+        for role in range(2):
+            slot = role ^ place
+            lists[slot] = picks[role][...] + product(outs_of[role][...], halo[slot])
+        deal(steps, lists, outs, pair)
+
+    on_each_pair(steps, lambda pair: on_each_side(lambda place: body(place, pair)))
 
 
 def give_back_kernel(steps, base, far, *refs):

time: 85.4 us -> 85.1 us (level)
  transfers between devices with their start and end apart: 30 -> 30, of which waited for: 9 -> 8; matrix products, arithmetic and copies ran while one was open for 0% -> 0% of each run, Pallas kernels for 17% -> 17%
where the time goes in v5:
time: 85.1 us; the launch traced here: 84.9 us
  starting transfers between devices  50.7 us (60%)
  Pallas kernels  19 us (22%)
  waiting for transfers between devices  12.4 us (15%)
  local copies, waits for them, and re-layouts  2.4 us (3%)
    ppermute x24, starting transfers between devices, exchange(): arrived.append(lax.ppermute(piece, 'rows', pairs))  48.5 us
    pallas_call x23, Pallas kernels, call(): pl.pallas_call(kernel, out_shape=[jax.ShapeDtypeStruct(shape, dtype) for...  19 us
    ppermute x24, waiting for transfers between devices, exchange(): arrived.append(lax.ppermute(piece, 'rows', pairs))  8.28 us
    ppermute x6, waiting for transfers between devices, swap(): return lax.ppermute(x, 'rows', [(i, i ^ 1) for i in range(devices)])  4.11 us
    unnamed x14, local copies, waits for them, and re-layouts  2.4 us
    ppermute x6, starting transfers between devices, swap(): return lax.ppermute(x, 'rows', [(i, i ^ 1) for i in range(devices)])  2.17 us
  transfers between devices with their start and end apart: 30, of which 8 were waited for; matrix products, arithmetic and copies ran while one was open for 0% of the time, Pallas kernels for 17%

profile of v5, /device:TPU:0, one launch (start us, length us, event | category | flops | bytes accessed | tf_op | source)
XLA Modules:
  0.0 84.9 jit_solution(4667648074543362293)
XLA Ops:
  0.0 1.6 %copy-done = f32[4,8,128,128]{3,2,1,0:T(8,128)S(1)} copy-done((f32[4,8,128,128]{3,2,1,0:T(8,128)S(1)}, f32[4,8,128,128]{3,2,1,0:T(8,128)}, u32[]{:S(2)}) %copy-start) | copy-done | bytes 2097176
  1.6 0.7 copy-done.3
  2.3 0.9 %shard_map.78.total = f32[4,7,128,128]{3,2,1,0:T(8,128)S(1)} custom-call(s32[4,8]{1,0:T(4,128)S(1)} %copy-done.3, f32[4,8,128,128]{3,2,1,0:T(8,128)S(1)} %copy-done), custom_call_target="tpu_custom_call" | custom-call | flops 1000000000 | tf_op jit(solution)/shard_map/pallas_call | solution.py:22
  3.2 0.0 copy-start.5
  3.2 0.6 collective-permute-start.3
  3.8 0.1 copy-done.1
  3.9 0.9 %shard_map.75.total = f32[4,7,128,128]{3,2,1,0:T(8,128)S(1)} custom-call(s32[4,8]{1,0:T(4,128)S(1)} %copy-done.4, f32[4,8,128,128]{3,2,1,0:T(8,128)S(1)} %copy-done.1), custom_call_target="tpu_custom_call" | custom-call | flops 1000000000 | tf_op jit(solution)/shard_map/pallas_call | solution.py:22
  4.8 0.0 copy-start.6
  4.8 0.0 copy-start.2
  4.8 0.6 collective-permute-start.2
  5.4 0.1 collective-permute-start
  5.5 0.5 collective-permute-start.1
  6.0 0.4 collective-permute-start.4
  6.4 3.7 %collective-permute-done.1.rows_other = s32[8,48]{1,0:T(8,128)S(1)} collective-permute-done((s32[8,48]{1,0:T(8,128)S(1)}, s32[8,48]{1,0:T(8,128)S(1)}, u32[]{:S(2)}, u32[]{:S(2)}) %collective-permute-start.1) | collective-permute-done | bytes 1568 | tf_op jit(solution)/shard_map/ppermute | solution.py:111
  10.2 0.0 collective-permute-done.other.refs_7_
  10.2 0.7 shard_map.74
  10.9 2.9 %collective-permute-start.5 = (f32[144,128]{1,0:T(8,128)S(1)}, f32[144,128]{1,0:T(8,128)S(1)}, u32[]{:S(2)}, u32[]{:S(2)}) collective-permute-start(f32[144,128]{1,0:T(8,128)S(1)} %get-tuple-element.90), channel_id=1, source_target_pairs={{0,4},{1,5},{2,30},{3,31},{4,8},{5,9},{6,10},{7,11},{8,12},{9,13},... | collective-permute-start | bytes 221192 | tf_op jit(solution)/shard_map/ppermute | solution.py:341
  13.8 4.1 %collective-permute-start.6 = (f32[192,128]{1,0:T(8,128)S(1)}, f32[192,128]{1,0:T(8,128)S(1)}, u32[]{:S(2)}, u32[]{:S(2)}) collective-permute-start(f32[192,128]{1,0:T(8,128)S(1)} %get-tuple-element.91), channel_id=1, source_target_pairs={{0,30},{1,31},{2,4},{3,5},{4,2},{5,3},{6,8},{7,9},{8,6},{9,7},{10,... | collective-permute-start | bytes 294920 | tf_op jit(solution)/shard_map/ppermute | solution.py:341
  17.9 0.8 shard_map.76
  18.7 0.8 shard_map.79
  19.5 0.0 collective-permute-done.3.total
  19.5 0.5 collective-permute-start.8
  20.0 0.8 shard_map.80
  20.7 0.0 collective-permute-done.4.refs_5_
  20.7 1.7 %collective-permute-start.7 = (f32[144,128]{1,0:T(8,128)S(1)}, f32[144,128]{1,0:T(8,128)S(1)}, u32[]{:S(2)}, u32[]{:S(2)}) collective-permute-start(f32[144,128]{1,0:T(8,128)S(1)} %get-tuple-element.92), channel_id=1, source_target_pairs={{0,28},{1,29},{2,6},{3,7},{4,0},{5,1},{6,2},{7,3},{8,4},{9,5},{10,... | collective-permute-start | bytes 221192 | tf_op jit(solution)/shard_map/ppermute | solution.py:341
  22.4 1.0 %shard_map.82 = (f32[512,128]{1,0:T(8,128)S(1)}, f32[512,128]{1,0:T(8,128)S(1)}, f32[384,128]{1,0:T(8,128)S(1)}, f32[384,128]{1,0:T(8,128)S(1)}) custom-call(bf16[384,512]{1,0:T(8,128)(2,1)S(1)} %get-tuple-element.77.onehot.refs_0_, bf16[384,512]{1,0:T(8,128)(2,1)S(1)} %get-tuple-element.78.onehot.refs_1_, bf16[512,1024]{1,0:T(8,128)(2,1)S(1)} %get-tuple-element.81.refs_2_, ...), custom_call_target="tpu_custom_call" | custom-call | flops 1000000000 | tf_op jit(solution)/shard_map/pallas_call | solution.py:22
  23.4 0.0 collective-permute-done.5.refs_9_.refs_5_
  23.4 1.7 %collective-permute-done.7.refs_11_.refs_7_ = f32[144,128]{1,0:T(8,128)S(1)} collective-permute-done((f32[144,128]{1,0:T(8,128)S(1)}, f32[144,128]{1,0:T(8,128)S(1)}, u32[]{:S(2)}, u32[]{:S(2)}) %collective-permute-start.7) | collective-permute-done | bytes 73760 | tf_op jit(solution)/shard_map/ppermute | solution.py:341
  25.1 0.0 collective-permute-done.8.refs_12_.refs_8_
  25.1 0.5 shard_map.84
  25.6 2.4 %collective-permute-start.9 = (f32[144,128]{1,0:T(8,128)S(1)}, f32[144,128]{1,0:T(8,128)S(1)}, u32[]{:S(2)}, u32[]{:S(2)}) collective-permute-start(f32[144,128]{1,0:T(8,128)S(1)} %get-tuple-element.103), channel_id=1, source_target_pairs={{0,4},{1,5},{2,30},{3,31},{4,8},{5,9},{6,10},{7,11},{8,12},{9,13},... | collective-permute-start | bytes 221192 | tf_op jit(solution)/shard_map/ppermute | solution.py:341
  28.1 3.4 %collective-permute-start.10 = (f32[192,128]{1,0:T(8,128)S(1)}, f32[192,128]{1,0:T(8,128)S(1)}, u32[]{:S(2)}, u32[]{:S(2)}) collective-permute-start(f32[192,128]{1,0:T(8,128)S(1)} %get-tuple-element.104), channel_id=1, source_target_pairs={{0,30},{1,31},{2,4},{3,5},{4,2},{5,3},{6,8},{7,9},{8,6},{9,7},{10,... | collective-permute-start | bytes 294920 | tf_op jit(solution)/shard_map/ppermute | solution.py:341
  31.5 0.8 shard_map.77
  32.2 1.5 %shard_map.83 = (f32[512,128]{1,0:T(8,128)S(1)}, f32[512,128]{1,0:T(8,128)S(1)}, f32[384,128]{1,0:T(8,128)S(1)}, f32[384,128]{1,0:T(8,128)S(1)}) custom-call(bf16[384,512]{1,0:T(8,128)(2,1)S(1)} %get-tuple-element.77.onehot.refs_0_, bf16[384,512]{1,0:T(8,128)(2,1)S(1)} %get-tuple-element.78.onehot.refs_1_, bf16[512,1024]{1,0:T(8,128)(2,1)S(1)} %get-tuple-element.79.refs_2_, ...), custom_call_target="tpu_custom_call" | custom-call | flops 1000000000 | tf_op jit(solution)/shard_map/pallas_call | solution.py:22
  33.8 3.1 %collective-permute-done.11.refs_13_.refs_7_ = f32[144,128]{1,0:T(8,128)S(1)} collective-permute-done((f32[144,128]{1,0:T(8,128)S(1)}, f32[144,128]{1,0:T(8,128)S(1)}, u32[]{:S(2)}, u32[]{:S(2)}) %collective-permute-start.11) | collective-permute-done | bytes 73760 | tf_op jit(solution)/shard_map/ppermute | solution.py:341
  36.9 0.0 collective-permute-done.10.refs_12_.refs_6_
  36.9 0.7 shard_map.86
  37.6 2.9 %collective-permute-start.14 = (f32[192,128]{1,0:T(8,128)S(1)}, f32[192,128]{1,0:T(8,128)S(1)}, u32[]{:S(2)}, u32[]{:S(2)}) collective-permute-start(f32[192,128]{1,0:T(8,128)S(1)} %get-tuple-element.115), channel_id=1, source_target_pairs={{0,30},{1,31},{2,4},{3,5},{4,2},{5,3},{6,8},{7,9},{8,6},{9,7},{10,... | collective-permute-start | bytes 294920 | tf_op jit(solution)/shard_map/ppermute | solution.py:341
  40.5 0.3 collective-permute-start.13
  40.8 4.4 %collective-permute-start.15 = (f32[144,128]{1,0:T(8,128)S(1)}, f32[144,128]{1,0:T(8,128)S(1)}, u32[]{:S(2)}, u32[]{:S(2)}) collective-permute-start(f32[144,128]{1,0:T(8,128)S(1)} %get-tuple-element.116), channel_id=1, source_target_pairs={{0,28},{1,29},{2,6},{3,7},{4,0},{5,1},{6,2},{7,3},{8,4},{9,5},{10,... | collective-permute-start | bytes 221192 | tf_op jit(solution)/shard_map/ppermute | solution.py:341
  45.2 1.5 %shard_map.85 = (f32[512,128]{1,0:T(8,128)S(1)}, f32[512,128]{1,0:T(8,128)S(1)}, f32[384,128]{1,0:T(8,128)S(1)}, f32[384,128]{1,0:T(8,128)S(1)}) custom-call(bf16[384,512]{1,0:T(8,128)(2,1)S(1)} %get-tuple-element.77.onehot.refs_0_, bf16[384,512]{1,0:T(8,128)(2,1)S(1)} %get-tuple-element.78.onehot.refs_1_, bf16[512,1024]{1,0:T(8,128)(2,1)S(1)} %get-tuple-element.81.refs_2_, ...), custom_call_target="tpu_custom_call" | custom-call | flops 1000000000 | tf_op jit(solution)/shard_map/pallas_call | solution.py:22
  46.8 0.8 collective-permute-done.13.refs_9_.refs_5_
  47.6 0.5 shard_map.88
  48.1 3.8 %collective-permute-start.18 = (f32[192,128]{1,0:T(8,128)S(1)}, f32[192,128]{1,0:T(8,128)S(1)}, u32[]{:S(2)}, u32[]{:S(2)}) collective-permute-start(f32[192,128]{1,0:T(8,128)S(1)} %get-tuple-element.124), channel_id=1, source_target_pairs={{0,30},{1,31},{2,4},{3,5},{4,2},{5,3},{6,8},{7,9},{8,6},{9,7},{10,... | collective-permute-start | bytes 294920 | tf_op jit(solution)/shard_map/ppermute | solution.py:341
  51.9 4.7 %collective-permute-start.19 = (f32[144,128]{1,0:T(8,128)S(1)}, f32[144,128]{1,0:T(8,128)S(1)}, u32[]{:S(2)}, u32[]{:S(2)}) collective-permute-start(f32[144,128]{1,0:T(8,128)S(1)} %get-tuple-element.125), channel_id=1, source_target_pairs={{0,28},{1,29},{2,6},{3,7},{4,0},{5,1},{6,2},{7,3},{8,4},{9,5},{10,... | collective-permute-start | bytes 221192 | tf_op jit(solution)/shard_map/ppermute | solution.py:341
  56.6 1.5 %shard_map.87 = (f32[512,128]{1,0:T(8,128)S(1)}, f32[512,128]{1,0:T(8,128)S(1)}, f32[384,128]{1,0:T(8,128)S(1)}, f32[384,128]{1,0:T(8,128)S(1)}) custom-call(bf16[384,512]{1,0:T(8,128)(2,1)S(1)} %get-tuple-element.77.onehot.refs_0_, bf16[384,512]{1,0:T(8,128)(2,1)S(1)} %get-tuple-element.78.onehot.refs_1_, bf16[512,1024]{1,0:T(8,128)(2,1)S(1)} %get-tuple-element.79.refs_2_, ...), custom_call_target="tpu_custom_call" | custom-call | flops 1000000000 | tf_op jit(solution)/shard_map/pallas_call | solution.py:22
  58.2 0.8 collective-permute-done.17.refs_11_.refs_5_
  59.0 0.5 shard_map.90
  59.5 3.5 %collective-permute-start.22 = (f32[192,128]{1,0:T(8,128)S(1)}, f32[192,128]{1,0:T(8,128)S(1)}, u32[]{:S(2)}, u32[]{:S(2)}) collective-permute-start(f32[192,128]{1,0:T(8,128)S(1)} %get-tuple-element.133), channel_id=1, source_target_pairs={{0,30},{1,31},{2,4},{3,5},{4,2},{5,3},{6,8},{7,9},{8,6},{9,7},{10,... | collective-permute-start | bytes 294920 | tf_op jit(solution)/shard_map/ppermute | solution.py:341
  63.0 0.6 collective-permute-start.21
  63.6 4.1 %collective-permute-start.23 = (f32[144,128]{1,0:T(8,128)S(1)}, f32[144,128]{1,0:T(8,128)S(1)}, u32[]{:S(2)}, u32[]{:S(2)}) collective-permute-start(f32[144,128]{1,0:T(8,128)S(1)} %get-tuple-element.134), channel_id=1, source_target_pairs={{0,28},{1,29},{2,6},{3,7},{4,0},{5,1},{6,2},{7,3},{8,4},{9,5},{10,... | collective-permute-start | bytes 221192 | tf_op jit(solution)/shard_map/ppermute | solution.py:341
  67.7 1.5 %shard_map.89 = (f32[512,128]{1,0:T(8,128)S(1)}, f32[512,128]{1,0:T(8,128)S(1)}, f32[384,128]{1,0:T(8,128)S(1)}, f32[384,128]{1,0:T(8,128)S(1)}) custom-call(bf16[384,512]{1,0:T(8,128)(2,1)S(1)} %get-tuple-element.77.onehot.refs_0_, bf16[384,512]{1,0:T(8,128)(2,1)S(1)} %get-tuple-element.78.onehot.refs_1_, bf16[512,1024]{1,0:T(8,128)(2,1)S(1)} %get-tuple-element.81.refs_2_, ...), custom_call_target="tpu_custom_call" | custom-call | flops 1000000000 | tf_op jit(solution)/shard_map/pallas_call | solution.py:22
  69.3 0.8 collective-permute-done.21.refs_9_.refs_5_
  70.1 0.5 shard_map.92
  70.6 4.3 %collective-permute-start.26 = (f32[192,128]{1,0:T(8,128)S(1)}, f32[192,128]{1,0:T(8,128)S(1)}, u32[]{:S(2)}, u32[]{:S(2)}) collective-permute-start(f32[192,128]{1,0:T(8,128)S(1)} %get-tuple-element.141), channel_id=1, source_target_pairs={{0,30},{1,31},{2,4},{3,5},{4,2},{5,3},{6,8},{7,9},{8,6},{9,7},{10,... | collective-permute-start | bytes 294920 | tf_op jit(solution)/shard_map/ppermute | solution.py:341
  74.9 0.0 collective-permute-start.25
  74.9 4.7 %collective-permute-start.27 = (f32[144,128]{1,0:T(8,128)S(1)}, f32[144,128]{1,0:T(8,128)S(1)}, u32[]{:S(2)}, u32[]{:S(2)}) collective-permute-start(f32[144,128]{1,0:T(8,128)S(1)} %get-tuple-element.142), channel_id=1, source_target_pairs={{0,28},{1,29},{2,6},{3,7},{4,0},{5,1},{6,2},{7,3},{8,4},{9,5},{10,... | collective-permute-start | bytes 221192 | tf_op jit(solution)/shard_map/ppermute | solution.py:341
  79.6 1.2 %shard_map.91 = (f32[512,128]{1,0:T(8,128)S(1)}, f32[512,128]{1,0:T(8,128)S(1)}) custom-call(bf16[384,512]{1,0:T(8,128)(2,1)S(1)} %get-tuple-element.77.onehot.refs_0_, bf16[384,512]{1,0:T(8,128)(2,1)S(1)} %get-tuple-element.78.onehot.refs_1_, bf16[512,1024]{1,0:T(8,128)(2,1)S(1)} %get-tuple-element.79.refs_2_, ...), custom_call_target="tpu_custom_call" | custom-call | flops 1000000000 | tf_op jit(solution)/shard_map/pallas_call | solution.py:22
  80.9 1.1 %collective-permute-done.25.refs_1_ = f32[144,128]{1,0:T(8,128)S(1)} collective-permute-done((f32[144,128]{1,0:T(8,128)S(1)}, f32[144,128]{1,0:T(8,128)S(1)}, u32[]{:S(2)}, u32[]{:S(2)}) %collective-permute-start.25) | collective-permute-done | bytes 73760 | tf_op jit(solution)/shard_map/ppermute | solution.py:341
  82.0 0.4 shard_map.93
  82.4 0.1 collective-permute-start.29
  82.5 1.2 %shard_map.94.begun = f32[512,256]{1,0:T(8,128)} custom-call(f32[512,128]{1,0:T(8,128)S(1)} %get-tuple-element.144.base, bf16[512,768]{1,0:T(8,128)(2,1)S(1)} %get-tuple-element.96.refs_8_.far, f32[96,128]{1,0:T(8,128)S(1)} %get-tuple-element.139.refs_0_, f32[144,128]{1,0:T(8,128)S(1)} %collective-permute-done.25.refs_1_, ...), custom_call_target="tpu_custom_call" | custom-call | flops 1000000000 | tf_op jit(solution)/shard_map/pallas_call | solution.py:22
  83.7 0.4 collective-permute-done.29.got
  84.0 0.7 shard_map.95
  (33 shorter events, 0.1 us)
Async XLA Ops:
  0.0 1.6 %copy-start = (f32[4,8,128,128]{3,2,1,0:T(8,128)S(1)}, f32[4,8,128,128]{3,2,1,0:T(8,128)}, u32[]{:S(2)}) copy-start(f32[4,8,128,128]{3,2,1,0:T(8,128)} %tiles.3) | copy-start | bytes 6291460
  1.6 0.7 copy-start.3
  2.3 1.6 %copy-start.1 = (f32[4,8,128,128]{3,2,1,0:T(8,128)S(1)}, f32[4,8,128,128]{3,2,1,0:T(8,128)}, u32[]{:S(2)}) copy-start(f32[4,8,128,128]{3,2,1,0:T(8,128)} %tiles.2) | copy-start | bytes 6291460
  2.3 1.6 %copy-start.4 = (s32[4,8]{1,0:T(4,128)S(1)}, s32[4,8]{1,0:T(4,128)}, u32[]{:S(2)}) copy-start(s32[4,8]{1,0:T(4,128)} %columns.2) | copy-start | bytes 388
  3.2 2.2 %copy-start.5 = (f32[512,256]{1,0:T(8,128)S(1)}, f32[512,256]{1,0:T(8,128)}, u32[]{:S(2)}) copy-start(f32[512,256]{1,0:T(8,128)} %x.2) | copy-start | bytes 1572868
  3.2 16.3 %collective-permute-start.3 = (f32[4,7,128,128]{3,2,1,0:T(8,128)S(1)}, f32[4,7,128,128]{3,2,1,0:T(8,128)S(1)}, u32[]{:S(2)}, u32[]{:S(2)}) collective-permute-start(f32[4,7,128,128]{3,2,1,0:T(8,128)S(1)} %shard_map.78.total), channel_id=1, source_target_pairs={{0,1},{1,0},{2,3},{3,2},{4,5},{5,4},{6,7},{7,6},{8,9},{9,8},{10,11... | collective-permute-start | bytes 5505032 | tf_op jit(solution)/shard_map/ppermute | solution.py:111
  4.8 0.7 copy-start.6
  4.8 1.2 %copy-start.2 = (f32[512,256]{1,0:T(8,128)S(1)}, f32[512,256]{1,0:T(8,128)}, u32[]{:S(2)}) copy-start(f32[512,256]{1,0:T(8,128)} %x.3) | copy-start | bytes 1572868
  4.8 26.7 %collective-permute-start.2 = (f32[4,7,128,128]{3,2,1,0:T(8,128)S(1)}, f32[4,7,128,128]{3,2,1,0:T(8,128)S(1)}, u32[]{:S(2)}, u32[]{:S(2)}) collective-permute-start(f32[4,7,128,128]{3,2,1,0:T(8,128)S(1)} %shard_map.75.total), channel_id=1, source_target_pairs={{0,1},{1,0},{2,3},{3,2},{4,5},{5,4},{6,7},{7,6},{8,9},{9,8},{10,11... | collective-permute-start | bytes 5505032 | tf_op jit(solution)/shard_map/ppermute | solution.py:111
  5.4 4.8 %collective-permute-start = (f32[512,128]{1,0:T(8,128)S(1)}, f32[512,128]{1,0:T(8,128)S(1)}, u32[]{:S(2)}, u32[]{:S(2)}) collective-permute-start(f32[512,128]{1,0:T(8,128)S(1)} %get-tuple-element.76), channel_id=1, source_target_pairs={{0,1},{1,0},{2,3},{3,2},{4,5},{5,4},{6,7},{7,6},{8,9},{9,8},{10,11... | collective-permute-start | bytes 786440 | tf_op jit(solution)/shard_map/ppermute | solution.py:111
  5.5 4.7 %collective-permute-start.1 = (s32[8,48]{1,0:T(8,128)S(1)}, s32[8,48]{1,0:T(8,128)S(1)}, u32[]{:S(2)}, u32[]{:S(2)}) collective-permute-start(s32[8,48]{1,0:T(8,128)S(1)} %copy-done.6), channel_id=1, source_target_pairs={{0,1},{1,0},{2,3},{3,2},{4,5},{5,4},{6,7},{7,6},{8,9},{9,8},{10,11... | collective-permute-start | bytes 4616 | tf_op jit(solution)/shard_map/ppermute | solution.py:111
  6.0 14.7 %collective-permute-start.4 = (f32[512,128]{1,0:T(8,128)S(1)}, f32[512,128]{1,0:T(8,128)S(1)}, u32[]{:S(2)}, u32[]{:S(2)}) collective-permute-start(f32[512,128]{1,0:T(8,128)S(1)} %get-tuple-element.84), channel_id=1, source_target_pairs={{0,1},{1,0},{2,3},{3,2},{4,5},{5,4},{6,7},{7,6},{8,9},{9,8},{10,11... | collective-permute-start | bytes 786440 | tf_op jit(solution)/shard_map/ppermute | solution.py:111
  10.9 12.5 %collective-permute-start.5 = (f32[144,128]{1,0:T(8,128)S(1)}, f32[144,128]{1,0:T(8,128)S(1)}, u32[]{:S(2)}, u32[]{:S(2)}) collective-permute-start(f32[144,128]{1,0:T(8,128)S(1)} %get-tuple-element.90), channel_id=1, source_target_pairs={{0,4},{1,5},{2,30},{3,31},{4,8},{5,9},{6,10},{7,11},{8,12},{9,13},... | collective-permute-start | bytes 221192 | tf_op jit(solution)/shard_map/ppermute | solution.py:341
  13.8 11.4 %collective-permute-start.6 = (f32[192,128]{1,0:T(8,128)S(1)}, f32[192,128]{1,0:T(8,128)S(1)}, u32[]{:S(2)}, u32[]{:S(2)}) collective-permute-start(f32[192,128]{1,0:T(8,128)S(1)} %get-tuple-element.91), channel_id=1, source_target_pairs={{0,30},{1,31},{2,4},{3,5},{4,2},{5,3},{6,8},{7,9},{8,6},{9,7},{10,... | collective-permute-start | bytes 294920 | tf_op jit(solution)/shard_map/ppermute | solution.py:341
  19.5 5.7 %collective-permute-start.8 = (f32[192,128]{1,0:T(8,128)S(1)}, f32[192,128]{1,0:T(8,128)S(1)}, u32[]{:S(2)}, u32[]{:S(2)}) collective-permute-start(f32[192,128]{1,0:T(8,128)S(1)} %get-tuple-element.93), channel_id=1, source_target_pairs={{0,2},{1,3},{2,0},{3,1},{4,6},{5,7},{6,4},{7,5},{8,10},{9,11},{10,... | collective-permute-start | bytes 294920 | tf_op jit(solution)/shard_map/ppermute | solution.py:341
  20.7 4.4 %collective-permute-start.7 = (f32[144,128]{1,0:T(8,128)S(1)}, f32[144,128]{1,0:T(8,128)S(1)}, u32[]{:S(2)}, u32[]{:S(2)}) collective-permute-start(f32[144,128]{1,0:T(8,128)S(1)} %get-tuple-element.92), channel_id=1, source_target_pairs={{0,28},{1,29},{2,6},{3,7},{4,0},{5,1},{6,2},{7,3},{8,4},{9,5},{10,... | collective-permute-start | bytes 221192 | tf_op jit(solution)/shard_map/ppermute | solution.py:341
  25.6 8.1 %collective-permute-start.9 = (f32[144,128]{1,0:T(8,128)S(1)}, f32[144,128]{1,0:T(8,128)S(1)}, u32[]{:S(2)}, u32[]{:S(2)}) collective-permute-start(f32[144,128]{1,0:T(8,128)S(1)} %get-tuple-element.103), channel_id=1, source_target_pairs={{0,4},{1,5},{2,30},{3,31},{4,8},{5,9},{6,10},{7,11},{8,12},{9,13},... | collective-permute-start | bytes 221192 | tf_op jit(solution)/shard_map/ppermute | solution.py:341
  28.1 8.8 %collective-permute-start.10 = (f32[192,128]{1,0:T(8,128)S(1)}, f32[192,128]{1,0:T(8,128)S(1)}, u32[]{:S(2)}, u32[]{:S(2)}) collective-permute-start(f32[192,128]{1,0:T(8,128)S(1)} %get-tuple-element.104), channel_id=1, source_target_pairs={{0,30},{1,31},{2,4},{3,5},{4,2},{5,3},{6,8},{7,9},{8,6},{9,7},{10,... | collective-permute-start | bytes 294920 | tf_op jit(solution)/shard_map/ppermute | solution.py:341
  31.5 5.4 %collective-permute-start.11 = (f32[144,128]{1,0:T(8,128)S(1)}, f32[144,128]{1,0:T(8,128)S(1)}, u32[]{:S(2)}, u32[]{:S(2)}) collective-permute-start(f32[144,128]{1,0:T(8,128)S(1)} %get-tuple-element.105), channel_id=1, source_target_pairs={{0,28},{1,29},{2,6},{3,7},{4,0},{5,1},{6,2},{7,3},{8,4},{9,5},{10,... | collective-permute-start | bytes 221192 | tf_op jit(solution)/shard_map/ppermute | solution.py:341
  31.5 5.4 %collective-permute-start.12 = (f32[192,128]{1,0:T(8,128)S(1)}, f32[192,128]{1,0:T(8,128)S(1)}, u32[]{:S(2)}, u32[]{:S(2)}) collective-permute-start(f32[192,128]{1,0:T(8,128)S(1)} %get-tuple-element.106), channel_id=1, source_target_pairs={{0,2},{1,3},{2,0},{3,1},{4,6},{5,7},{6,4},{7,5},{8,10},{9,11},{10,... | collective-permute-start | bytes 294920 | tf_op jit(solution)/shard_map/ppermute | solution.py:341
  37.6 10.0 %collective-permute-start.14 = (f32[192,128]{1,0:T(8,128)S(1)}, f32[192,128]{1,0:T(8,128)S(1)}, u32[]{:S(2)}, u32[]{:S(2)}) collective-permute-start(f32[192,128]{1,0:T(8,128)S(1)} %get-tuple-element.115), channel_id=1, source_target_pairs={{0,30},{1,31},{2,4},{3,5},{4,2},{5,3},{6,8},{7,9},{8,6},{9,7},{10,... | collective-permute-start | bytes 294920 | tf_op jit(solution)/shard_map/ppermute | solution.py:341
  40.5 7.1 %collective-permute-start.16 = (f32[192,128]{1,0:T(8,128)S(1)}, f32[192,128]{1,0:T(8,128)S(1)}, u32[]{:S(2)}, u32[]{:S(2)}) collective-permute-start(f32[192,128]{1,0:T(8,128)S(1)} %get-tuple-element.117), channel_id=1, source_target_pairs={{0,2},{1,3},{2,0},{3,1},{4,6},{5,7},{6,4},{7,5},{8,10},{9,11},{10,... | collective-permute-start | bytes 294920 | tf_op jit(solution)/shard_map/ppermute | solution.py:341
  40.5 7.0 %collective-permute-start.13 = (f32[144,128]{1,0:T(8,128)S(1)}, f32[144,128]{1,0:T(8,128)S(1)}, u32[]{:S(2)}, u32[]{:S(2)}) collective-permute-start(f32[144,128]{1,0:T(8,128)S(1)} %get-tuple-element.114), channel_id=1, source_target_pairs={{0,4},{1,5},{2,30},{3,31},{4,8},{5,9},{6,10},{7,11},{8,12},{9,13},... | collective-permute-start | bytes 221192 | tf_op jit(solution)/shard_map/ppermute | solution.py:341
  40.8 6.7 %collective-permute-start.15 = (f32[144,128]{1,0:T(8,128)S(1)}, f32[144,128]{1,0:T(8,128)S(1)}, u32[]{:S(2)}, u32[]{:S(2)}) collective-permute-start(f32[144,128]{1,0:T(8,128)S(1)} %get-tuple-element.116), channel_id=1, source_target_pairs={{0,28},{1,29},{2,6},{3,7},{4,0},{5,1},{6,2},{7,3},{8,4},{9,5},{10,... | collective-permute-start | bytes 221192 | tf_op jit(solution)/shard_map/ppermute | solution.py:341
  48.1 10.9 %collective-permute-start.18 = (f32[192,128]{1,0:T(8,128)S(1)}, f32[192,128]{1,0:T(8,128)S(1)}, u32[]{:S(2)}, u32[]{:S(2)}) collective-permute-start(f32[192,128]{1,0:T(8,128)S(1)} %get-tuple-element.124), channel_id=1, source_target_pairs={{0,30},{1,31},{2,4},{3,5},{4,2},{5,3},{6,8},{7,9},{8,6},{9,7},{10,... | collective-permute-start | bytes 294920 | tf_op jit(solution)/shard_map/ppermute | solution.py:341
  51.9 7.1 %collective-permute-start.20 = (f32[192,128]{1,0:T(8,128)S(1)}, f32[192,128]{1,0:T(8,128)S(1)}, u32[]{:S(2)}, u32[]{:S(2)}) collective-permute-start(f32[192,128]{1,0:T(8,128)S(1)} %get-tuple-element.126), channel_id=1, source_target_pairs={{0,2},{1,3},{2,0},{3,1},{4,6},{5,7},{6,4},{7,5},{8,10},{9,11},{10,... | collective-permute-start | bytes 294920 | tf_op jit(solution)/shard_map/ppermute | solution.py:341
  51.9 7.0 %collective-permute-start.17 = (f32[144,128]{1,0:T(8,128)S(1)}, f32[144,128]{1,0:T(8,128)S(1)}, u32[]{:S(2)}, u32[]{:S(2)}) collective-permute-start(f32[144,128]{1,0:T(8,128)S(1)} %get-tuple-element.123), channel_id=1, source_target_pairs={{0,4},{1,5},{2,30},{3,31},{4,8},{5,9},{6,10},{7,11},{8,12},{9,13},... | collective-permute-start | bytes 221192 | tf_op jit(solution)/shard_map/ppermute | solution.py:341
  51.9 7.0 %collective-permute-start.19 = (f32[144,128]{1,0:T(8,128)S(1)}, f32[144,128]{1,0:T(8,128)S(1)}, u32[]{:S(2)}, u32[]{:S(2)}) collective-permute-start(f32[144,128]{1,0:T(8,128)S(1)} %get-tuple-element.125), channel_id=1, source_target_pairs={{0,28},{1,29},{2,6},{3,7},{4,0},{5,1},{6,2},{7,3},{8,4},{9,5},{10,... | collective-permute-start | bytes 221192 | tf_op jit(solution)/shard_map/ppermute | solution.py:341
  59.5 10.6 %collective-permute-start.22 = (f32[192,128]{1,0:T(8,128)S(1)}, f32[192,128]{1,0:T(8,128)S(1)}, u32[]{:S(2)}, u32[]{:S(2)}) collective-permute-start(f32[192,128]{1,0:T(8,128)S(1)} %get-tuple-element.133), channel_id=1, source_target_pairs={{0,30},{1,31},{2,4},{3,5},{4,2},{5,3},{6,8},{7,9},{8,6},{9,7},{10,... | collective-permute-start | bytes 294920 | tf_op jit(solution)/shard_map/ppermute | solution.py:341
  63.0 7.1 %collective-permute-start.24 = (f32[192,128]{1,0:T(8,128)S(1)}, f32[192,128]{1,0:T(8,128)S(1)}, u32[]{:S(2)}, u32[]{:S(2)}) collective-permute-start(f32[192,128]{1,0:T(8,128)S(1)} %get-tuple-element.135), channel_id=1, source_target_pairs={{0,2},{1,3},{2,0},{3,1},{4,6},{5,7},{6,4},{7,5},{8,10},{9,11},{10,... | collective-permute-start | bytes 294920 | tf_op jit(solution)/shard_map/ppermute | solution.py:341
  63.0 7.0 %collective-permute-start.21 = (f32[144,128]{1,0:T(8,128)S(1)}, f32[144,128]{1,0:T(8,128)S(1)}, u32[]{:S(2)}, u32[]{:S(2)}) collective-permute-start(f32[144,128]{1,0:T(8,128)S(1)} %get-tuple-element.132), channel_id=1, source_target_pairs={{0,4},{1,5},{2,30},{3,31},{4,8},{5,9},{6,10},{7,11},{8,12},{9,13},... | collective-permute-start | bytes 221192 | tf_op jit(solution)/shard_map/ppermute | solution.py:341
  63.6 6.4 %collective-permute-start.23 = (f32[144,128]{1,0:T(8,128)S(1)}, f32[144,128]{1,0:T(8,128)S(1)}, u32[]{:S(2)}, u32[]{:S(2)}) collective-permute-start(f32[144,128]{1,0:T(8,128)S(1)} %get-tuple-element.134), channel_id=1, source_target_pairs={{0,28},{1,29},{2,6},{3,7},{4,0},{5,1},{6,2},{7,3},{8,4},{9,5},{10,... | collective-permute-start | bytes 221192 | tf_op jit(solution)/shard_map/ppermute | solution.py:341
  70.6 11.4 %collective-permute-start.26 = (f32[192,128]{1,0:T(8,128)S(1)}, f32[192,128]{1,0:T(8,128)S(1)}, u32[]{:S(2)}, u32[]{:S(2)}) collective-permute-start(f32[192,128]{1,0:T(8,128)S(1)} %get-tuple-element.141), channel_id=1, source_target_pairs={{0,30},{1,31},{2,4},{3,5},{4,2},{5,3},{6,8},{7,9},{8,6},{9,7},{10,... | collective-permute-start | bytes 294920 | tf_op jit(solution)/shard_map/ppermute | solution.py:341
  74.9 7.1 %collective-permute-start.28 = (f32[192,128]{1,0:T(8,128)S(1)}, f32[192,128]{1,0:T(8,128)S(1)}, u32[]{:S(2)}, u32[]{:S(2)}) collective-permute-start(f32[192,128]{1,0:T(8,128)S(1)} %get-tuple-element.143), channel_id=1, source_target_pairs={{0,2},{1,3},{2,0},{3,1},{4,6},{5,7},{6,4},{7,5},{8,10},{9,11},{10,... | collective-permute-start | bytes 294920 | tf_op jit(solution)/shard_map/ppermute | solution.py:341
  74.9 7.0 %collective-permute-start.25 = (f32[144,128]{1,0:T(8,128)S(1)}, f32[144,128]{1,0:T(8,128)S(1)}, u32[]{:S(2)}, u32[]{:S(2)}) collective-permute-start(f32[144,128]{1,0:T(8,128)S(1)} %get-tuple-element.140), channel_id=1, source_target_pairs={{0,4},{1,5},{2,30},{3,31},{4,8},{5,9},{6,10},{7,11},{8,12},{9,13},... | collective-permute-start | bytes 221192 | tf_op jit(solution)/shard_map/ppermute | solution.py:341
  74.9 7.0 %collective-permute-start.27 = (f32[144,128]{1,0:T(8,128)S(1)}, f32[144,128]{1,0:T(8,128)S(1)}, u32[]{:S(2)}, u32[]{:S(2)}) collective-permute-start(f32[144,128]{1,0:T(8,128)S(1)} %get-tuple-element.142), channel_id=1, source_target_pairs={{0,28},{1,29},{2,6},{3,7},{4,0},{5,1},{6,2},{7,3},{8,4},{9,5},{10,... | collective-permute-start | bytes 221192 | tf_op jit(solution)/shard_map/ppermute | solution.py:341
  82.4 1.6 %collective-permute-start.29 = (f32[512,128]{1,0:T(8,128)S(1)}, f32[512,128]{1,0:T(8,128)S(1)}, u32[]{:S(2)}, u32[]{:S(2)}) collective-permute-start(f32[512,128]{1,0:T(8,128)S(1)} %shard_map.93), channel_id=1, source_target_pairs={{0,1},{1,0},{2,3},{3,2},{4,5},{5,4},{6,7},{7,6},{8,9},{9,8},{10,11... | collective-permute-start | bytes 786440 | tf_op jit(solution)/shard_map/ppermute | solution.py:111

commit v6 on v5

--- a/solution.py
+++ b/solution.py
@@ -132,12 +132,8 @@
 
 def pick_rows(onehot, x):
     half = x.shape[1]
-    high = x.astype(BF16)
-    rest = x - high.astype(F32)
-    mid = rest.astype(BF16)
-    low = (rest - mid.astype(F32)).astype(BF16)
-    got = dot(onehot, jnp.concatenate([high, mid, low], axis=1))
-    return got[:, :half] + (got[:, half : 2 * half] + got[:, 2 * half :])
+    got = dot(onehot, terms(x))
+    return got[:, :half] + got[:, half:]
 
 
 def on_each_side(body):
@@ -257,9 +253,7 @@
     for role in range(2):
         bases[role][...] = total[role]
         if not last:
-            got = dot(onehots[role][...], terms(total[role]))
-            half = got.shape[1] // 2
-            picks[role][...] = got[:, :half] + got[:, half:]
+            picks[role][...] = pick_rows(onehots[role][...], total[role])
 
 
 def payload_kernel(steps, *refs):

time: 85.1 us -> 84.9 us (level)
  no operation moved by 1% of the time
where the time goes in v6:
time: 84.9 us; the launch traced here: 84.7 us
  starting transfers between devices  50.7 us (60%)
  Pallas kernels  18.8 us (22%)
  waiting for transfers between devices  12.4 us (15%)
  local copies, waits for them, and re-layouts  2.4 us (3%)
    ppermute x24, starting transfers between devices, exchange(): arrived.append(lax.ppermute(piece, 'rows', pairs))  48.5 us
    pallas_call x23, Pallas kernels, call(): pl.pallas_call(kernel, out_shape=[jax.ShapeDtypeStruct(shape, dtype) for...  18.8 us
    ppermute x24, waiting for transfers between devices, exchange(): arrived.append(lax.ppermute(piece, 'rows', pairs))  8.26 us
    ppermute x6, waiting for transfers between devices, swap(): return lax.ppermute(x, 'rows', [(i, i ^ 1) for i in range(devices)])  4.12 us
    unnamed x14, local copies, waits for them, and re-layouts  2.4 us
    ppermute x6, starting transfers between devices, swap(): return lax.ppermute(x, 'rows', [(i, i ^ 1) for i in range(devices)])  2.17 us
  transfers between devices with their start and end apart: 30, of which 8 were waited for; matrix products, arithmetic and copies ran while one was open for 0% of the time, Pallas kernels for 17%

profile of v6, /device:TPU:0, one launch (start us, length us, event | category | flops | bytes accessed | tf_op | source)
XLA Modules:
  0.0 84.7 jit_solution(12374922091465915885)
XLA Ops:
  0.0 1.6 %copy-done = f32[4,8,128,128]{3,2,1,0:T(8,128)S(1)} copy-done((f32[4,8,128,128]{3,2,1,0:T(8,128)S(1)}, f32[4,8,128,128]{3,2,1,0:T(8,128)}, u32[]{:S(2)}) %copy-start) | copy-done | bytes 2097176
  1.6 0.7 copy-done.3
  2.3 0.9 %shard_map.78.total = f32[4,7,128,128]{3,2,1,0:T(8,128)S(1)} custom-call(s32[4,8]{1,0:T(4,128)S(1)} %copy-done.3, f32[4,8,128,128]{3,2,1,0:T(8,128)S(1)} %copy-done), custom_call_target="tpu_custom_call" | custom-call | flops 1000000000 | tf_op jit(solution)/shard_map/pallas_call | solution.py:22
  3.2 0.0 copy-start.5
  3.2 0.6 collective-permute-start.3
  3.8 0.1 copy-done.1
  3.9 0.9 %shard_map.75.total = f32[4,7,128,128]{3,2,1,0:T(8,128)S(1)} custom-call(s32[4,8]{1,0:T(4,128)S(1)} %copy-done.4, f32[4,8,128,128]{3,2,1,0:T(8,128)S(1)} %copy-done.1), custom_call_target="tpu_custom_call" | custom-call | flops 1000000000 | tf_op jit(solution)/shard_map/pallas_call | solution.py:22
  4.8 0.0 copy-start.6
  4.8 0.0 copy-start.2
  4.8 0.6 collective-permute-start.2
  5.4 0.1 collective-permute-start
  5.5 0.5 collective-permute-start.1
  6.0 0.4 collective-permute-start.4
  6.4 3.7 %collective-permute-done.1.rows_other = s32[8,48]{1,0:T(8,128)S(1)} collective-permute-done((s32[8,48]{1,0:T(8,128)S(1)}, s32[8,48]{1,0:T(8,128)S(1)}, u32[]{:S(2)}, u32[]{:S(2)}) %collective-permute-start.1) | collective-permute-done | bytes 1568 | tf_op jit(solution)/shard_map/ppermute | solution.py:111
  10.2 0.0 collective-permute-done.other.refs_7_
  10.2 0.5 shard_map.74
  10.7 2.9 %collective-permute-start.5 = (f32[144,128]{1,0:T(8,128)S(1)}, f32[144,128]{1,0:T(8,128)S(1)}, u32[]{:S(2)}, u32[]{:S(2)}) collective-permute-start(f32[144,128]{1,0:T(8,128)S(1)} %get-tuple-element.90), channel_id=1, source_target_pairs={{0,4},{1,5},{2,30},{3,31},{4,8},{5,9},{6,10},{7,11},{8,12},{9,13},... | collective-permute-start | bytes 221192 | tf_op jit(solution)/shard_map/ppermute | solution.py:335
  13.6 4.1 %collective-permute-start.6 = (f32[192,128]{1,0:T(8,128)S(1)}, f32[192,128]{1,0:T(8,128)S(1)}, u32[]{:S(2)}, u32[]{:S(2)}) collective-permute-start(f32[192,128]{1,0:T(8,128)S(1)} %get-tuple-element.91), channel_id=1, source_target_pairs={{0,30},{1,31},{2,4},{3,5},{4,2},{5,3},{6,8},{7,9},{8,6},{9,7},{10,... | collective-permute-start | bytes 294920 | tf_op jit(solution)/shard_map/ppermute | solution.py:335
  17.8 0.8 shard_map.76
  18.5 0.8 shard_map.79
  19.3 0.0 collective-permute-done.3.total
  19.3 0.5 collective-permute-start.8
  19.8 0.8 shard_map.80
  20.5 0.0 collective-permute-done.4.refs_5_
  20.6 1.7 %collective-permute-start.7 = (f32[144,128]{1,0:T(8,128)S(1)}, f32[144,128]{1,0:T(8,128)S(1)}, u32[]{:S(2)}, u32[]{:S(2)}) collective-permute-start(f32[144,128]{1,0:T(8,128)S(1)} %get-tuple-element.92), channel_id=1, source_target_pairs={{0,28},{1,29},{2,6},{3,7},{4,0},{5,1},{6,2},{7,3},{8,4},{9,5},{10,... | collective-permute-start | bytes 221192 | tf_op jit(solution)/shard_map/ppermute | solution.py:335
  22.3 1.0 %shard_map.82 = (f32[512,128]{1,0:T(8,128)S(1)}, f32[512,128]{1,0:T(8,128)S(1)}, f32[384,128]{1,0:T(8,128)S(1)}, f32[384,128]{1,0:T(8,128)S(1)}) custom-call(bf16[384,512]{1,0:T(8,128)(2,1)S(1)} %get-tuple-element.77.onehot.refs_0_, bf16[384,512]{1,0:T(8,128)(2,1)S(1)} %get-tuple-element.78.onehot.refs_1_, bf16[512,1024]{1,0:T(8,128)(2,1)S(1)} %get-tuple-element.81.refs_2_, ...), custom_call_target="tpu_custom_call" | custom-call | flops 1000000000 | tf_op jit(solution)/shard_map/pallas_call | solution.py:22
  23.3 0.0 collective-permute-done.5.refs_9_.refs_5_
  23.3 1.7 %collective-permute-done.7.refs_11_.refs_7_ = f32[144,128]{1,0:T(8,128)S(1)} collective-permute-done((f32[144,128]{1,0:T(8,128)S(1)}, f32[144,128]{1,0:T(8,128)S(1)}, u32[]{:S(2)}, u32[]{:S(2)}) %collective-permute-start.7) | collective-permute-done | bytes 73760 | tf_op jit(solution)/shard_map/ppermute | solution.py:335
  25.0 0.0 collective-permute-done.6.refs_10_.refs_6_
  25.0 0.0 collective-permute-done.8.refs_12_.refs_8_
  25.0 0.5 shard_map.84
  25.5 2.4 %collective-permute-start.9 = (f32[144,128]{1,0:T(8,128)S(1)}, f32[144,128]{1,0:T(8,128)S(1)}, u32[]{:S(2)}, u32[]{:S(2)}) collective-permute-start(f32[144,128]{1,0:T(8,128)S(1)} %get-tuple-element.103), channel_id=1, source_target_pairs={{0,4},{1,5},{2,30},{3,31},{4,8},{5,9},{6,10},{7,11},{8,12},{9,13},... | collective-permute-start | bytes 221192 | tf_op jit(solution)/shard_map/ppermute | solution.py:335
  27.9 3.4 %collective-permute-start.10 = (f32[192,128]{1,0:T(8,128)S(1)}, f32[192,128]{1,0:T(8,128)S(1)}, u32[]{:S(2)}, u32[]{:S(2)}) collective-permute-start(f32[192,128]{1,0:T(8,128)S(1)} %get-tuple-element.104), channel_id=1, source_target_pairs={{0,30},{1,31},{2,4},{3,5},{4,2},{5,3},{6,8},{7,9},{8,6},{9,7},{10,... | collective-permute-start | bytes 294920 | tf_op jit(solution)/shard_map/ppermute | solution.py:335
  31.3 0.8 shard_map.77
  32.1 1.5 %shard_map.83 = (f32[512,128]{1,0:T(8,128)S(1)}, f32[512,128]{1,0:T(8,128)S(1)}, f32[384,128]{1,0:T(8,128)S(1)}, f32[384,128]{1,0:T(8,128)S(1)}) custom-call(bf16[384,512]{1,0:T(8,128)(2,1)S(1)} %get-tuple-element.77.onehot.refs_0_, bf16[384,512]{1,0:T(8,128)(2,1)S(1)} %get-tuple-element.78.onehot.refs_1_, bf16[512,1024]{1,0:T(8,128)(2,1)S(1)} %get-tuple-element.79.refs_2_, ...), custom_call_target="tpu_custom_call" | custom-call | flops 1000000000 | tf_op jit(solution)/shard_map/pallas_call | solution.py:22
  33.6 3.1 %collective-permute-done.11.refs_13_.refs_7_ = f32[144,128]{1,0:T(8,128)S(1)} collective-permute-done((f32[144,128]{1,0:T(8,128)S(1)}, f32[144,128]{1,0:T(8,128)S(1)}, u32[]{:S(2)}, u32[]{:S(2)}) %collective-permute-start.11) | collective-permute-done | bytes 73760 | tf_op jit(solution)/shard_map/ppermute | solution.py:335
  36.7 0.7 shard_map.86
  37.4 2.9 %collective-permute-start.14 = (f32[192,128]{1,0:T(8,128)S(1)}, f32[192,128]{1,0:T(8,128)S(1)}, u32[]{:S(2)}, u32[]{:S(2)}) collective-permute-start(f32[192,128]{1,0:T(8,128)S(1)} %get-tuple-element.115), channel_id=1, source_target_pairs={{0,30},{1,31},{2,4},{3,5},{4,2},{5,3},{6,8},{7,9},{8,6},{9,7},{10,... | collective-permute-start | bytes 294920 | tf_op jit(solution)/shard_map/ppermute | solution.py:335
  40.4 0.3 collective-permute-start.13
  40.7 4.4 %collective-permute-start.15 = (f32[144,128]{1,0:T(8,128)S(1)}, f32[144,128]{1,0:T(8,128)S(1)}, u32[]{:S(2)}, u32[]{:S(2)}) collective-permute-start(f32[144,128]{1,0:T(8,128)S(1)} %get-tuple-element.116), channel_id=1, source_target_pairs={{0,28},{1,29},{2,6},{3,7},{4,0},{5,1},{6,2},{7,3},{8,4},{9,5},{10,... | collective-permute-start | bytes 221192 | tf_op jit(solution)/shard_map/ppermute | solution.py:335
  45.1 1.5 %shard_map.85 = (f32[512,128]{1,0:T(8,128)S(1)}, f32[512,128]{1,0:T(8,128)S(1)}, f32[384,128]{1,0:T(8,128)S(1)}, f32[384,128]{1,0:T(8,128)S(1)}) custom-call(bf16[384,512]{1,0:T(8,128)(2,1)S(1)} %get-tuple-element.77.onehot.refs_0_, bf16[384,512]{1,0:T(8,128)(2,1)S(1)} %get-tuple-element.78.onehot.refs_1_, bf16[512,1024]{1,0:T(8,128)(2,1)S(1)} %get-tuple-element.81.refs_2_, ...), custom_call_target="tpu_custom_call" | custom-call | flops 1000000000 | tf_op jit(solution)/shard_map/pallas_call | solution.py:22
  46.6 0.8 collective-permute-done.13.refs_9_.refs_5_
  47.4 0.5 shard_map.88
  47.9 3.8 %collective-permute-start.18 = (f32[192,128]{1,0:T(8,128)S(1)}, f32[192,128]{1,0:T(8,128)S(1)}, u32[]{:S(2)}, u32[]{:S(2)}) collective-permute-start(f32[192,128]{1,0:T(8,128)S(1)} %get-tuple-element.124), channel_id=1, source_target_pairs={{0,30},{1,31},{2,4},{3,5},{4,2},{5,3},{6,8},{7,9},{8,6},{9,7},{10,... | collective-permute-start | bytes 294920 | tf_op jit(solution)/shard_map/ppermute | solution.py:335
  51.8 4.7 %collective-permute-start.19 = (f32[144,128]{1,0:T(8,128)S(1)}, f32[144,128]{1,0:T(8,128)S(1)}, u32[]{:S(2)}, u32[]{:S(2)}) collective-permute-start(f32[144,128]{1,0:T(8,128)S(1)} %get-tuple-element.125), channel_id=1, source_target_pairs={{0,28},{1,29},{2,6},{3,7},{4,0},{5,1},{6,2},{7,3},{8,4},{9,5},{10,... | collective-permute-start | bytes 221192 | tf_op jit(solution)/shard_map/ppermute | solution.py:335
  56.5 1.5 %shard_map.87 = (f32[512,128]{1,0:T(8,128)S(1)}, f32[512,128]{1,0:T(8,128)S(1)}, f32[384,128]{1,0:T(8,128)S(1)}, f32[384,128]{1,0:T(8,128)S(1)}) custom-call(bf16[384,512]{1,0:T(8,128)(2,1)S(1)} %get-tuple-element.77.onehot.refs_0_, bf16[384,512]{1,0:T(8,128)(2,1)S(1)} %get-tuple-element.78.onehot.refs_1_, bf16[512,1024]{1,0:T(8,128)(2,1)S(1)} %get-tuple-element.79.refs_2_, ...), custom_call_target="tpu_custom_call" | custom-call | flops 1000000000 | tf_op jit(solution)/shard_map/pallas_call | solution.py:22
  58.0 0.8 collective-permute-done.17.refs_11_.refs_5_
  58.8 0.5 shard_map.90
  59.3 3.5 %collective-permute-start.22 = (f32[192,128]{1,0:T(8,128)S(1)}, f32[192,128]{1,0:T(8,128)S(1)}, u32[]{:S(2)}, u32[]{:S(2)}) collective-permute-start(f32[192,128]{1,0:T(8,128)S(1)} %get-tuple-element.133), channel_id=1, source_target_pairs={{0,30},{1,31},{2,4},{3,5},{4,2},{5,3},{6,8},{7,9},{8,6},{9,7},{10,... | collective-permute-start | bytes 294920 | tf_op jit(solution)/shard_map/ppermute | solution.py:335
  62.9 0.6 collective-permute-start.21
  63.5 4.1 %collective-permute-start.23 = (f32[144,128]{1,0:T(8,128)S(1)}, f32[144,128]{1,0:T(8,128)S(1)}, u32[]{:S(2)}, u32[]{:S(2)}) collective-permute-start(f32[144,128]{1,0:T(8,128)S(1)} %get-tuple-element.134), channel_id=1, source_target_pairs={{0,28},{1,29},{2,6},{3,7},{4,0},{5,1},{6,2},{7,3},{8,4},{9,5},{10,... | collective-permute-start | bytes 221192 | tf_op jit(solution)/shard_map/ppermute | solution.py:335
  67.6 1.5 %shard_map.89 = (f32[512,128]{1,0:T(8,128)S(1)}, f32[512,128]{1,0:T(8,128)S(1)}, f32[384,128]{1,0:T(8,128)S(1)}, f32[384,128]{1,0:T(8,128)S(1)}) custom-call(bf16[384,512]{1,0:T(8,128)(2,1)S(1)} %get-tuple-element.77.onehot.refs_0_, bf16[384,512]{1,0:T(8,128)(2,1)S(1)} %get-tuple-element.78.onehot.refs_1_, bf16[512,1024]{1,0:T(8,128)(2,1)S(1)} %get-tuple-element.81.refs_2_, ...), custom_call_target="tpu_custom_call" | custom-call | flops 1000000000 | tf_op jit(solution)/shard_map/pallas_call | solution.py:22
  69.1 0.8 collective-permute-done.21.refs_9_.refs_5_
  69.9 0.5 shard_map.92
  70.4 4.3 %collective-permute-start.26 = (f32[192,128]{1,0:T(8,128)S(1)}, f32[192,128]{1,0:T(8,128)S(1)}, u32[]{:S(2)}, u32[]{:S(2)}) collective-permute-start(f32[192,128]{1,0:T(8,128)S(1)} %get-tuple-element.141), channel_id=1, source_target_pairs={{0,30},{1,31},{2,4},{3,5},{4,2},{5,3},{6,8},{7,9},{8,6},{9,7},{10,... | collective-permute-start | bytes 294920 | tf_op jit(solution)/shard_map/ppermute | solution.py:335
  74.8 0.0 collective-permute-start.25
  74.8 4.7 %collective-permute-start.27 = (f32[144,128]{1,0:T(8,128)S(1)}, f32[144,128]{1,0:T(8,128)S(1)}, u32[]{:S(2)}, u32[]{:S(2)}) collective-permute-start(f32[144,128]{1,0:T(8,128)S(1)} %get-tuple-element.142), channel_id=1, source_target_pairs={{0,28},{1,29},{2,6},{3,7},{4,0},{5,1},{6,2},{7,3},{8,4},{9,5},{10,... | collective-permute-start | bytes 221192 | tf_op jit(solution)/shard_map/ppermute | solution.py:335
  79.5 1.2 %shard_map.91 = (f32[512,128]{1,0:T(8,128)S(1)}, f32[512,128]{1,0:T(8,128)S(1)}) custom-call(bf16[384,512]{1,0:T(8,128)(2,1)S(1)} %get-tuple-element.77.onehot.refs_0_, bf16[384,512]{1,0:T(8,128)(2,1)S(1)} %get-tuple-element.78.onehot.refs_1_, bf16[512,1024]{1,0:T(8,128)(2,1)S(1)} %get-tuple-element.79.refs_2_, ...), custom_call_target="tpu_custom_call" | custom-call | flops 1000000000 | tf_op jit(solution)/shard_map/pallas_call | solution.py:22
  80.7 1.1 %collective-permute-done.25.refs_1_ = f32[144,128]{1,0:T(8,128)S(1)} collective-permute-done((f32[144,128]{1,0:T(8,128)S(1)}, f32[144,128]{1,0:T(8,128)S(1)}, u32[]{:S(2)}, u32[]{:S(2)}) %collective-permute-start.25) | collective-permute-done | bytes 73760 | tf_op jit(solution)/shard_map/ppermute | solution.py:335
  81.8 0.4 shard_map.93
  82.3 0.1 collective-permute-start.29
  82.3 1.1 %shard_map.94.begun = f32[512,256]{1,0:T(8,128)} custom-call(f32[512,128]{1,0:T(8,128)S(1)} %get-tuple-element.144.base, bf16[512,768]{1,0:T(8,128)(2,1)S(1)} %get-tuple-element.96.refs_8_.far, f32[96,128]{1,0:T(8,128)S(1)} %get-tuple-element.139.refs_0_, f32[144,128]{1,0:T(8,128)S(1)} %collective-permute-done.25.refs_1_, ...), custom_call_target="tpu_custom_call" | custom-call | flops 1000000000 | tf_op jit(solution)/shard_map/pallas_call | solution.py:22
  83.5 0.4 collective-permute-done.29.got
  83.9 0.7 shard_map.95
  (33 shorter events, 0.1 us)
Async XLA Ops:
  0.0 1.6 %copy-start = (f32[4,8,128,128]{3,2,1,0:T(8,128)S(1)}, f32[4,8,128,128]{3,2,1,0:T(8,128)}, u32[]{:S(2)}) copy-start(f32[4,8,128,128]{3,2,1,0:T(8,128)} %tiles.3) | copy-start | bytes 6291460
  1.6 0.7 copy-start.3
  2.3 1.6 %copy-start.1 = (f32[4,8,128,128]{3,2,1,0:T(8,128)S(1)}, f32[4,8,128,128]{3,2,1,0:T(8,128)}, u32[]{:S(2)}) copy-start(f32[4,8,128,128]{3,2,1,0:T(8,128)} %tiles.2) | copy-start | bytes 6291460
  2.3 1.6 %copy-start.4 = (s32[4,8]{1,0:T(4,128)S(1)}, s32[4,8]{1,0:T(4,128)}, u32[]{:S(2)}) copy-start(s32[4,8]{1,0:T(4,128)} %columns.2) | copy-start | bytes 388
  3.2 2.2 %copy-start.5 = (f32[512,256]{1,0:T(8,128)S(1)}, f32[512,256]{1,0:T(8,128)}, u32[]{:S(2)}) copy-start(f32[512,256]{1,0:T(8,128)} %x.2) | copy-start | bytes 1572868
  3.2 16.1 %collective-permute-start.3 = (f32[4,7,128,128]{3,2,1,0:T(8,128)S(1)}, f32[4,7,128,128]{3,2,1,0:T(8,128)S(1)}, u32[]{:S(2)}, u32[]{:S(2)}) collective-permute-start(f32[4,7,128,128]{3,2,1,0:T(8,128)S(1)} %shard_map.78.total), channel_id=1, source_target_pairs={{0,1},{1,0},{2,3},{3,2},{4,5},{5,4},{6,7},{7,6},{8,9},{9,8},{10,11... | collective-permute-start | bytes 5505032 | tf_op jit(solution)/shard_map/ppermute | solution.py:111
  4.8 0.7 copy-start.6
  4.8 1.2 %copy-start.2 = (f32[512,256]{1,0:T(8,128)S(1)}, f32[512,256]{1,0:T(8,128)}, u32[]{:S(2)}) copy-start(f32[512,256]{1,0:T(8,128)} %x.3) | copy-start | bytes 1572868
  4.8 26.5 %collective-permute-start.2 = (f32[4,7,128,128]{3,2,1,0:T(8,128)S(1)}, f32[4,7,128,128]{3,2,1,0:T(8,128)S(1)}, u32[]{:S(2)}, u32[]{:S(2)}) collective-permute-start(f32[4,7,128,128]{3,2,1,0:T(8,128)S(1)} %shard_map.75.total), channel_id=1, source_target_pairs={{0,1},{1,0},{2,3},{3,2},{4,5},{5,4},{6,7},{7,6},{8,9},{9,8},{10,11... | collective-permute-start | bytes 5505032 | tf_op jit(solution)/shard_map/ppermute | solution.py:111
  5.4 4.8 %collective-permute-start = (f32[512,128]{1,0:T(8,128)S(1)}, f32[512,128]{1,0:T(8,128)S(1)}, u32[]{:S(2)}, u32[]{:S(2)}) collective-permute-start(f32[512,128]{1,0:T(8,128)S(1)} %get-tuple-element.76), channel_id=1, source_target_pairs={{0,1},{1,0},{2,3},{3,2},{4,5},{5,4},{6,7},{7,6},{8,9},{9,8},{10,11... | collective-permute-start | bytes 786440 | tf_op jit(solution)/shard_map/ppermute | solution.py:111
  5.5 4.7 %collective-permute-start.1 = (s32[8,48]{1,0:T(8,128)S(1)}, s32[8,48]{1,0:T(8,128)S(1)}, u32[]{:S(2)}, u32[]{:S(2)}) collective-permute-start(s32[8,48]{1,0:T(8,128)S(1)} %copy-done.6), channel_id=1, source_target_pairs={{0,1},{1,0},{2,3},{3,2},{4,5},{5,4},{6,7},{7,6},{8,9},{9,8},{10,11... | collective-permute-start | bytes 4616 | tf_op jit(solution)/shard_map/ppermute | solution.py:111
  6.0 14.5 %collective-permute-start.4 = (f32[512,128]{1,0:T(8,128)S(1)}, f32[512,128]{1,0:T(8,128)S(1)}, u32[]{:S(2)}, u32[]{:S(2)}) collective-permute-start(f32[512,128]{1,0:T(8,128)S(1)} %get-tuple-element.84), channel_id=1, source_target_pairs={{0,1},{1,0},{2,3},{3,2},{4,5},{5,4},{6,7},{7,6},{8,9},{9,8},{10,11... | collective-permute-start | bytes 786440 | tf_op jit(solution)/shard_map/ppermute | solution.py:111
  10.7 12.6 %collective-permute-start.5 = (f32[144,128]{1,0:T(8,128)S(1)}, f32[144,128]{1,0:T(8,128)S(1)}, u32[]{:S(2)}, u32[]{:S(2)}) collective-permute-start(f32[144,128]{1,0:T(8,128)S(1)} %get-tuple-element.90), channel_id=1, source_target_pairs={{0,4},{1,5},{2,30},{3,31},{4,8},{5,9},{6,10},{7,11},{8,12},{9,13},... | collective-permute-start | bytes 221192 | tf_op jit(solution)/shard_map/ppermute | solution.py:335
  13.6 11.3 %collective-permute-start.6 = (f32[192,128]{1,0:T(8,128)S(1)}, f32[192,128]{1,0:T(8,128)S(1)}, u32[]{:S(2)}, u32[]{:S(2)}) collective-permute-start(f32[192,128]{1,0:T(8,128)S(1)} %get-tuple-element.91), channel_id=1, source_target_pairs={{0,30},{1,31},{2,4},{3,5},{4,2},{5,3},{6,8},{7,9},{8,6},{9,7},{10,... | collective-permute-start | bytes 294920 | tf_op jit(solution)/shard_map/ppermute | solution.py:335
  19.3 5.6 %collective-permute-start.8 = (f32[192,128]{1,0:T(8,128)S(1)}, f32[192,128]{1,0:T(8,128)S(1)}, u32[]{:S(2)}, u32[]{:S(2)}) collective-permute-start(f32[192,128]{1,0:T(8,128)S(1)} %get-tuple-element.93), channel_id=1, source_target_pairs={{0,2},{1,3},{2,0},{3,1},{4,6},{5,7},{6,4},{7,5},{8,10},{9,11},{10,... | collective-permute-start | bytes 294920 | tf_op jit(solution)/shard_map/ppermute | solution.py:335
  20.6 4.4 %collective-permute-start.7 = (f32[144,128]{1,0:T(8,128)S(1)}, f32[144,128]{1,0:T(8,128)S(1)}, u32[]{:S(2)}, u32[]{:S(2)}) collective-permute-start(f32[144,128]{1,0:T(8,128)S(1)} %get-tuple-element.92), channel_id=1, source_target_pairs={{0,28},{1,29},{2,6},{3,7},{4,0},{5,1},{6,2},{7,3},{8,4},{9,5},{10,... | collective-permute-start | bytes 221192 | tf_op jit(solution)/shard_map/ppermute | solution.py:335
  25.5 8.2 %collective-permute-start.9 = (f32[144,128]{1,0:T(8,128)S(1)}, f32[144,128]{1,0:T(8,128)S(1)}, u32[]{:S(2)}, u32[]{:S(2)}) collective-permute-start(f32[144,128]{1,0:T(8,128)S(1)} %get-tuple-element.103), channel_id=1, source_target_pairs={{0,4},{1,5},{2,30},{3,31},{4,8},{5,9},{6,10},{7,11},{8,12},{9,13},... | collective-permute-start | bytes 221192 | tf_op jit(solution)/shard_map/ppermute | solution.py:335
  27.9 8.8 %collective-permute-start.10 = (f32[192,128]{1,0:T(8,128)S(1)}, f32[192,128]{1,0:T(8,128)S(1)}, u32[]{:S(2)}, u32[]{:S(2)}) collective-permute-start(f32[192,128]{1,0:T(8,128)S(1)} %get-tuple-element.104), channel_id=1, source_target_pairs={{0,30},{1,31},{2,4},{3,5},{4,2},{5,3},{6,8},{7,9},{8,6},{9,7},{10,... | collective-permute-start | bytes 294920 | tf_op jit(solution)/shard_map/ppermute | solution.py:335
  31.3 5.4 %collective-permute-start.11 = (f32[144,128]{1,0:T(8,128)S(1)}, f32[144,128]{1,0:T(8,128)S(1)}, u32[]{:S(2)}, u32[]{:S(2)}) collective-permute-start(f32[144,128]{1,0:T(8,128)S(1)} %get-tuple-element.105), channel_id=1, source_target_pairs={{0,28},{1,29},{2,6},{3,7},{4,0},{5,1},{6,2},{7,3},{8,4},{9,5},{10,... | collective-permute-start | bytes 221192 | tf_op jit(solution)/shard_map/ppermute | solution.py:335
  31.3 5.4 %collective-permute-start.12 = (f32[192,128]{1,0:T(8,128)S(1)}, f32[192,128]{1,0:T(8,128)S(1)}, u32[]{:S(2)}, u32[]{:S(2)}) collective-permute-start(f32[192,128]{1,0:T(8,128)S(1)} %get-tuple-element.106), channel_id=1, source_target_pairs={{0,2},{1,3},{2,0},{3,1},{4,6},{5,7},{6,4},{7,5},{8,10},{9,11},{10,... | collective-permute-start | bytes 294920 | tf_op jit(solution)/shard_map/ppermute | solution.py:335
  37.4 10.0 %collective-permute-start.14 = (f32[192,128]{1,0:T(8,128)S(1)}, f32[192,128]{1,0:T(8,128)S(1)}, u32[]{:S(2)}, u32[]{:S(2)}) collective-permute-start(f32[192,128]{1,0:T(8,128)S(1)} %get-tuple-element.115), channel_id=1, source_target_pairs={{0,30},{1,31},{2,4},{3,5},{4,2},{5,3},{6,8},{7,9},{8,6},{9,7},{10,... | collective-permute-start | bytes 294920 | tf_op jit(solution)/shard_map/ppermute | solution.py:335
  40.4 7.1 %collective-permute-start.16 = (f32[192,128]{1,0:T(8,128)S(1)}, f32[192,128]{1,0:T(8,128)S(1)}, u32[]{:S(2)}, u32[]{:S(2)}) collective-permute-start(f32[192,128]{1,0:T(8,128)S(1)} %get-tuple-element.117), channel_id=1, source_target_pairs={{0,2},{1,3},{2,0},{3,1},{4,6},{5,7},{6,4},{7,5},{8,10},{9,11},{10,... | collective-permute-start | bytes 294920 | tf_op jit(solution)/shard_map/ppermute | solution.py:335
  40.4 7.0 %collective-permute-start.13 = (f32[144,128]{1,0:T(8,128)S(1)}, f32[144,128]{1,0:T(8,128)S(1)}, u32[]{:S(2)}, u32[]{:S(2)}) collective-permute-start(f32[144,128]{1,0:T(8,128)S(1)} %get-tuple-element.114), channel_id=1, source_target_pairs={{0,4},{1,5},{2,30},{3,31},{4,8},{5,9},{6,10},{7,11},{8,12},{9,13},... | collective-permute-start | bytes 221192 | tf_op jit(solution)/shard_map/ppermute | solution.py:335
  40.7 6.8 %collective-permute-start.15 = (f32[144,128]{1,0:T(8,128)S(1)}, f32[144,128]{1,0:T(8,128)S(1)}, u32[]{:S(2)}, u32[]{:S(2)}) collective-permute-start(f32[144,128]{1,0:T(8,128)S(1)} %get-tuple-element.116), channel_id=1, source_target_pairs={{0,28},{1,29},{2,6},{3,7},{4,0},{5,1},{6,2},{7,3},{8,4},{9,5},{10,... | collective-permute-start | bytes 221192 | tf_op jit(solution)/shard_map/ppermute | solution.py:335
  47.9 10.9 %collective-permute-start.18 = (f32[192,128]{1,0:T(8,128)S(1)}, f32[192,128]{1,0:T(8,128)S(1)}, u32[]{:S(2)}, u32[]{:S(2)}) collective-permute-start(f32[192,128]{1,0:T(8,128)S(1)} %get-tuple-element.124), channel_id=1, source_target_pairs={{0,30},{1,31},{2,4},{3,5},{4,2},{5,3},{6,8},{7,9},{8,6},{9,7},{10,... | collective-permute-start | bytes 294920 | tf_op jit(solution)/shard_map/ppermute | solution.py:335
  51.7 7.1 %collective-permute-start.20 = (f32[192,128]{1,0:T(8,128)S(1)}, f32[192,128]{1,0:T(8,128)S(1)}, u32[]{:S(2)}, u32[]{:S(2)}) collective-permute-start(f32[192,128]{1,0:T(8,128)S(1)} %get-tuple-element.126), channel_id=1, source_target_pairs={{0,2},{1,3},{2,0},{3,1},{4,6},{5,7},{6,4},{7,5},{8,10},{9,11},{10,... | collective-permute-start | bytes 294920 | tf_op jit(solution)/shard_map/ppermute | solution.py:335
  51.7 7.0 %collective-permute-start.17 = (f32[144,128]{1,0:T(8,128)S(1)}, f32[144,128]{1,0:T(8,128)S(1)}, u32[]{:S(2)}, u32[]{:S(2)}) collective-permute-start(f32[144,128]{1,0:T(8,128)S(1)} %get-tuple-element.123), channel_id=1, source_target_pairs={{0,4},{1,5},{2,30},{3,31},{4,8},{5,9},{6,10},{7,11},{8,12},{9,13},... | collective-permute-start | bytes 221192 | tf_op jit(solution)/shard_map/ppermute | solution.py:335
  51.8 7.0 %collective-permute-start.19 = (f32[144,128]{1,0:T(8,128)S(1)}, f32[144,128]{1,0:T(8,128)S(1)}, u32[]{:S(2)}, u32[]{:S(2)}) collective-permute-start(f32[144,128]{1,0:T(8,128)S(1)} %get-tuple-element.125), channel_id=1, source_target_pairs={{0,28},{1,29},{2,6},{3,7},{4,0},{5,1},{6,2},{7,3},{8,4},{9,5},{10,... | collective-permute-start | bytes 221192 | tf_op jit(solution)/shard_map/ppermute | solution.py:335
  59.3 10.6 %collective-permute-start.22 = (f32[192,128]{1,0:T(8,128)S(1)}, f32[192,128]{1,0:T(8,128)S(1)}, u32[]{:S(2)}, u32[]{:S(2)}) collective-permute-start(f32[192,128]{1,0:T(8,128)S(1)} %get-tuple-element.133), channel_id=1, source_target_pairs={{0,30},{1,31},{2,4},{3,5},{4,2},{5,3},{6,8},{7,9},{8,6},{9,7},{10,... | collective-permute-start | bytes 294920 | tf_op jit(solution)/shard_map/ppermute | solution.py:335
  62.8 7.1 %collective-permute-start.24 = (f32[192,128]{1,0:T(8,128)S(1)}, f32[192,128]{1,0:T(8,128)S(1)}, u32[]{:S(2)}, u32[]{:S(2)}) collective-permute-start(f32[192,128]{1,0:T(8,128)S(1)} %get-tuple-element.135), channel_id=1, source_target_pairs={{0,2},{1,3},{2,0},{3,1},{4,6},{5,7},{6,4},{7,5},{8,10},{9,11},{10,... | collective-permute-start | bytes 294920 | tf_op jit(solution)/shard_map/ppermute | solution.py:335
  62.9 7.0 %collective-permute-start.21 = (f32[144,128]{1,0:T(8,128)S(1)}, f32[144,128]{1,0:T(8,128)S(1)}, u32[]{:S(2)}, u32[]{:S(2)}) collective-permute-start(f32[144,128]{1,0:T(8,128)S(1)} %get-tuple-element.132), channel_id=1, source_target_pairs={{0,4},{1,5},{2,30},{3,31},{4,8},{5,9},{6,10},{7,11},{8,12},{9,13},... | collective-permute-start | bytes 221192 | tf_op jit(solution)/shard_map/ppermute | solution.py:335
  63.5 6.4 %collective-permute-start.23 = (f32[144,128]{1,0:T(8,128)S(1)}, f32[144,128]{1,0:T(8,128)S(1)}, u32[]{:S(2)}, u32[]{:S(2)}) collective-permute-start(f32[144,128]{1,0:T(8,128)S(1)} %get-tuple-element.134), channel_id=1, source_target_pairs={{0,28},{1,29},{2,6},{3,7},{4,0},{5,1},{6,2},{7,3},{8,4},{9,5},{10,... | collective-permute-start | bytes 221192 | tf_op jit(solution)/shard_map/ppermute | solution.py:335
  70.4 11.4 %collective-permute-start.26 = (f32[192,128]{1,0:T(8,128)S(1)}, f32[192,128]{1,0:T(8,128)S(1)}, u32[]{:S(2)}, u32[]{:S(2)}) collective-permute-start(f32[192,128]{1,0:T(8,128)S(1)} %get-tuple-element.141), channel_id=1, source_target_pairs={{0,30},{1,31},{2,4},{3,5},{4,2},{5,3},{6,8},{7,9},{8,6},{9,7},{10,... | collective-permute-start | bytes 294920 | tf_op jit(solution)/shard_map/ppermute | solution.py:335
  74.8 7.1 %collective-permute-start.28 = (f32[192,128]{1,0:T(8,128)S(1)}, f32[192,128]{1,0:T(8,128)S(1)}, u32[]{:S(2)}, u32[]{:S(2)}) collective-permute-start(f32[192,128]{1,0:T(8,128)S(1)} %get-tuple-element.143), channel_id=1, source_target_pairs={{0,2},{1,3},{2,0},{3,1},{4,6},{5,7},{6,4},{7,5},{8,10},{9,11},{10,... | collective-permute-start | bytes 294920 | tf_op jit(solution)/shard_map/ppermute | solution.py:335
  74.8 7.0 %collective-permute-start.25 = (f32[144,128]{1,0:T(8,128)S(1)}, f32[144,128]{1,0:T(8,128)S(1)}, u32[]{:S(2)}, u32[]{:S(2)}) collective-permute-start(f32[144,128]{1,0:T(8,128)S(1)} %get-tuple-element.140), channel_id=1, source_target_pairs={{0,4},{1,5},{2,30},{3,31},{4,8},{5,9},{6,10},{7,11},{8,12},{9,13},... | collective-permute-start | bytes 221192 | tf_op jit(solution)/shard_map/ppermute | solution.py:335
  74.8 7.0 %collective-permute-start.27 = (f32[144,128]{1,0:T(8,128)S(1)}, f32[144,128]{1,0:T(8,128)S(1)}, u32[]{:S(2)}, u32[]{:S(2)}) collective-permute-start(f32[144,128]{1,0:T(8,128)S(1)} %get-tuple-element.142), channel_id=1, source_target_pairs={{0,28},{1,29},{2,6},{3,7},{4,0},{5,1},{6,2},{7,3},{8,4},{9,5},{10,... | collective-permute-start | bytes 221192 | tf_op jit(solution)/shard_map/ppermute | solution.py:335
  82.3 1.6 %collective-permute-start.29 = (f32[512,128]{1,0:T(8,128)S(1)}, f32[512,128]{1,0:T(8,128)S(1)}, u32[]{:S(2)}, u32[]{:S(2)}) collective-permute-start(f32[512,128]{1,0:T(8,128)S(1)} %shard_map.93), channel_id=1, source_target_pairs={{0,1},{1,0},{2,3},{3,2},{4,5},{5,4},{6,7},{7,6},{8,9},{9,8},{10,11... | collective-permute-start | bytes 786440 | tf_op jit(solution)/shard_map/ppermute | solution.py:111

commit v7 on v6

--- a/solution.py
+++ b/solution.py
@@ -181,14 +181,18 @@
 
 def split_kernel(total, onehot, own, far, out):
     blocks, columns, size, _ = total.shape
-    for block in range(blocks):
-        at = slice(block * size, (block + 1) * size)
-        for column in range(columns):
-            to = own if column < blocks else far
-            place = (column if column < blocks else column - blocks) * size
-            low_place = place + to.shape[1] // 2
-            to[at, place : place + size], to[at, low_place : low_place + size] = split2(total[block, column])
+
+    def put(to, first, last):
+        for block in range(blocks):
+            at = slice(block * size, (block + 1) * size)
+            for column in range(first, last):
+                place = (column - first) * size
+                low_place = place + to.shape[1] // 2
+                to[at, place : place + size], to[at, low_place : low_place + size] = split2(total[block, column])
+
+    put(far, blocks, columns)
     out[...] = dot(onehot[...], far[...]).astype(BF16)
+    put(own, 0, blocks)
 
 
 def deal(steps, lists, outs, pair=None):

time: 84.9 us -> 84.6 us (level)
  no operation moved by 1% of the time
where the time goes in v7:
time: 84.6 us; the launch traced here: 84.4 us
  starting transfers between devices  50.7 us (60%)
  Pallas kernels  18.4 us (22%)
  waiting for transfers between devices  12.4 us (15%)
  local copies, waits for them, and re-layouts  2.4 us (3%)
    ppermute x24, starting transfers between devices, exchange(): arrived.append(lax.ppermute(piece, 'rows', pairs))  48.5 us
    pallas_call x23, Pallas kernels, call(): pl.pallas_call(kernel, out_shape=[jax.ShapeDtypeStruct(shape, dtype) for...  18.4 us
    ppermute x24, waiting for transfers between devices, exchange(): arrived.append(lax.ppermute(piece, 'rows', pairs))  8.32 us
    ppermute x6, waiting for transfers between devices, swap(): return lax.ppermute(x, 'rows', [(i, i ^ 1) for i in range(devices)])  4.11 us
    unnamed x14, local copies, waits for them, and re-layouts  2.4 us
    ppermute x6, starting transfers between devices, swap(): return lax.ppermute(x, 'rows', [(i, i ^ 1) for i in range(devices)])  2.17 us
  transfers between devices with their start and end apart: 30, of which 8 were waited for; matrix products, arithmetic and copies ran while one was open for 0% of the time, Pallas kernels for 17%

profile of v7, /device:TPU:0, one launch (start us, length us, event | category | flops | bytes accessed | tf_op | source)
XLA Modules:
  0.0 84.4 jit_solution(11084442341499213808)
XLA Ops:
  0.0 1.6 %copy-done = f32[4,8,128,128]{3,2,1,0:T(8,128)S(1)} copy-done((f32[4,8,128,128]{3,2,1,0:T(8,128)S(1)}, f32[4,8,128,128]{3,2,1,0:T(8,128)}, u32[]{:S(2)}) %copy-start) | copy-done | bytes 2097176
  1.6 0.7 copy-done.3
  2.3 0.9 %shard_map.78.total = f32[4,7,128,128]{3,2,1,0:T(8,128)S(1)} custom-call(s32[4,8]{1,0:T(4,128)S(1)} %copy-done.3, f32[4,8,128,128]{3,2,1,0:T(8,128)S(1)} %copy-done), custom_call_target="tpu_custom_call" | custom-call | flops 1000000000 | tf_op jit(solution)/shard_map/pallas_call | solution.py:22
  3.2 0.0 copy-start.5
  3.2 0.6 collective-permute-start.3
  3.8 0.1 copy-done.1
  3.9 0.9 %shard_map.75.total = f32[4,7,128,128]{3,2,1,0:T(8,128)S(1)} custom-call(s32[4,8]{1,0:T(4,128)S(1)} %copy-done.4, f32[4,8,128,128]{3,2,1,0:T(8,128)S(1)} %copy-done.1), custom_call_target="tpu_custom_call" | custom-call | flops 1000000000 | tf_op jit(solution)/shard_map/pallas_call | solution.py:22
  4.8 0.0 copy-start.6
  4.8 0.0 copy-start.2
  4.8 0.6 collective-permute-start.2
  5.4 0.1 collective-permute-start
  5.5 0.5 collective-permute-start.1
  6.0 0.4 collective-permute-start.4
  6.4 3.7 %collective-permute-done.1.rows_other = s32[8,48]{1,0:T(8,128)S(1)} collective-permute-done((s32[8,48]{1,0:T(8,128)S(1)}, s32[8,48]{1,0:T(8,128)S(1)}, u32[]{:S(2)}, u32[]{:S(2)}) %collective-permute-start.1) | collective-permute-done | bytes 1568 | tf_op jit(solution)/shard_map/ppermute | solution.py:111
  10.2 0.0 collective-permute-done.other.refs_7_
  10.2 0.5 shard_map.74
  10.7 2.9 %collective-permute-start.5 = (f32[144,128]{1,0:T(8,128)S(1)}, f32[144,128]{1,0:T(8,128)S(1)}, u32[]{:S(2)}, u32[]{:S(2)}) collective-permute-start(f32[144,128]{1,0:T(8,128)S(1)} %get-tuple-element.90), channel_id=1, source_target_pairs={{0,4},{1,5},{2,30},{3,31},{4,8},{5,9},{6,10},{7,11},{8,12},{9,13},... | collective-permute-start | bytes 221192 | tf_op jit(solution)/shard_map/ppermute | solution.py:339
  13.6 4.1 %collective-permute-start.6 = (f32[192,128]{1,0:T(8,128)S(1)}, f32[192,128]{1,0:T(8,128)S(1)}, u32[]{:S(2)}, u32[]{:S(2)}) collective-permute-start(f32[192,128]{1,0:T(8,128)S(1)} %get-tuple-element.91), channel_id=1, source_target_pairs={{0,30},{1,31},{2,4},{3,5},{4,2},{5,3},{6,8},{7,9},{8,6},{9,7},{10,... | collective-permute-start | bytes 294920 | tf_op jit(solution)/shard_map/ppermute | solution.py:339
  17.8 0.7 shard_map.76
  18.5 0.7 shard_map.79
  19.2 0.5 collective-permute-start.8
  19.7 0.7 shard_map.80
  20.4 1.7 %collective-permute-start.7 = (f32[144,128]{1,0:T(8,128)S(1)}, f32[144,128]{1,0:T(8,128)S(1)}, u32[]{:S(2)}, u32[]{:S(2)}) collective-permute-start(f32[144,128]{1,0:T(8,128)S(1)} %get-tuple-element.92), channel_id=1, source_target_pairs={{0,28},{1,29},{2,6},{3,7},{4,0},{5,1},{6,2},{7,3},{8,4},{9,5},{10,... | collective-permute-start | bytes 221192 | tf_op jit(solution)/shard_map/ppermute | solution.py:339
  22.1 1.0 %shard_map.82 = (f32[512,128]{1,0:T(8,128)S(1)}, f32[512,128]{1,0:T(8,128)S(1)}, f32[384,128]{1,0:T(8,128)S(1)}, f32[384,128]{1,0:T(8,128)S(1)}) custom-call(bf16[384,512]{1,0:T(8,128)(2,1)S(1)} %get-tuple-element.77.onehot.refs_0_, bf16[384,512]{1,0:T(8,128)(2,1)S(1)} %get-tuple-element.78.onehot.refs_1_, bf16[512,1024]{1,0:T(8,128)(2,1)S(1)} %get-tuple-element.81.refs_2_, ...), custom_call_target="tpu_custom_call" | custom-call | flops 1000000000 | tf_op jit(solution)/shard_map/pallas_call | solution.py:22
  23.1 1.7 %collective-permute-done.7.refs_11_.refs_7_ = f32[144,128]{1,0:T(8,128)S(1)} collective-permute-done((f32[144,128]{1,0:T(8,128)S(1)}, f32[144,128]{1,0:T(8,128)S(1)}, u32[]{:S(2)}, u32[]{:S(2)}) %collective-permute-start.7) | collective-permute-done | bytes 73760 | tf_op jit(solution)/shard_map/ppermute | solution.py:339
  24.8 0.5 shard_map.84
  25.3 2.4 %collective-permute-start.9 = (f32[144,128]{1,0:T(8,128)S(1)}, f32[144,128]{1,0:T(8,128)S(1)}, u32[]{:S(2)}, u32[]{:S(2)}) collective-permute-start(f32[144,128]{1,0:T(8,128)S(1)} %get-tuple-element.103), channel_id=1, source_target_pairs={{0,4},{1,5},{2,30},{3,31},{4,8},{5,9},{6,10},{7,11},{8,12},{9,13},... | collective-permute-start | bytes 221192 | tf_op jit(solution)/shard_map/ppermute | solution.py:339
  27.7 3.4 %collective-permute-start.10 = (f32[192,128]{1,0:T(8,128)S(1)}, f32[192,128]{1,0:T(8,128)S(1)}, u32[]{:S(2)}, u32[]{:S(2)}) collective-permute-start(f32[192,128]{1,0:T(8,128)S(1)} %get-tuple-element.104), channel_id=1, source_target_pairs={{0,30},{1,31},{2,4},{3,5},{4,2},{5,3},{6,8},{7,9},{8,6},{9,7},{10,... | collective-permute-start | bytes 294920 | tf_op jit(solution)/shard_map/ppermute | solution.py:339
  31.1 0.0 collective-permute-start.11
  31.1 0.0 collective-permute-start.12
  31.2 0.0 collective-permute-done.2.total
  31.2 0.7 shard_map.77
  31.9 1.5 %shard_map.83 = (f32[512,128]{1,0:T(8,128)S(1)}, f32[512,128]{1,0:T(8,128)S(1)}, f32[384,128]{1,0:T(8,128)S(1)}, f32[384,128]{1,0:T(8,128)S(1)}) custom-call(bf16[384,512]{1,0:T(8,128)(2,1)S(1)} %get-tuple-element.77.onehot.refs_0_, bf16[384,512]{1,0:T(8,128)(2,1)S(1)} %get-tuple-element.78.onehot.refs_1_, bf16[512,1024]{1,0:T(8,128)(2,1)S(1)} %get-tuple-element.79.refs_2_, ...), custom_call_target="tpu_custom_call" | custom-call | flops 1000000000 | tf_op jit(solution)/shard_map/pallas_call | solution.py:22
  33.4 3.1 %collective-permute-done.11.refs_13_.refs_7_ = f32[144,128]{1,0:T(8,128)S(1)} collective-permute-done((f32[144,128]{1,0:T(8,128)S(1)}, f32[144,128]{1,0:T(8,128)S(1)}, u32[]{:S(2)}, u32[]{:S(2)}) %collective-permute-start.11) | collective-permute-done | bytes 73760 | tf_op jit(solution)/shard_map/ppermute | solution.py:339
  36.6 0.0 collective-permute-done.12.refs_14_.refs_8_
  36.6 0.5 shard_map.86
  37.1 2.9 %collective-permute-start.14 = (f32[192,128]{1,0:T(8,128)S(1)}, f32[192,128]{1,0:T(8,128)S(1)}, u32[]{:S(2)}, u32[]{:S(2)}) collective-permute-start(f32[192,128]{1,0:T(8,128)S(1)} %get-tuple-element.115), channel_id=1, source_target_pairs={{0,30},{1,31},{2,4},{3,5},{4,2},{5,3},{6,8},{7,9},{8,6},{9,7},{10,... | collective-permute-start | bytes 294920 | tf_op jit(solution)/shard_map/ppermute | solution.py:339
  40.0 0.0 collective-permute-start.16
  40.0 0.5 collective-permute-start.13
  40.5 4.3 %collective-permute-start.15 = (f32[144,128]{1,0:T(8,128)S(1)}, f32[144,128]{1,0:T(8,128)S(1)}, u32[]{:S(2)}, u32[]{:S(2)}) collective-permute-start(f32[144,128]{1,0:T(8,128)S(1)} %get-tuple-element.116), channel_id=1, source_target_pairs={{0,28},{1,29},{2,6},{3,7},{4,0},{5,1},{6,2},{7,3},{8,4},{9,5},{10,... | collective-permute-start | bytes 221192 | tf_op jit(solution)/shard_map/ppermute | solution.py:339
  44.7 1.5 %shard_map.85 = (f32[512,128]{1,0:T(8,128)S(1)}, f32[512,128]{1,0:T(8,128)S(1)}, f32[384,128]{1,0:T(8,128)S(1)}, f32[384,128]{1,0:T(8,128)S(1)}) custom-call(bf16[384,512]{1,0:T(8,128)(2,1)S(1)} %get-tuple-element.77.onehot.refs_0_, bf16[384,512]{1,0:T(8,128)(2,1)S(1)} %get-tuple-element.78.onehot.refs_1_, bf16[512,1024]{1,0:T(8,128)(2,1)S(1)} %get-tuple-element.81.refs_2_, ...), custom_call_target="tpu_custom_call" | custom-call | flops 1000000000 | tf_op jit(solution)/shard_map/pallas_call | solution.py:22
  46.3 0.8 collective-permute-done.13.refs_9_.refs_5_
  47.1 0.5 shard_map.88
  47.6 3.8 %collective-permute-start.18 = (f32[192,128]{1,0:T(8,128)S(1)}, f32[192,128]{1,0:T(8,128)S(1)}, u32[]{:S(2)}, u32[]{:S(2)}) collective-permute-start(f32[192,128]{1,0:T(8,128)S(1)} %get-tuple-element.124), channel_id=1, source_target_pairs={{0,30},{1,31},{2,4},{3,5},{4,2},{5,3},{6,8},{7,9},{8,6},{9,7},{10,... | collective-permute-start | bytes 294920 | tf_op jit(solution)/shard_map/ppermute | solution.py:339
  51.4 4.7 %collective-permute-start.19 = (f32[144,128]{1,0:T(8,128)S(1)}, f32[144,128]{1,0:T(8,128)S(1)}, u32[]{:S(2)}, u32[]{:S(2)}) collective-permute-start(f32[144,128]{1,0:T(8,128)S(1)} %get-tuple-element.125), channel_id=1, source_target_pairs={{0,28},{1,29},{2,6},{3,7},{4,0},{5,1},{6,2},{7,3},{8,4},{9,5},{10,... | collective-permute-start | bytes 221192 | tf_op jit(solution)/shard_map/ppermute | solution.py:339
  56.1 1.5 %shard_map.87 = (f32[512,128]{1,0:T(8,128)S(1)}, f32[512,128]{1,0:T(8,128)S(1)}, f32[384,128]{1,0:T(8,128)S(1)}, f32[384,128]{1,0:T(8,128)S(1)}) custom-call(bf16[384,512]{1,0:T(8,128)(2,1)S(1)} %get-tuple-element.77.onehot.refs_0_, bf16[384,512]{1,0:T(8,128)(2,1)S(1)} %get-tuple-element.78.onehot.refs_1_, bf16[512,1024]{1,0:T(8,128)(2,1)S(1)} %get-tuple-element.79.refs_2_, ...), custom_call_target="tpu_custom_call" | custom-call | flops 1000000000 | tf_op jit(solution)/shard_map/pallas_call | solution.py:22
  57.7 0.8 collective-permute-done.17.refs_11_.refs_5_
  58.5 0.5 shard_map.90
  59.0 3.5 %collective-permute-start.22 = (f32[192,128]{1,0:T(8,128)S(1)}, f32[192,128]{1,0:T(8,128)S(1)}, u32[]{:S(2)}, u32[]{:S(2)}) collective-permute-start(f32[192,128]{1,0:T(8,128)S(1)} %get-tuple-element.133), channel_id=1, source_target_pairs={{0,30},{1,31},{2,4},{3,5},{4,2},{5,3},{6,8},{7,9},{8,6},{9,7},{10,... | collective-permute-start | bytes 294920 | tf_op jit(solution)/shard_map/ppermute | solution.py:339
  62.5 0.6 collective-permute-start.21
  63.1 4.1 %collective-permute-start.23 = (f32[144,128]{1,0:T(8,128)S(1)}, f32[144,128]{1,0:T(8,128)S(1)}, u32[]{:S(2)}, u32[]{:S(2)}) collective-permute-start(f32[144,128]{1,0:T(8,128)S(1)} %get-tuple-element.134), channel_id=1, source_target_pairs={{0,28},{1,29},{2,6},{3,7},{4,0},{5,1},{6,2},{7,3},{8,4},{9,5},{10,... | collective-permute-start | bytes 221192 | tf_op jit(solution)/shard_map/ppermute | solution.py:339
  67.2 1.5 %shard_map.89 = (f32[512,128]{1,0:T(8,128)S(1)}, f32[512,128]{1,0:T(8,128)S(1)}, f32[384,128]{1,0:T(8,128)S(1)}, f32[384,128]{1,0:T(8,128)S(1)}) custom-call(bf16[384,512]{1,0:T(8,128)(2,1)S(1)} %get-tuple-element.77.onehot.refs_0_, bf16[384,512]{1,0:T(8,128)(2,1)S(1)} %get-tuple-element.78.onehot.refs_1_, bf16[512,1024]{1,0:T(8,128)(2,1)S(1)} %get-tuple-element.81.refs_2_, ...), custom_call_target="tpu_custom_call" | custom-call | flops 1000000000 | tf_op jit(solution)/shard_map/pallas_call | solution.py:22
  68.8 0.8 collective-permute-done.21.refs_9_.refs_5_
  69.6 0.5 shard_map.92
  70.1 4.3 %collective-permute-start.26 = (f32[192,128]{1,0:T(8,128)S(1)}, f32[192,128]{1,0:T(8,128)S(1)}, u32[]{:S(2)}, u32[]{:S(2)}) collective-permute-start(f32[192,128]{1,0:T(8,128)S(1)} %get-tuple-element.141), channel_id=1, source_target_pairs={{0,30},{1,31},{2,4},{3,5},{4,2},{5,3},{6,8},{7,9},{8,6},{9,7},{10,... | collective-permute-start | bytes 294920 | tf_op jit(solution)/shard_map/ppermute | solution.py:339
  74.4 0.0 collective-permute-start.25
  74.4 4.7 %collective-permute-start.27 = (f32[144,128]{1,0:T(8,128)S(1)}, f32[144,128]{1,0:T(8,128)S(1)}, u32[]{:S(2)}, u32[]{:S(2)}) collective-permute-start(f32[144,128]{1,0:T(8,128)S(1)} %get-tuple-element.142), channel_id=1, source_target_pairs={{0,28},{1,29},{2,6},{3,7},{4,0},{5,1},{6,2},{7,3},{8,4},{9,5},{10,... | collective-permute-start | bytes 221192 | tf_op jit(solution)/shard_map/ppermute | solution.py:339
  79.1 1.2 %shard_map.91 = (f32[512,128]{1,0:T(8,128)S(1)}, f32[512,128]{1,0:T(8,128)S(1)}) custom-call(bf16[384,512]{1,0:T(8,128)(2,1)S(1)} %get-tuple-element.77.onehot.refs_0_, bf16[384,512]{1,0:T(8,128)(2,1)S(1)} %get-tuple-element.78.onehot.refs_1_, bf16[512,1024]{1,0:T(8,128)(2,1)S(1)} %get-tuple-element.79.refs_2_, ...), custom_call_target="tpu_custom_call" | custom-call | flops 1000000000 | tf_op jit(solution)/shard_map/pallas_call | solution.py:22
  80.4 1.1 %collective-permute-done.25.refs_1_ = f32[144,128]{1,0:T(8,128)S(1)} collective-permute-done((f32[144,128]{1,0:T(8,128)S(1)}, f32[144,128]{1,0:T(8,128)S(1)}, u32[]{:S(2)}, u32[]{:S(2)}) %collective-permute-start.25) | collective-permute-done | bytes 73760 | tf_op jit(solution)/shard_map/ppermute | solution.py:339
  81.5 0.4 shard_map.93
  81.9 0.1 collective-permute-start.29
  82.0 1.1 %shard_map.94.begun = f32[512,256]{1,0:T(8,128)} custom-call(f32[512,128]{1,0:T(8,128)S(1)} %get-tuple-element.144.base, bf16[512,768]{1,0:T(8,128)(2,1)S(1)} %get-tuple-element.96.refs_8_.far, f32[96,128]{1,0:T(8,128)S(1)} %get-tuple-element.139.refs_0_, f32[144,128]{1,0:T(8,128)S(1)} %collective-permute-done.25.refs_1_, ...), custom_call_target="tpu_custom_call" | custom-call | flops 1000000000 | tf_op jit(solution)/shard_map/pallas_call | solution.py:22
  83.2 0.4 collective-permute-done.29.got
  83.5 0.7 shard_map.95
  (33 shorter events, 0.1 us)
Async XLA Ops:
  0.0 1.6 %copy-start = (f32[4,8,128,128]{3,2,1,0:T(8,128)S(1)}, f32[4,8,128,128]{3,2,1,0:T(8,128)}, u32[]{:S(2)}) copy-start(f32[4,8,128,128]{3,2,1,0:T(8,128)} %tiles.3) | copy-start | bytes 6291460
  1.6 0.7 copy-start.3
  2.3 1.6 %copy-start.1 = (f32[4,8,128,128]{3,2,1,0:T(8,128)S(1)}, f32[4,8,128,128]{3,2,1,0:T(8,128)}, u32[]{:S(2)}) copy-start(f32[4,8,128,128]{3,2,1,0:T(8,128)} %tiles.2) | copy-start | bytes 6291460
  2.3 1.6 %copy-start.4 = (s32[4,8]{1,0:T(4,128)S(1)}, s32[4,8]{1,0:T(4,128)}, u32[]{:S(2)}) copy-start(s32[4,8]{1,0:T(4,128)} %columns.2) | copy-start | bytes 388
  3.2 2.2 %copy-start.5 = (f32[512,256]{1,0:T(8,128)S(1)}, f32[512,256]{1,0:T(8,128)}, u32[]{:S(2)}) copy-start(f32[512,256]{1,0:T(8,128)} %x.2) | copy-start | bytes 1572868
  3.2 16.0 %collective-permute-start.3 = (f32[4,7,128,128]{3,2,1,0:T(8,128)S(1)}, f32[4,7,128,128]{3,2,1,0:T(8,128)S(1)}, u32[]{:S(2)}, u32[]{:S(2)}) collective-permute-start(f32[4,7,128,128]{3,2,1,0:T(8,128)S(1)} %shard_map.78.total), channel_id=1, source_target_pairs={{0,1},{1,0},{2,3},{3,2},{4,5},{5,4},{6,7},{7,6},{8,9},{9,8},{10,11... | collective-permute-start | bytes 5505032 | tf_op jit(solution)/shard_map/ppermute | solution.py:111
  4.8 0.7 copy-start.6
  4.8 1.2 %copy-start.2 = (f32[512,256]{1,0:T(8,128)S(1)}, f32[512,256]{1,0:T(8,128)}, u32[]{:S(2)}) copy-start(f32[512,256]{1,0:T(8,128)} %x.3) | copy-start | bytes 1572868
  4.8 26.3 %collective-permute-start.2 = (f32[4,7,128,128]{3,2,1,0:T(8,128)S(1)}, f32[4,7,128,128]{3,2,1,0:T(8,128)S(1)}, u32[]{:S(2)}, u32[]{:S(2)}) collective-permute-start(f32[4,7,128,128]{3,2,1,0:T(8,128)S(1)} %shard_map.75.total), channel_id=1, source_target_pairs={{0,1},{1,0},{2,3},{3,2},{4,5},{5,4},{6,7},{7,6},{8,9},{9,8},{10,11... | collective-permute-start | bytes 5505032 | tf_op jit(solution)/shard_map/ppermute | solution.py:111
  5.4 4.8 %collective-permute-start = (f32[512,128]{1,0:T(8,128)S(1)}, f32[512,128]{1,0:T(8,128)S(1)}, u32[]{:S(2)}, u32[]{:S(2)}) collective-permute-start(f32[512,128]{1,0:T(8,128)S(1)} %get-tuple-element.76), channel_id=1, source_target_pairs={{0,1},{1,0},{2,3},{3,2},{4,5},{5,4},{6,7},{7,6},{8,9},{9,8},{10,11... | collective-permute-start | bytes 786440 | tf_op jit(solution)/shard_map/ppermute | solution.py:111
  5.5 4.7 %collective-permute-start.1 = (s32[8,48]{1,0:T(8,128)S(1)}, s32[8,48]{1,0:T(8,128)S(1)}, u32[]{:S(2)}, u32[]{:S(2)}) collective-permute-start(s32[8,48]{1,0:T(8,128)S(1)} %copy-done.6), channel_id=1, source_target_pairs={{0,1},{1,0},{2,3},{3,2},{4,5},{5,4},{6,7},{7,6},{8,9},{9,8},{10,11... | collective-permute-start | bytes 4616 | tf_op jit(solution)/shard_map/ppermute | solution.py:111
  6.0 14.3 %collective-permute-start.4 = (f32[512,128]{1,0:T(8,128)S(1)}, f32[512,128]{1,0:T(8,128)S(1)}, u32[]{:S(2)}, u32[]{:S(2)}) collective-permute-start(f32[512,128]{1,0:T(8,128)S(1)} %get-tuple-element.84), channel_id=1, source_target_pairs={{0,1},{1,0},{2,3},{3,2},{4,5},{5,4},{6,7},{7,6},{8,9},{9,8},{10,11... | collective-permute-start | bytes 786440 | tf_op jit(solution)/shard_map/ppermute | solution.py:111
  10.7 12.4 %collective-permute-start.5 = (f32[144,128]{1,0:T(8,128)S(1)}, f32[144,128]{1,0:T(8,128)S(1)}, u32[]{:S(2)}, u32[]{:S(2)}) collective-permute-start(f32[144,128]{1,0:T(8,128)S(1)} %get-tuple-element.90), channel_id=1, source_target_pairs={{0,4},{1,5},{2,30},{3,31},{4,8},{5,9},{6,10},{7,11},{8,12},{9,13},... | collective-permute-start | bytes 221192 | tf_op jit(solution)/shard_map/ppermute | solution.py:339
  13.6 11.2 %collective-permute-start.6 = (f32[192,128]{1,0:T(8,128)S(1)}, f32[192,128]{1,0:T(8,128)S(1)}, u32[]{:S(2)}, u32[]{:S(2)}) collective-permute-start(f32[192,128]{1,0:T(8,128)S(1)} %get-tuple-element.91), channel_id=1, source_target_pairs={{0,30},{1,31},{2,4},{3,5},{4,2},{5,3},{6,8},{7,9},{8,6},{9,7},{10,... | collective-permute-start | bytes 294920 | tf_op jit(solution)/shard_map/ppermute | solution.py:339
  19.2 5.6 %collective-permute-start.8 = (f32[192,128]{1,0:T(8,128)S(1)}, f32[192,128]{1,0:T(8,128)S(1)}, u32[]{:S(2)}, u32[]{:S(2)}) collective-permute-start(f32[192,128]{1,0:T(8,128)S(1)} %get-tuple-element.93), channel_id=1, source_target_pairs={{0,2},{1,3},{2,0},{3,1},{4,6},{5,7},{6,4},{7,5},{8,10},{9,11},{10,... | collective-permute-start | bytes 294920 | tf_op jit(solution)/shard_map/ppermute | solution.py:339
  20.4 4.4 %collective-permute-start.7 = (f32[144,128]{1,0:T(8,128)S(1)}, f32[144,128]{1,0:T(8,128)S(1)}, u32[]{:S(2)}, u32[]{:S(2)}) collective-permute-start(f32[144,128]{1,0:T(8,128)S(1)} %get-tuple-element.92), channel_id=1, source_target_pairs={{0,28},{1,29},{2,6},{3,7},{4,0},{5,1},{6,2},{7,3},{8,4},{9,5},{10,... | collective-permute-start | bytes 221192 | tf_op jit(solution)/shard_map/ppermute | solution.py:339
  25.3 8.1 %collective-permute-start.9 = (f32[144,128]{1,0:T(8,128)S(1)}, f32[144,128]{1,0:T(8,128)S(1)}, u32[]{:S(2)}, u32[]{:S(2)}) collective-permute-start(f32[144,128]{1,0:T(8,128)S(1)} %get-tuple-element.103), channel_id=1, source_target_pairs={{0,4},{1,5},{2,30},{3,31},{4,8},{5,9},{6,10},{7,11},{8,12},{9,13},... | collective-permute-start | bytes 221192 | tf_op jit(solution)/shard_map/ppermute | solution.py:339
  27.7 8.8 %collective-permute-start.10 = (f32[192,128]{1,0:T(8,128)S(1)}, f32[192,128]{1,0:T(8,128)S(1)}, u32[]{:S(2)}, u32[]{:S(2)}) collective-permute-start(f32[192,128]{1,0:T(8,128)S(1)} %get-tuple-element.104), channel_id=1, source_target_pairs={{0,30},{1,31},{2,4},{3,5},{4,2},{5,3},{6,8},{7,9},{8,6},{9,7},{10,... | collective-permute-start | bytes 294920 | tf_op jit(solution)/shard_map/ppermute | solution.py:339
  31.1 5.4 %collective-permute-start.11 = (f32[144,128]{1,0:T(8,128)S(1)}, f32[144,128]{1,0:T(8,128)S(1)}, u32[]{:S(2)}, u32[]{:S(2)}) collective-permute-start(f32[144,128]{1,0:T(8,128)S(1)} %get-tuple-element.105), channel_id=1, source_target_pairs={{0,28},{1,29},{2,6},{3,7},{4,0},{5,1},{6,2},{7,3},{8,4},{9,5},{10,... | collective-permute-start | bytes 221192 | tf_op jit(solution)/shard_map/ppermute | solution.py:339
  31.1 5.4 %collective-permute-start.12 = (f32[192,128]{1,0:T(8,128)S(1)}, f32[192,128]{1,0:T(8,128)S(1)}, u32[]{:S(2)}, u32[]{:S(2)}) collective-permute-start(f32[192,128]{1,0:T(8,128)S(1)} %get-tuple-element.106), channel_id=1, source_target_pairs={{0,2},{1,3},{2,0},{3,1},{4,6},{5,7},{6,4},{7,5},{8,10},{9,11},{10,... | collective-permute-start | bytes 294920 | tf_op jit(solution)/shard_map/ppermute | solution.py:339
  37.1 10.0 %collective-permute-start.14 = (f32[192,128]{1,0:T(8,128)S(1)}, f32[192,128]{1,0:T(8,128)S(1)}, u32[]{:S(2)}, u32[]{:S(2)}) collective-permute-start(f32[192,128]{1,0:T(8,128)S(1)} %get-tuple-element.115), channel_id=1, source_target_pairs={{0,30},{1,31},{2,4},{3,5},{4,2},{5,3},{6,8},{7,9},{8,6},{9,7},{10,... | collective-permute-start | bytes 294920 | tf_op jit(solution)/shard_map/ppermute | solution.py:339
  40.0 7.1 %collective-permute-start.16 = (f32[192,128]{1,0:T(8,128)S(1)}, f32[192,128]{1,0:T(8,128)S(1)}, u32[]{:S(2)}, u32[]{:S(2)}) collective-permute-start(f32[192,128]{1,0:T(8,128)S(1)} %get-tuple-element.117), channel_id=1, source_target_pairs={{0,2},{1,3},{2,0},{3,1},{4,6},{5,7},{6,4},{7,5},{8,10},{9,11},{10,... | collective-permute-start | bytes 294920 | tf_op jit(solution)/shard_map/ppermute | solution.py:339
  40.0 7.1 %collective-permute-start.13 = (f32[144,128]{1,0:T(8,128)S(1)}, f32[144,128]{1,0:T(8,128)S(1)}, u32[]{:S(2)}, u32[]{:S(2)}) collective-permute-start(f32[144,128]{1,0:T(8,128)S(1)} %get-tuple-element.114), channel_id=1, source_target_pairs={{0,4},{1,5},{2,30},{3,31},{4,8},{5,9},{6,10},{7,11},{8,12},{9,13},... | collective-permute-start | bytes 221192 | tf_op jit(solution)/shard_map/ppermute | solution.py:339
  40.5 6.6 %collective-permute-start.15 = (f32[144,128]{1,0:T(8,128)S(1)}, f32[144,128]{1,0:T(8,128)S(1)}, u32[]{:S(2)}, u32[]{:S(2)}) collective-permute-start(f32[144,128]{1,0:T(8,128)S(1)} %get-tuple-element.116), channel_id=1, source_target_pairs={{0,28},{1,29},{2,6},{3,7},{4,0},{5,1},{6,2},{7,3},{8,4},{9,5},{10,... | collective-permute-start | bytes 221192 | tf_op jit(solution)/shard_map/ppermute | solution.py:339
  47.6 10.9 %collective-permute-start.18 = (f32[192,128]{1,0:T(8,128)S(1)}, f32[192,128]{1,0:T(8,128)S(1)}, u32[]{:S(2)}, u32[]{:S(2)}) collective-permute-start(f32[192,128]{1,0:T(8,128)S(1)} %get-tuple-element.124), channel_id=1, source_target_pairs={{0,30},{1,31},{2,4},{3,5},{4,2},{5,3},{6,8},{7,9},{8,6},{9,7},{10,... | collective-permute-start | bytes 294920 | tf_op jit(solution)/shard_map/ppermute | solution.py:339
  51.4 7.1 %collective-permute-start.20 = (f32[192,128]{1,0:T(8,128)S(1)}, f32[192,128]{1,0:T(8,128)S(1)}, u32[]{:S(2)}, u32[]{:S(2)}) collective-permute-start(f32[192,128]{1,0:T(8,128)S(1)} %get-tuple-element.126), channel_id=1, source_target_pairs={{0,2},{1,3},{2,0},{3,1},{4,6},{5,7},{6,4},{7,5},{8,10},{9,11},{10,... | collective-permute-start | bytes 294920 | tf_op jit(solution)/shard_map/ppermute | solution.py:339
  51.4 7.0 %collective-permute-start.17 = (f32[144,128]{1,0:T(8,128)S(1)}, f32[144,128]{1,0:T(8,128)S(1)}, u32[]{:S(2)}, u32[]{:S(2)}) collective-permute-start(f32[144,128]{1,0:T(8,128)S(1)} %get-tuple-element.123), channel_id=1, source_target_pairs={{0,4},{1,5},{2,30},{3,31},{4,8},{5,9},{6,10},{7,11},{8,12},{9,13},... | collective-permute-start | bytes 221192 | tf_op jit(solution)/shard_map/ppermute | solution.py:339
  51.4 7.0 %collective-permute-start.19 = (f32[144,128]{1,0:T(8,128)S(1)}, f32[144,128]{1,0:T(8,128)S(1)}, u32[]{:S(2)}, u32[]{:S(2)}) collective-permute-start(f32[144,128]{1,0:T(8,128)S(1)} %get-tuple-element.125), channel_id=1, source_target_pairs={{0,28},{1,29},{2,6},{3,7},{4,0},{5,1},{6,2},{7,3},{8,4},{9,5},{10,... | collective-permute-start | bytes 221192 | tf_op jit(solution)/shard_map/ppermute | solution.py:339
  59.0 10.6 %collective-permute-start.22 = (f32[192,128]{1,0:T(8,128)S(1)}, f32[192,128]{1,0:T(8,128)S(1)}, u32[]{:S(2)}, u32[]{:S(2)}) collective-permute-start(f32[192,128]{1,0:T(8,128)S(1)} %get-tuple-element.133), channel_id=1, source_target_pairs={{0,30},{1,31},{2,4},{3,5},{4,2},{5,3},{6,8},{7,9},{8,6},{9,7},{10,... | collective-permute-start | bytes 294920 | tf_op jit(solution)/shard_map/ppermute | solution.py:339
  62.5 7.1 %collective-permute-start.24 = (f32[192,128]{1,0:T(8,128)S(1)}, f32[192,128]{1,0:T(8,128)S(1)}, u32[]{:S(2)}, u32[]{:S(2)}) collective-permute-start(f32[192,128]{1,0:T(8,128)S(1)} %get-tuple-element.135), channel_id=1, source_target_pairs={{0,2},{1,3},{2,0},{3,1},{4,6},{5,7},{6,4},{7,5},{8,10},{9,11},{10,... | collective-permute-start | bytes 294920 | tf_op jit(solution)/shard_map/ppermute | solution.py:339
  62.5 7.0 %collective-permute-start.21 = (f32[144,128]{1,0:T(8,128)S(1)}, f32[144,128]{1,0:T(8,128)S(1)}, u32[]{:S(2)}, u32[]{:S(2)}) collective-permute-start(f32[144,128]{1,0:T(8,128)S(1)} %get-tuple-element.132), channel_id=1, source_target_pairs={{0,4},{1,5},{2,30},{3,31},{4,8},{5,9},{6,10},{7,11},{8,12},{9,13},... | collective-permute-start | bytes 221192 | tf_op jit(solution)/shard_map/ppermute | solution.py:339
  63.1 6.5 %collective-permute-start.23 = (f32[144,128]{1,0:T(8,128)S(1)}, f32[144,128]{1,0:T(8,128)S(1)}, u32[]{:S(2)}, u32[]{:S(2)}) collective-permute-start(f32[144,128]{1,0:T(8,128)S(1)} %get-tuple-element.134), channel_id=1, source_target_pairs={{0,28},{1,29},{2,6},{3,7},{4,0},{5,1},{6,2},{7,3},{8,4},{9,5},{10,... | collective-permute-start | bytes 221192 | tf_op jit(solution)/shard_map/ppermute | solution.py:339
  70.1 11.4 %collective-permute-start.26 = (f32[192,128]{1,0:T(8,128)S(1)}, f32[192,128]{1,0:T(8,128)S(1)}, u32[]{:S(2)}, u32[]{:S(2)}) collective-permute-start(f32[192,128]{1,0:T(8,128)S(1)} %get-tuple-element.141), channel_id=1, source_target_pairs={{0,30},{1,31},{2,4},{3,5},{4,2},{5,3},{6,8},{7,9},{8,6},{9,7},{10,... | collective-permute-start | bytes 294920 | tf_op jit(solution)/shard_map/ppermute | solution.py:339
  74.4 7.1 %collective-permute-start.28 = (f32[192,128]{1,0:T(8,128)S(1)}, f32[192,128]{1,0:T(8,128)S(1)}, u32[]{:S(2)}, u32[]{:S(2)}) collective-permute-start(f32[192,128]{1,0:T(8,128)S(1)} %get-tuple-element.143), channel_id=1, source_target_pairs={{0,2},{1,3},{2,0},{3,1},{4,6},{5,7},{6,4},{7,5},{8,10},{9,11},{10,... | collective-permute-start | bytes 294920 | tf_op jit(solution)/shard_map/ppermute | solution.py:339
  74.4 7.0 %collective-permute-start.25 = (f32[144,128]{1,0:T(8,128)S(1)}, f32[144,128]{1,0:T(8,128)S(1)}, u32[]{:S(2)}, u32[]{:S(2)}) collective-permute-start(f32[144,128]{1,0:T(8,128)S(1)} %get-tuple-element.140), channel_id=1, source_target_pairs={{0,4},{1,5},{2,30},{3,31},{4,8},{5,9},{6,10},{7,11},{8,12},{9,13},... | collective-permute-start | bytes 221192 | tf_op jit(solution)/shard_map/ppermute | solution.py:339
  74.4 7.0 %collective-permute-start.27 = (f32[144,128]{1,0:T(8,128)S(1)}, f32[144,128]{1,0:T(8,128)S(1)}, u32[]{:S(2)}, u32[]{:S(2)}) collective-permute-start(f32[144,128]{1,0:T(8,128)S(1)} %get-tuple-element.142), channel_id=1, source_target_pairs={{0,28},{1,29},{2,6},{3,7},{4,0},{5,1},{6,2},{7,3},{8,4},{9,5},{10,... | collective-permute-start | bytes 221192 | tf_op jit(solution)/shard_map/ppermute | solution.py:339
  81.9 1.6 %collective-permute-start.29 = (f32[512,128]{1,0:T(8,128)S(1)}, f32[512,128]{1,0:T(8,128)S(1)}, u32[]{:S(2)}, u32[]{:S(2)}) collective-permute-start(f32[512,128]{1,0:T(8,128)S(1)} %shard_map.93), channel_id=1, source_target_pairs={{0,1},{1,0},{2,3},{3,2},{4,5},{5,4},{6,7},{7,6},{8,9},{9,8},{10,11... | collective-permute-start | bytes 786440 | tf_op jit(solution)/shard_map/ppermute | solution.py:111

commit v8 on v7

--- a/solution.py
+++ b/solution.py
@@ -13,7 +13,6 @@
 COST = 10**9
 
 VMEM = pl.BlockSpec(memory_space=pltpu.VMEM)
-SMEM = pl.BlockSpec(memory_space=pltpu.SMEM)
 ANY = pl.BlockSpec(memory_space=pl.ANY)
 F32, BF16 = jnp.float32, jnp.bfloat16
 
@@ -167,16 +166,15 @@
     on_each_side(body)
 
 
-def add_blocks(columns, tiles, total, block):
-    for slot in range(tiles.shape[1]):
-        column = columns[block, slot]
-        total[block, column] += tiles[block, slot]
-
-
-def merge_kernel(columns, tiles, total):
+def merge_kernel(columns_in, tiles, total, columns, done):
+    fetch = pltpu.make_async_copy(columns_in, columns, done)
+    fetch.start()
     total[...] = jnp.zeros_like(total)
+    fetch.wait()
     for block in range(tiles.shape[0]):
-        add_blocks(columns, tiles, total, block)
+        for slot in range(tiles.shape[1]):
+            column = columns[block, slot]
+            total[block, column] += tiles[block, slot]
 
 
 def split_kernel(total, onehot, own, far, out):
@@ -306,7 +304,7 @@
     devices = lax.axis_size("rows")
     local_rows, panels = tracers_init.shape
     half = panels // 2
-    blocks, _, size, _ = explicit_tiles.shape
+    blocks, slots, size, _ = explicit_tiles.shape
     partners, length = send_rows.shape
     halo_rows = partners * length
     columns = blocks + halo_rows // size
@@ -322,7 +320,13 @@
         return call(halves_kernel, [state_half] * 2, [VMEM], (x,), cost=cost)
 
     def merge(tiles, cols):
-        return call(merge_kernel, [((blocks, columns, size, size), F32)], [SMEM, VMEM], (cols, tiles))[0]
+        return call(
+            merge_kernel,
+            [((blocks, columns, size, size), F32)],
+            [ANY, VMEM],
+            (cols, tiles),
+            [pltpu.SMEM((blocks, slots), jnp.int32), pltpu.SemaphoreType.DMA],
+        )[0]
 
     def split(total, onehot):
         return call(

time: 84.6 us -> 84.5 us (level)
  no operation moved by 1% of the time
where the time goes in v8:
time: 84.5 us; the launch traced here: 84.3 us
  starting transfers between devices  50.7 us (60%)
  Pallas kernels  18.2 us (22%)
  waiting for transfers between devices  12.4 us (15%)
  local copies, waits for them, and re-layouts  2.49 us (3%)
    ppermute x24, starting transfers between devices, exchange(): arrived.append(lax.ppermute(piece, 'rows', pairs))  48.5 us
    pallas_call x23, Pallas kernels, call(): pl.pallas_call(kernel, out_shape=[jax.ShapeDtypeStruct(shape, dtype) for...  18.2 us
    ppermute x24, waiting for transfers between devices, exchange(): arrived.append(lax.ppermute(piece, 'rows', pairs))  8.32 us
    ppermute x6, waiting for transfers between devices, swap(): return lax.ppermute(x, 'rows', [(i, i ^ 1) for i in range(devices)])  4.11 us
    unnamed x14, local copies, waits for them, and re-layouts  2.49 us
    ppermute x6, starting transfers between devices, swap(): return lax.ppermute(x, 'rows', [(i, i ^ 1) for i in range(devices)])  2.16 us
  transfers between devices with their start and end apart: 30, of which 8 were waited for; matrix products, arithmetic and copies ran while one was open for 0% of the time, Pallas kernels for 17%

profile of v8, /device:TPU:0, one launch (start us, length us, event | category | flops | bytes accessed | tf_op | source)
XLA Modules:
  0.0 84.3 jit_solution(7277160401980475669)
XLA Ops:
  0.0 1.6 %copy-done = f32[4,8,128,128]{3,2,1,0:T(8,128)S(1)} copy-done((f32[4,8,128,128]{3,2,1,0:T(8,128)S(1)}, f32[4,8,128,128]{3,2,1,0:T(8,128)}, u32[]{:S(2)}) %copy-start) | copy-done | bytes 2097176
  1.6 0.7 copy-done.3
  2.3 0.8 shard_map.78.total
  3.1 0.0 copy-start.5
  3.1 0.6 collective-permute-start.3
  3.7 0.2 copy-done.1
  3.9 0.8 shard_map.75.total
  4.7 0.0 copy-start.6
  4.7 0.0 copy-start.2
  4.7 0.6 collective-permute-start.2
  5.3 0.1 collective-permute-start
  5.4 0.5 collective-permute-start.1
  5.9 0.4 collective-permute-start.4
  6.3 3.7 %collective-permute-done.1.rows_other = s32[8,48]{1,0:T(8,128)S(1)} collective-permute-done((s32[8,48]{1,0:T(8,128)S(1)}, s32[8,48]{1,0:T(8,128)S(1)}, u32[]{:S(2)}, u32[]{:S(2)}) %collective-permute-start.1) | collective-permute-done | bytes 1568 | tf_op jit(solution)/shard_map/ppermute | solution.py:110
  10.1 0.0 collective-permute-done.other.refs_7_
  10.1 0.5 shard_map.74
  10.6 2.9 %collective-permute-start.5 = (f32[144,128]{1,0:T(8,128)S(1)}, f32[144,128]{1,0:T(8,128)S(1)}, u32[]{:S(2)}, u32[]{:S(2)}) collective-permute-start(f32[144,128]{1,0:T(8,128)S(1)} %get-tuple-element.90), channel_id=1, source_target_pairs={{0,4},{1,5},{2,30},{3,31},{4,8},{5,9},{6,10},{7,11},{8,12},{9,13},... | collective-permute-start | bytes 221192 | tf_op jit(solution)/shard_map/ppermute | solution.py:343
  13.5 4.1 %collective-permute-start.6 = (f32[192,128]{1,0:T(8,128)S(1)}, f32[192,128]{1,0:T(8,128)S(1)}, u32[]{:S(2)}, u32[]{:S(2)}) collective-permute-start(f32[192,128]{1,0:T(8,128)S(1)} %get-tuple-element.91), channel_id=1, source_target_pairs={{0,30},{1,31},{2,4},{3,5},{4,2},{5,3},{6,8},{7,9},{8,6},{9,7},{10,... | collective-permute-start | bytes 294920 | tf_op jit(solution)/shard_map/ppermute | solution.py:343
  17.7 0.7 shard_map.76
  18.4 0.7 shard_map.79
  19.1 0.0 collective-permute-done.3.total
  19.1 0.5 collective-permute-start.8
  19.6 0.7 shard_map.80
  20.3 0.0 collective-permute-done.4.refs_5_
  20.3 1.7 %collective-permute-start.7 = (f32[144,128]{1,0:T(8,128)S(1)}, f32[144,128]{1,0:T(8,128)S(1)}, u32[]{:S(2)}, u32[]{:S(2)}) collective-permute-start(f32[144,128]{1,0:T(8,128)S(1)} %get-tuple-element.92), channel_id=1, source_target_pairs={{0,28},{1,29},{2,6},{3,7},{4,0},{5,1},{6,2},{7,3},{8,4},{9,5},{10,... | collective-permute-start | bytes 221192 | tf_op jit(solution)/shard_map/ppermute | solution.py:343
  22.0 1.0 %shard_map.82 = (f32[512,128]{1,0:T(8,128)S(1)}, f32[512,128]{1,0:T(8,128)S(1)}, f32[384,128]{1,0:T(8,128)S(1)}, f32[384,128]{1,0:T(8,128)S(1)}) custom-call(bf16[384,512]{1,0:T(8,128)(2,1)S(1)} %get-tuple-element.77.onehot.refs_0_, bf16[384,512]{1,0:T(8,128)(2,1)S(1)} %get-tuple-element.78.onehot.refs_1_, bf16[512,1024]{1,0:T(8,128)(2,1)S(1)} %get-tuple-element.81.refs_2_, ...), custom_call_target="tpu_custom_call" | custom-call | flops 1000000000 | tf_op jit(solution)/shard_map/pallas_call | solution.py:21
  23.0 0.0 collective-permute-done.5.refs_9_.refs_5_
  23.0 1.7 %collective-permute-done.7.refs_11_.refs_7_ = f32[144,128]{1,0:T(8,128)S(1)} collective-permute-done((f32[144,128]{1,0:T(8,128)S(1)}, f32[144,128]{1,0:T(8,128)S(1)}, u32[]{:S(2)}, u32[]{:S(2)}) %collective-permute-start.7) | collective-permute-done | bytes 73760 | tf_op jit(solution)/shard_map/ppermute | solution.py:343
  24.7 0.0 collective-permute-done.6.refs_10_.refs_6_
  24.7 0.0 collective-permute-done.8.refs_12_.refs_8_
  24.7 0.5 shard_map.84
  25.2 2.4 %collective-permute-start.9 = (f32[144,128]{1,0:T(8,128)S(1)}, f32[144,128]{1,0:T(8,128)S(1)}, u32[]{:S(2)}, u32[]{:S(2)}) collective-permute-start(f32[144,128]{1,0:T(8,128)S(1)} %get-tuple-element.103), channel_id=1, source_target_pairs={{0,4},{1,5},{2,30},{3,31},{4,8},{5,9},{6,10},{7,11},{8,12},{9,13},... | collective-permute-start | bytes 221192 | tf_op jit(solution)/shard_map/ppermute | solution.py:343
  27.6 3.4 %collective-permute-start.10 = (f32[192,128]{1,0:T(8,128)S(1)}, f32[192,128]{1,0:T(8,128)S(1)}, u32[]{:S(2)}, u32[]{:S(2)}) collective-permute-start(f32[192,128]{1,0:T(8,128)S(1)} %get-tuple-element.104), channel_id=1, source_target_pairs={{0,30},{1,31},{2,4},{3,5},{4,2},{5,3},{6,8},{7,9},{8,6},{9,7},{10,... | collective-permute-start | bytes 294920 | tf_op jit(solution)/shard_map/ppermute | solution.py:343
  31.1 0.7 shard_map.77
  31.8 1.5 %shard_map.83 = (f32[512,128]{1,0:T(8,128)S(1)}, f32[512,128]{1,0:T(8,128)S(1)}, f32[384,128]{1,0:T(8,128)S(1)}, f32[384,128]{1,0:T(8,128)S(1)}) custom-call(bf16[384,512]{1,0:T(8,128)(2,1)S(1)} %get-tuple-element.77.onehot.refs_0_, bf16[384,512]{1,0:T(8,128)(2,1)S(1)} %get-tuple-element.78.onehot.refs_1_, bf16[512,1024]{1,0:T(8,128)(2,1)S(1)} %get-tuple-element.79.refs_2_, ...), custom_call_target="tpu_custom_call" | custom-call | flops 1000000000 | tf_op jit(solution)/shard_map/pallas_call | solution.py:21
  33.3 3.1 %collective-permute-done.11.refs_13_.refs_7_ = f32[144,128]{1,0:T(8,128)S(1)} collective-permute-done((f32[144,128]{1,0:T(8,128)S(1)}, f32[144,128]{1,0:T(8,128)S(1)}, u32[]{:S(2)}, u32[]{:S(2)}) %collective-permute-start.11) | collective-permute-done | bytes 73760 | tf_op jit(solution)/shard_map/ppermute | solution.py:343
  36.5 0.5 shard_map.86
  37.0 2.9 %collective-permute-start.14 = (f32[192,128]{1,0:T(8,128)S(1)}, f32[192,128]{1,0:T(8,128)S(1)}, u32[]{:S(2)}, u32[]{:S(2)}) collective-permute-start(f32[192,128]{1,0:T(8,128)S(1)} %get-tuple-element.115), channel_id=1, source_target_pairs={{0,30},{1,31},{2,4},{3,5},{4,2},{5,3},{6,8},{7,9},{8,6},{9,7},{10,... | collective-permute-start | bytes 294920 | tf_op jit(solution)/shard_map/ppermute | solution.py:343
  39.9 0.5 collective-permute-start.13
  40.4 4.3 %collective-permute-start.15 = (f32[144,128]{1,0:T(8,128)S(1)}, f32[144,128]{1,0:T(8,128)S(1)}, u32[]{:S(2)}, u32[]{:S(2)}) collective-permute-start(f32[144,128]{1,0:T(8,128)S(1)} %get-tuple-element.116), channel_id=1, source_target_pairs={{0,28},{1,29},{2,6},{3,7},{4,0},{5,1},{6,2},{7,3},{8,4},{9,5},{10,... | collective-permute-start | bytes 221192 | tf_op jit(solution)/shard_map/ppermute | solution.py:343
  44.6 1.5 %shard_map.85 = (f32[512,128]{1,0:T(8,128)S(1)}, f32[512,128]{1,0:T(8,128)S(1)}, f32[384,128]{1,0:T(8,128)S(1)}, f32[384,128]{1,0:T(8,128)S(1)}) custom-call(bf16[384,512]{1,0:T(8,128)(2,1)S(1)} %get-tuple-element.77.onehot.refs_0_, bf16[384,512]{1,0:T(8,128)(2,1)S(1)} %get-tuple-element.78.onehot.refs_1_, bf16[512,1024]{1,0:T(8,128)(2,1)S(1)} %get-tuple-element.81.refs_2_, ...), custom_call_target="tpu_custom_call" | custom-call | flops 1000000000 | tf_op jit(solution)/shard_map/pallas_call | solution.py:21
  46.2 0.8 collective-permute-done.13.refs_9_.refs_5_
  47.0 0.5 shard_map.88
  47.5 3.8 %collective-permute-start.18 = (f32[192,128]{1,0:T(8,128)S(1)}, f32[192,128]{1,0:T(8,128)S(1)}, u32[]{:S(2)}, u32[]{:S(2)}) collective-permute-start(f32[192,128]{1,0:T(8,128)S(1)} %get-tuple-element.124), channel_id=1, source_target_pairs={{0,30},{1,31},{2,4},{3,5},{4,2},{5,3},{6,8},{7,9},{8,6},{9,7},{10,... | collective-permute-start | bytes 294920 | tf_op jit(solution)/shard_map/ppermute | solution.py:343
  51.3 4.7 %collective-permute-start.19 = (f32[144,128]{1,0:T(8,128)S(1)}, f32[144,128]{1,0:T(8,128)S(1)}, u32[]{:S(2)}, u32[]{:S(2)}) collective-permute-start(f32[144,128]{1,0:T(8,128)S(1)} %get-tuple-element.125), channel_id=1, source_target_pairs={{0,28},{1,29},{2,6},{3,7},{4,0},{5,1},{6,2},{7,3},{8,4},{9,5},{10,... | collective-permute-start | bytes 221192 | tf_op jit(solution)/shard_map/ppermute | solution.py:343
  56.0 1.5 %shard_map.87 = (f32[512,128]{1,0:T(8,128)S(1)}, f32[512,128]{1,0:T(8,128)S(1)}, f32[384,128]{1,0:T(8,128)S(1)}, f32[384,128]{1,0:T(8,128)S(1)}) custom-call(bf16[384,512]{1,0:T(8,128)(2,1)S(1)} %get-tuple-element.77.onehot.refs_0_, bf16[384,512]{1,0:T(8,128)(2,1)S(1)} %get-tuple-element.78.onehot.refs_1_, bf16[512,1024]{1,0:T(8,128)(2,1)S(1)} %get-tuple-element.79.refs_2_, ...), custom_call_target="tpu_custom_call" | custom-call | flops 1000000000 | tf_op jit(solution)/shard_map/pallas_call | solution.py:21
  57.6 0.8 collective-permute-done.17.refs_11_.refs_5_
  58.4 0.5 shard_map.90
  58.9 3.5 %collective-permute-start.22 = (f32[192,128]{1,0:T(8,128)S(1)}, f32[192,128]{1,0:T(8,128)S(1)}, u32[]{:S(2)}, u32[]{:S(2)}) collective-permute-start(f32[192,128]{1,0:T(8,128)S(1)} %get-tuple-element.133), channel_id=1, source_target_pairs={{0,30},{1,31},{2,4},{3,5},{4,2},{5,3},{6,8},{7,9},{8,6},{9,7},{10,... | collective-permute-start | bytes 294920 | tf_op jit(solution)/shard_map/ppermute | solution.py:343
  62.4 0.6 collective-permute-start.21
  63.0 4.1 %collective-permute-start.23 = (f32[144,128]{1,0:T(8,128)S(1)}, f32[144,128]{1,0:T(8,128)S(1)}, u32[]{:S(2)}, u32[]{:S(2)}) collective-permute-start(f32[144,128]{1,0:T(8,128)S(1)} %get-tuple-element.134), channel_id=1, source_target_pairs={{0,28},{1,29},{2,6},{3,7},{4,0},{5,1},{6,2},{7,3},{8,4},{9,5},{10,... | collective-permute-start | bytes 221192 | tf_op jit(solution)/shard_map/ppermute | solution.py:343
  67.1 1.5 %shard_map.89 = (f32[512,128]{1,0:T(8,128)S(1)}, f32[512,128]{1,0:T(8,128)S(1)}, f32[384,128]{1,0:T(8,128)S(1)}, f32[384,128]{1,0:T(8,128)S(1)}) custom-call(bf16[384,512]{1,0:T(8,128)(2,1)S(1)} %get-tuple-element.77.onehot.refs_0_, bf16[384,512]{1,0:T(8,128)(2,1)S(1)} %get-tuple-element.78.onehot.refs_1_, bf16[512,1024]{1,0:T(8,128)(2,1)S(1)} %get-tuple-element.81.refs_2_, ...), custom_call_target="tpu_custom_call" | custom-call | flops 1000000000 | tf_op jit(solution)/shard_map/pallas_call | solution.py:21
  68.7 0.8 collective-permute-done.21.refs_9_.refs_5_
  69.5 0.5 shard_map.92
  70.0 4.3 %collective-permute-start.26 = (f32[192,128]{1,0:T(8,128)S(1)}, f32[192,128]{1,0:T(8,128)S(1)}, u32[]{:S(2)}, u32[]{:S(2)}) collective-permute-start(f32[192,128]{1,0:T(8,128)S(1)} %get-tuple-element.141), channel_id=1, source_target_pairs={{0,30},{1,31},{2,4},{3,5},{4,2},{5,3},{6,8},{7,9},{8,6},{9,7},{10,... | collective-permute-start | bytes 294920 | tf_op jit(solution)/shard_map/ppermute | solution.py:343
  74.3 0.0 collective-permute-start.25
  74.3 4.7 %collective-permute-start.27 = (f32[144,128]{1,0:T(8,128)S(1)}, f32[144,128]{1,0:T(8,128)S(1)}, u32[]{:S(2)}, u32[]{:S(2)}) collective-permute-start(f32[144,128]{1,0:T(8,128)S(1)} %get-tuple-element.142), channel_id=1, source_target_pairs={{0,28},{1,29},{2,6},{3,7},{4,0},{5,1},{6,2},{7,3},{8,4},{9,5},{10,... | collective-permute-start | bytes 221192 | tf_op jit(solution)/shard_map/ppermute | solution.py:343
  79.0 1.2 %shard_map.91 = (f32[512,128]{1,0:T(8,128)S(1)}, f32[512,128]{1,0:T(8,128)S(1)}) custom-call(bf16[384,512]{1,0:T(8,128)(2,1)S(1)} %get-tuple-element.77.onehot.refs_0_, bf16[384,512]{1,0:T(8,128)(2,1)S(1)} %get-tuple-element.78.onehot.refs_1_, bf16[512,1024]{1,0:T(8,128)(2,1)S(1)} %get-tuple-element.79.refs_2_, ...), custom_call_target="tpu_custom_call" | custom-call | flops 1000000000 | tf_op jit(solution)/shard_map/pallas_call | solution.py:21
  80.3 1.1 %collective-permute-done.25.refs_1_ = f32[144,128]{1,0:T(8,128)S(1)} collective-permute-done((f32[144,128]{1,0:T(8,128)S(1)}, f32[144,128]{1,0:T(8,128)S(1)}, u32[]{:S(2)}, u32[]{:S(2)}) %collective-permute-start.25) | collective-permute-done | bytes 73760 | tf_op jit(solution)/shard_map/ppermute | solution.py:343
  81.4 0.4 shard_map.93
  81.8 0.1 collective-permute-start.29
  81.9 1.1 %shard_map.94.begun = f32[512,256]{1,0:T(8,128)} custom-call(f32[512,128]{1,0:T(8,128)S(1)} %get-tuple-element.144.base, bf16[512,768]{1,0:T(8,128)(2,1)S(1)} %get-tuple-element.96.refs_8_.far, f32[96,128]{1,0:T(8,128)S(1)} %get-tuple-element.139.refs_0_, f32[144,128]{1,0:T(8,128)S(1)} %collective-permute-done.25.refs_1_, ...), custom_call_target="tpu_custom_call" | custom-call | flops 1000000000 | tf_op jit(solution)/shard_map/pallas_call | solution.py:21
  83.1 0.4 collective-permute-done.29.got
  83.4 0.7 shard_map.95
  (33 shorter events, 0.1 us)
Async XLA Ops:
  0.0 1.6 %copy-start = (f32[4,8,128,128]{3,2,1,0:T(8,128)S(1)}, f32[4,8,128,128]{3,2,1,0:T(8,128)}, u32[]{:S(2)}) copy-start(f32[4,8,128,128]{3,2,1,0:T(8,128)} %tiles.3) | copy-start | bytes 6291460
  1.6 0.7 copy-start.3
  2.3 1.6 %copy-start.1 = (f32[4,8,128,128]{3,2,1,0:T(8,128)S(1)}, f32[4,8,128,128]{3,2,1,0:T(8,128)}, u32[]{:S(2)}) copy-start(f32[4,8,128,128]{3,2,1,0:T(8,128)} %tiles.2) | copy-start | bytes 6291460
  2.3 1.6 %copy-start.4 = (s32[4,8]{1,0:T(4,128)S(1)}, s32[4,8]{1,0:T(4,128)}, u32[]{:S(2)}) copy-start(s32[4,8]{1,0:T(4,128)} %columns_in.2) | copy-start | bytes 388
  3.1 2.2 %copy-start.5 = (f32[512,256]{1,0:T(8,128)S(1)}, f32[512,256]{1,0:T(8,128)}, u32[]{:S(2)}) copy-start(f32[512,256]{1,0:T(8,128)} %x.2) | copy-start | bytes 1572868
  3.1 16.0 %collective-permute-start.3 = (f32[4,7,128,128]{3,2,1,0:T(8,128)S(1)}, f32[4,7,128,128]{3,2,1,0:T(8,128)S(1)}, u32[]{:S(2)}, u32[]{:S(2)}) collective-permute-start(f32[4,7,128,128]{3,2,1,0:T(8,128)S(1)} %shard_map.78.total), channel_id=1, source_target_pairs={{0,1},{1,0},{2,3},{3,2},{4,5},{5,4},{6,7},{7,6},{8,9},{9,8},{10,11... | collective-permute-start | bytes 5505032 | tf_op jit(solution)/shard_map/ppermute | solution.py:110
  4.7 0.7 copy-start.6
  4.7 1.2 %copy-start.2 = (f32[512,256]{1,0:T(8,128)S(1)}, f32[512,256]{1,0:T(8,128)}, u32[]{:S(2)}) copy-start(f32[512,256]{1,0:T(8,128)} %x.3) | copy-start | bytes 1572868
  4.7 26.4 %collective-permute-start.2 = (f32[4,7,128,128]{3,2,1,0:T(8,128)S(1)}, f32[4,7,128,128]{3,2,1,0:T(8,128)S(1)}, u32[]{:S(2)}, u32[]{:S(2)}) collective-permute-start(f32[4,7,128,128]{3,2,1,0:T(8,128)S(1)} %shard_map.75.total), channel_id=1, source_target_pairs={{0,1},{1,0},{2,3},{3,2},{4,5},{5,4},{6,7},{7,6},{8,9},{9,8},{10,11... | collective-permute-start | bytes 5505032 | tf_op jit(solution)/shard_map/ppermute | solution.py:110
  5.3 4.8 %collective-permute-start = (f32[512,128]{1,0:T(8,128)S(1)}, f32[512,128]{1,0:T(8,128)S(1)}, u32[]{:S(2)}, u32[]{:S(2)}) collective-permute-start(f32[512,128]{1,0:T(8,128)S(1)} %get-tuple-element.76), channel_id=1, source_target_pairs={{0,1},{1,0},{2,3},{3,2},{4,5},{5,4},{6,7},{7,6},{8,9},{9,8},{10,11... | collective-permute-start | bytes 786440 | tf_op jit(solution)/shard_map/ppermute | solution.py:110
  5.4 4.7 %collective-permute-start.1 = (s32[8,48]{1,0:T(8,128)S(1)}, s32[8,48]{1,0:T(8,128)S(1)}, u32[]{:S(2)}, u32[]{:S(2)}) collective-permute-start(s32[8,48]{1,0:T(8,128)S(1)} %copy-done.6), channel_id=1, source_target_pairs={{0,1},{1,0},{2,3},{3,2},{4,5},{5,4},{6,7},{7,6},{8,9},{9,8},{10,11... | collective-permute-start | bytes 4616 | tf_op jit(solution)/shard_map/ppermute | solution.py:110
  5.9 14.4 %collective-permute-start.4 = (f32[512,128]{1,0:T(8,128)S(1)}, f32[512,128]{1,0:T(8,128)S(1)}, u32[]{:S(2)}, u32[]{:S(2)}) collective-permute-start(f32[512,128]{1,0:T(8,128)S(1)} %get-tuple-element.84), channel_id=1, source_target_pairs={{0,1},{1,0},{2,3},{3,2},{4,5},{5,4},{6,7},{7,6},{8,9},{9,8},{10,11... | collective-permute-start | bytes 786440 | tf_op jit(solution)/shard_map/ppermute | solution.py:110
  10.6 12.4 %collective-permute-start.5 = (f32[144,128]{1,0:T(8,128)S(1)}, f32[144,128]{1,0:T(8,128)S(1)}, u32[]{:S(2)}, u32[]{:S(2)}) collective-permute-start(f32[144,128]{1,0:T(8,128)S(1)} %get-tuple-element.90), channel_id=1, source_target_pairs={{0,4},{1,5},{2,30},{3,31},{4,8},{5,9},{6,10},{7,11},{8,12},{9,13},... | collective-permute-start | bytes 221192 | tf_op jit(solution)/shard_map/ppermute | solution.py:343
  13.5 11.2 %collective-permute-start.6 = (f32[192,128]{1,0:T(8,128)S(1)}, f32[192,128]{1,0:T(8,128)S(1)}, u32[]{:S(2)}, u32[]{:S(2)}) collective-permute-start(f32[192,128]{1,0:T(8,128)S(1)} %get-tuple-element.91), channel_id=1, source_target_pairs={{0,30},{1,31},{2,4},{3,5},{4,2},{5,3},{6,8},{7,9},{8,6},{9,7},{10,... | collective-permute-start | bytes 294920 | tf_op jit(solution)/shard_map/ppermute | solution.py:343
  19.1 5.6 %collective-permute-start.8 = (f32[192,128]{1,0:T(8,128)S(1)}, f32[192,128]{1,0:T(8,128)S(1)}, u32[]{:S(2)}, u32[]{:S(2)}) collective-permute-start(f32[192,128]{1,0:T(8,128)S(1)} %get-tuple-element.93), channel_id=1, source_target_pairs={{0,2},{1,3},{2,0},{3,1},{4,6},{5,7},{6,4},{7,5},{8,10},{9,11},{10,... | collective-permute-start | bytes 294920 | tf_op jit(solution)/shard_map/ppermute | solution.py:343
  20.3 4.4 %collective-permute-start.7 = (f32[144,128]{1,0:T(8,128)S(1)}, f32[144,128]{1,0:T(8,128)S(1)}, u32[]{:S(2)}, u32[]{:S(2)}) collective-permute-start(f32[144,128]{1,0:T(8,128)S(1)} %get-tuple-element.92), channel_id=1, source_target_pairs={{0,28},{1,29},{2,6},{3,7},{4,0},{5,1},{6,2},{7,3},{8,4},{9,5},{10,... | collective-permute-start | bytes 221192 | tf_op jit(solution)/shard_map/ppermute | solution.py:343
  25.2 8.1 %collective-permute-start.9 = (f32[144,128]{1,0:T(8,128)S(1)}, f32[144,128]{1,0:T(8,128)S(1)}, u32[]{:S(2)}, u32[]{:S(2)}) collective-permute-start(f32[144,128]{1,0:T(8,128)S(1)} %get-tuple-element.103), channel_id=1, source_target_pairs={{0,4},{1,5},{2,30},{3,31},{4,8},{5,9},{6,10},{7,11},{8,12},{9,13},... | collective-permute-start | bytes 221192 | tf_op jit(solution)/shard_map/ppermute | solution.py:343
  27.6 8.8 %collective-permute-start.10 = (f32[192,128]{1,0:T(8,128)S(1)}, f32[192,128]{1,0:T(8,128)S(1)}, u32[]{:S(2)}, u32[]{:S(2)}) collective-permute-start(f32[192,128]{1,0:T(8,128)S(1)} %get-tuple-element.104), channel_id=1, source_target_pairs={{0,30},{1,31},{2,4},{3,5},{4,2},{5,3},{6,8},{7,9},{8,6},{9,7},{10,... | collective-permute-start | bytes 294920 | tf_op jit(solution)/shard_map/ppermute | solution.py:343
  31.1 5.4 %collective-permute-start.11 = (f32[144,128]{1,0:T(8,128)S(1)}, f32[144,128]{1,0:T(8,128)S(1)}, u32[]{:S(2)}, u32[]{:S(2)}) collective-permute-start(f32[144,128]{1,0:T(8,128)S(1)} %get-tuple-element.105), channel_id=1, source_target_pairs={{0,28},{1,29},{2,6},{3,7},{4,0},{5,1},{6,2},{7,3},{8,4},{9,5},{10,... | collective-permute-start | bytes 221192 | tf_op jit(solution)/shard_map/ppermute | solution.py:343
  31.1 5.4 %collective-permute-start.12 = (f32[192,128]{1,0:T(8,128)S(1)}, f32[192,128]{1,0:T(8,128)S(1)}, u32[]{:S(2)}, u32[]{:S(2)}) collective-permute-start(f32[192,128]{1,0:T(8,128)S(1)} %get-tuple-element.106), channel_id=1, source_target_pairs={{0,2},{1,3},{2,0},{3,1},{4,6},{5,7},{6,4},{7,5},{8,10},{9,11},{10,... | collective-permute-start | bytes 294920 | tf_op jit(solution)/shard_map/ppermute | solution.py:343
  37.0 10.0 %collective-permute-start.14 = (f32[192,128]{1,0:T(8,128)S(1)}, f32[192,128]{1,0:T(8,128)S(1)}, u32[]{:S(2)}, u32[]{:S(2)}) collective-permute-start(f32[192,128]{1,0:T(8,128)S(1)} %get-tuple-element.115), channel_id=1, source_target_pairs={{0,30},{1,31},{2,4},{3,5},{4,2},{5,3},{6,8},{7,9},{8,6},{9,7},{10,... | collective-permute-start | bytes 294920 | tf_op jit(solution)/shard_map/ppermute | solution.py:343
  39.9 7.1 %collective-permute-start.16 = (f32[192,128]{1,0:T(8,128)S(1)}, f32[192,128]{1,0:T(8,128)S(1)}, u32[]{:S(2)}, u32[]{:S(2)}) collective-permute-start(f32[192,128]{1,0:T(8,128)S(1)} %get-tuple-element.117), channel_id=1, source_target_pairs={{0,2},{1,3},{2,0},{3,1},{4,6},{5,7},{6,4},{7,5},{8,10},{9,11},{10,... | collective-permute-start | bytes 294920 | tf_op jit(solution)/shard_map/ppermute | solution.py:343
  39.9 7.1 %collective-permute-start.13 = (f32[144,128]{1,0:T(8,128)S(1)}, f32[144,128]{1,0:T(8,128)S(1)}, u32[]{:S(2)}, u32[]{:S(2)}) collective-permute-start(f32[144,128]{1,0:T(8,128)S(1)} %get-tuple-element.114), channel_id=1, source_target_pairs={{0,4},{1,5},{2,30},{3,31},{4,8},{5,9},{6,10},{7,11},{8,12},{9,13},... | collective-permute-start | bytes 221192 | tf_op jit(solution)/shard_map/ppermute | solution.py:343
  40.4 6.6 %collective-permute-start.15 = (f32[144,128]{1,0:T(8,128)S(1)}, f32[144,128]{1,0:T(8,128)S(1)}, u32[]{:S(2)}, u32[]{:S(2)}) collective-permute-start(f32[144,128]{1,0:T(8,128)S(1)} %get-tuple-element.116), channel_id=1, source_target_pairs={{0,28},{1,29},{2,6},{3,7},{4,0},{5,1},{6,2},{7,3},{8,4},{9,5},{10,... | collective-permute-start | bytes 221192 | tf_op jit(solution)/shard_map/ppermute | solution.py:343
  47.5 10.9 %collective-permute-start.18 = (f32[192,128]{1,0:T(8,128)S(1)}, f32[192,128]{1,0:T(8,128)S(1)}, u32[]{:S(2)}, u32[]{:S(2)}) collective-permute-start(f32[192,128]{1,0:T(8,128)S(1)} %get-tuple-element.124), channel_id=1, source_target_pairs={{0,30},{1,31},{2,4},{3,5},{4,2},{5,3},{6,8},{7,9},{8,6},{9,7},{10,... | collective-permute-start | bytes 294920 | tf_op jit(solution)/shard_map/ppermute | solution.py:343
  51.3 7.1 %collective-permute-start.20 = (f32[192,128]{1,0:T(8,128)S(1)}, f32[192,128]{1,0:T(8,128)S(1)}, u32[]{:S(2)}, u32[]{:S(2)}) collective-permute-start(f32[192,128]{1,0:T(8,128)S(1)} %get-tuple-element.126), channel_id=1, source_target_pairs={{0,2},{1,3},{2,0},{3,1},{4,6},{5,7},{6,4},{7,5},{8,10},{9,11},{10,... | collective-permute-start | bytes 294920 | tf_op jit(solution)/shard_map/ppermute | solution.py:343
  51.3 7.0 %collective-permute-start.17 = (f32[144,128]{1,0:T(8,128)S(1)}, f32[144,128]{1,0:T(8,128)S(1)}, u32[]{:S(2)}, u32[]{:S(2)}) collective-permute-start(f32[144,128]{1,0:T(8,128)S(1)} %get-tuple-element.123), channel_id=1, source_target_pairs={{0,4},{1,5},{2,30},{3,31},{4,8},{5,9},{6,10},{7,11},{8,12},{9,13},... | collective-permute-start | bytes 221192 | tf_op jit(solution)/shard_map/ppermute | solution.py:343
  51.3 7.0 %collective-permute-start.19 = (f32[144,128]{1,0:T(8,128)S(1)}, f32[144,128]{1,0:T(8,128)S(1)}, u32[]{:S(2)}, u32[]{:S(2)}) collective-permute-start(f32[144,128]{1,0:T(8,128)S(1)} %get-tuple-element.125), channel_id=1, source_target_pairs={{0,28},{1,29},{2,6},{3,7},{4,0},{5,1},{6,2},{7,3},{8,4},{9,5},{10,... | collective-permute-start | bytes 221192 | tf_op jit(solution)/shard_map/ppermute | solution.py:343
  58.9 10.6 %collective-permute-start.22 = (f32[192,128]{1,0:T(8,128)S(1)}, f32[192,128]{1,0:T(8,128)S(1)}, u32[]{:S(2)}, u32[]{:S(2)}) collective-permute-start(f32[192,128]{1,0:T(8,128)S(1)} %get-tuple-element.133), channel_id=1, source_target_pairs={{0,30},{1,31},{2,4},{3,5},{4,2},{5,3},{6,8},{7,9},{8,6},{9,7},{10,... | collective-permute-start | bytes 294920 | tf_op jit(solution)/shard_map/ppermute | solution.py:343
  62.4 7.1 %collective-permute-start.24 = (f32[192,128]{1,0:T(8,128)S(1)}, f32[192,128]{1,0:T(8,128)S(1)}, u32[]{:S(2)}, u32[]{:S(2)}) collective-permute-start(f32[192,128]{1,0:T(8,128)S(1)} %get-tuple-element.135), channel_id=1, source_target_pairs={{0,2},{1,3},{2,0},{3,1},{4,6},{5,7},{6,4},{7,5},{8,10},{9,11},{10,... | collective-permute-start | bytes 294920 | tf_op jit(solution)/shard_map/ppermute | solution.py:343
  62.4 7.0 %collective-permute-start.21 = (f32[144,128]{1,0:T(8,128)S(1)}, f32[144,128]{1,0:T(8,128)S(1)}, u32[]{:S(2)}, u32[]{:S(2)}) collective-permute-start(f32[144,128]{1,0:T(8,128)S(1)} %get-tuple-element.132), channel_id=1, source_target_pairs={{0,4},{1,5},{2,30},{3,31},{4,8},{5,9},{6,10},{7,11},{8,12},{9,13},... | collective-permute-start | bytes 221192 | tf_op jit(solution)/shard_map/ppermute | solution.py:343
  63.0 6.5 %collective-permute-start.23 = (f32[144,128]{1,0:T(8,128)S(1)}, f32[144,128]{1,0:T(8,128)S(1)}, u32[]{:S(2)}, u32[]{:S(2)}) collective-permute-start(f32[144,128]{1,0:T(8,128)S(1)} %get-tuple-element.134), channel_id=1, source_target_pairs={{0,28},{1,29},{2,6},{3,7},{4,0},{5,1},{6,2},{7,3},{8,4},{9,5},{10,... | collective-permute-start | bytes 221192 | tf_op jit(solution)/shard_map/ppermute | solution.py:343
  70.0 11.4 %collective-permute-start.26 = (f32[192,128]{1,0:T(8,128)S(1)}, f32[192,128]{1,0:T(8,128)S(1)}, u32[]{:S(2)}, u32[]{:S(2)}) collective-permute-start(f32[192,128]{1,0:T(8,128)S(1)} %get-tuple-element.141), channel_id=1, source_target_pairs={{0,30},{1,31},{2,4},{3,5},{4,2},{5,3},{6,8},{7,9},{8,6},{9,7},{10,... | collective-permute-start | bytes 294920 | tf_op jit(solution)/shard_map/ppermute | solution.py:343
  74.3 7.1 %collective-permute-start.28 = (f32[192,128]{1,0:T(8,128)S(1)}, f32[192,128]{1,0:T(8,128)S(1)}, u32[]{:S(2)}, u32[]{:S(2)}) collective-permute-start(f32[192,128]{1,0:T(8,128)S(1)} %get-tuple-element.143), channel_id=1, source_target_pairs={{0,2},{1,3},{2,0},{3,1},{4,6},{5,7},{6,4},{7,5},{8,10},{9,11},{10,... | collective-permute-start | bytes 294920 | tf_op jit(solution)/shard_map/ppermute | solution.py:343
  74.3 7.0 %collective-permute-start.25 = (f32[144,128]{1,0:T(8,128)S(1)}, f32[144,128]{1,0:T(8,128)S(1)}, u32[]{:S(2)}, u32[]{:S(2)}) collective-permute-start(f32[144,128]{1,0:T(8,128)S(1)} %get-tuple-element.140), channel_id=1, source_target_pairs={{0,4},{1,5},{2,30},{3,31},{4,8},{5,9},{6,10},{7,11},{8,12},{9,13},... | collective-permute-start | bytes 221192 | tf_op jit(solution)/shard_map/ppermute | solution.py:343
  74.3 7.0 %collective-permute-start.27 = (f32[144,128]{1,0:T(8,128)S(1)}, f32[144,128]{1,0:T(8,128)S(1)}, u32[]{:S(2)}, u32[]{:S(2)}) collective-permute-start(f32[144,128]{1,0:T(8,128)S(1)} %get-tuple-element.142), channel_id=1, source_target_pairs={{0,28},{1,29},{2,6},{3,7},{4,0},{5,1},{6,2},{7,3},{8,4},{9,5},{10,... | collective-permute-start | bytes 221192 | tf_op jit(solution)/shard_map/ppermute | solution.py:343
  81.8 1.6 %collective-permute-start.29 = (f32[512,128]{1,0:T(8,128)S(1)}, f32[512,128]{1,0:T(8,128)S(1)}, u32[]{:S(2)}, u32[]{:S(2)}) collective-permute-start(f32[512,128]{1,0:T(8,128)S(1)} %shard_map.93), channel_id=1, source_target_pairs={{0,1},{1,0},{2,3},{3,2},{4,5},{5,4},{6,7},{7,6},{8,9},{9,8},{10,11... | collective-permute-start | bytes 786440 | tf_op jit(solution)/shard_map/ppermute | solution.py:110
